TPU v7x, 32 devices: a whole 2x2x4 slice. The times are simulated.
32 devices in a mesh: dp: 8 (over y, x, core), tensor: 4 (over z).
Axes of the slice: x: 2, y: 2, z: 4, core: 2. Of those that a mesh axis runs over, the one named last changes fastest.
Arguments:
- hidden_in: bfloat16 [16384, 1024], P(('dp', 'tensor')), may hold values from -6 to 6
- out_grad: bfloat16 [16384, 1024], P(('dp', 'tensor')), may hold values from -6 to 6
- attn_weight: bfloat16 [4, 1024, 1024], P(None, 'dp', 'tensor'), may hold values from -2 to 2
- mlp_weight: bfloat16 [3, 1024, 2624], P(None, 'dp', 'tensor'), may hold values from -2 to 2
- norm_gain: bfloat16 [2, 1024], replicated, may hold values from 0.5 to 1.5
- attn_first: float32 [4, 1024, 1024], P(None, 'dp', 'tensor'), may hold values from -60 to 60
- attn_second: float32 [4, 1024, 1024], P(None, 'dp', 'tensor'), may hold values from 100 to 3000
- attn_left: float32 [4, 1024, 512], P(None, 'dp', 'tensor'), may hold values from -2 to 3
- attn_right: float32 [4, 2048, 1024], P(None, 'dp', 'tensor'), may hold values from -2 to 3
- mlp_first: float32 [3, 1024, 2624], P(None, 'dp', 'tensor'), may hold values from -60 to 60
- mlp_second: float32 [3, 1024, 2624], P(None, 'dp', 'tensor'), may hold values from 100 to 3000
- mlp_left: float32 [3, 1024, 512], P(None, 'dp', 'tensor'), may hold values from -2 to 3
- mlp_right: float32 [3, 5248, 2624], P(None, 'dp', 'tensor'), may hold values from -2 to 3
- gain_first: float32 [2, 1024], replicated, may hold values from -60 to 60
- gain_second: float32 [2, 1024], replicated, may hold values from 100 to 3000
- owner_rows: int32 [8], replicated, may hold values from 0 to 7, each once
- segment_ids: int32 [16384], P('dp'), may hold values from 0 to 15, as said below
- positions: int32 [16384], P('dp'), may hold values from 0 to 1023, as said below
- valid: int32 [16384], P('dp'), may hold values from 0 to 1, as said below
- step: int32 [], replicated, may hold values from 1 to 20
- learn_rate: float32 [], replicated, may hold values from 0.03 to 0.08
- beta_first: float32 [], replicated, may hold values from 0.8 to 0.95
- beta_second: float32 [], replicated, may hold values from 0.9 to 0.99
Outputs:
- output: bfloat16 [16384, 1024], P(('dp', 'tensor'))
- input_grad: bfloat16 [16384, 1024], P(('dp', 'tensor'))
- attn_grad: float32 [4, 1024, 1024], P(None, 'dp', 'tensor')
- mlp_grad: float32 [3, 1024, 2624], P(None, 'dp', 'tensor')
- gain_grad: float32 [2, 1024], replicated
- attn_first_new: float32 [4, 1024, 1024], P(None, 'dp', 'tensor')
- attn_second_new: float32 [4, 1024, 1024], P(None, 'dp', 'tensor')
- mlp_first_new: float32 [3, 1024, 2624], P(None, 'dp', 'tensor')
- mlp_second_new: float32 [3, 1024, 2624], P(None, 'dp', 'tensor')
- gain_first_new: float32 [2, 1024], replicated
- gain_second_new: float32 [2, 1024], replicated
- attn_update: float32 [4, 1024, 1024], P(None, 'dp', 'tensor')
- mlp_update: float32 [3, 1024, 2624], P(None, 'dp', 'tensor')
- gain_update: float32 [2, 1024], replicated
- norm_scale: float32 [7, 8, 4], P(None, 'dp', 'tensor')
- root_means: float32 [4], replicated
Inputs may be any that keep to these rules, and one draw needn't show every extreme that they name: `owner_rows`: each index of dp owns a different row block of 128 rows. `segment_ids`: ids restart at 0 with every sequence of 1024 tokens and never fall within it; every document but the last of a sequence has 64 tokens or more. `positions`: 0 at the start of every sequence and wherever segment_ids changes, else one more than the token before. `valid`: within each sequence: 1 on a leading run of at least half of its tokens, 0 after it.
All inputs are finite; a program needn't handle non-finite values.
Results may differ from a plain program's by a relative error of at most 0.014.
Values may be sent and summed in bfloat16 or wider, within the bound.
No kernel may reach another device: no remote copies, remote signals or barrier semaphores. Data moves between devices by JAX's collectives and lax.ppermute only.
A program may use at most 256 MiB of HBM per device.

v0:
```python
import math

import jax
import jax.numpy as jnp
from jax import lax
from jax.sharding import PartitionSpec as P

D = 1024
HEADS = 16
HEAD_DIM = 64
SEQ_LEN = 1024


NORM_EPS = 1e-05
ROPE_BASE = 160000.0
ADAM_EPS = 1e-08
SCALE_EPS = 1e-06
MASKED = -1e30
PRECISE = lax.Precision.HIGHEST


def layer_norm(values, gain_row):
    average = jnp.mean(values, axis=-1, keepdims=True)
    centred = values - average
    spread = jnp.mean(centred * centred, axis=-1, keepdims=True)
    return centred * lax.rsqrt(spread + NORM_EPS) * gain_row


def rope_tables(positions):
    half_dim = HEAD_DIM // 2
    frequency = jnp.exp(
        jnp.arange(half_dim, dtype=jnp.float32) * (-2.0 * math.log(ROPE_BASE) / HEAD_DIM)
    )
    angles = positions.astype(jnp.float32)[:, None] * frequency[None, :]
    return (jnp.cos(angles)[:, None, :], jnp.sin(angles)[:, None, :])


def rotate(values, cos_table, sin_table):
    half_dim = values.shape[-1] // 2
    lower_half = values[..., :half_dim]
    upper_half = values[..., half_dim:]
    return jnp.concatenate(
        [
            lower_half * cos_table - upper_half * sin_table,
            upper_half * cos_table + lower_half * sin_table,
        ],
        axis=-1,
    )


def rotate_back(grads_in, cos_table, sin_table):
    half_dim = grads_in.shape[-1] // 2
    lower_half = grads_in[..., :half_dim]
    upper_half = grads_in[..., half_dim:]
    return jnp.concatenate(
        [
            lower_half * cos_table + upper_half * sin_table,
            upper_half * cos_table - lower_half * sin_table,
        ],
        axis=-1,
    )


def allowed_mask(seg_block, seg_all, keep_all, block_rows):
    location = jnp.arange(seg_all.shape[0])
    return (seg_block[:, None] == seg_all[None, :]) & (
        (keep_all[None, :] > 0) | (block_rows[:, None] == location[None, :])
    )


def block_scores(query_block, key_rows, seg_all, keep_all, first_row, block_size):
    seg_block = lax.dynamic_slice_in_dim(seg_all, first_row, block_size, 0)
    block_rows = first_row + jnp.arange(block_size)
    allowed = allowed_mask(seg_block, seg_all, keep_all, block_rows)
    raw = jnp.einsum("qhe,khe->hqk", query_block, key_rows, preferred_element_type=jnp.float32)
    return jnp.where(allowed[None], raw * (1.0 / math.sqrt(HEAD_DIM)), MASKED)


def sequence_forward(pieces):
    queries, key_rows, value_rows, seg_all, keep_all = pieces
    length = queries.shape[0]
    block_size = min(512, length)
    block_count = length // block_size

    def one_block(block_index):
        first_row = block_index * block_size
        query_block = lax.dynamic_slice_in_dim(queries, first_row, block_size, 0)
        scores = block_scores(query_block, key_rows, seg_all, keep_all, first_row, block_size)
        highest = jnp.max(scores, axis=-1, keepdims=True)
        exponent = jnp.exp(scores - highest)
        summed = jnp.sum(exponent, axis=-1, keepdims=True)
        weights = (exponent / summed).astype(jnp.bfloat16)
        mixture = jnp.einsum(
            "hqk,khe->qhe", weights, value_rows, preferred_element_type=jnp.float32
        )
        return (mixture, (highest + jnp.log(summed))[..., 0])

    mixture, log_sums = lax.map(one_block, jnp.arange(block_count))
    return (mixture.reshape(length, mixture.shape[2], mixture.shape[3]), log_sums)


def sequence_backward(pieces):
    queries, key_rows, value_rows, seg_all, keep_all, log_sums, mix_grad = pieces
    length = queries.shape[0]
    block_size = min(512, length)
    block_count = length // block_size
    factor = 1.0 / math.sqrt(HEAD_DIM)

    def one_block(carried, block_index):
        key_grad, value_grad = carried
        first_row = block_index * block_size
        query_block = lax.dynamic_slice_in_dim(queries, first_row, block_size, 0)
        scores = block_scores(query_block, key_rows, seg_all, keep_all, first_row, block_size)
        probability = jnp.exp(
            scores - lax.dynamic_index_in_dim(log_sums, block_index, 0, keepdims=False)[..., None]
        )
        weights = probability.astype(jnp.bfloat16)
        grad_block = lax.dynamic_slice_in_dim(mix_grad, first_row, block_size, 0)
        prob_grad = jnp.einsum(
            "qhe,khe->hqk", grad_block, value_rows, preferred_element_type=jnp.float32
        )
        score_grad = probability * (
            prob_grad - jnp.sum(probability * prob_grad, axis=-1, keepdims=True)
        )
        raw_grad = (score_grad * factor).astype(jnp.bfloat16)
        query_grad = jnp.einsum(
            "hqk,khe->qhe", raw_grad, key_rows, preferred_element_type=jnp.float32
        )
        key_grad = key_grad + jnp.einsum(
            "hqk,qhe->khe", raw_grad, query_block, preferred_element_type=jnp.float32
        )
        value_grad = value_grad + jnp.einsum(
            "hqk,qhe->khe", weights, grad_block, preferred_element_type=jnp.float32
        )
        return ((key_grad, value_grad), query_grad)

    zero_rows = jnp.zeros(key_rows.shape, jnp.float32)
    (key_grad, value_grad), query_grad = lax.scan(
        one_block, (zero_rows, zero_rows), jnp.arange(block_count)
    )
    return (query_grad.reshape(queries.shape), key_grad, value_grad)


def to_model(stored, inverse, owners):
    kind_count, row_total, col_total = stored.shape
    return jnp.take(
        stored.reshape(kind_count, owners, row_total // owners, col_total), inverse, axis=1
    ).reshape(kind_count, row_total, col_total)


def to_owner(model, owner_rows, owners):
    kind_count, row_total, col_total = model.shape
    return jnp.take(
        model.reshape(kind_count, owners, row_total // owners, col_total), owner_rows, axis=1
    ).reshape(kind_count, row_total, col_total)


def soap_block(grad_block, first, second, left, right, step_size, beta_one, beta_two):
    half_turn = jnp.einsum("kab,kac->kbc", left, grad_block, precision=PRECISE)
    rotated = jnp.einsum("kbc,kce->kbe", half_turn, right, precision=PRECISE)
    first_new = beta_one * first + (1.0 - beta_one) * rotated
    second_new = beta_two * second + (1.0 - beta_two) * rotated * rotated
    direction = first_new / (jnp.sqrt(second_new) + ADAM_EPS)
    back_half = jnp.einsum("kab,kbe->kae", left, direction, precision=PRECISE)
    turned = jnp.einsum("kae,kce->kac", back_half, right, precision=PRECISE)
    factor = jnp.sqrt(jnp.mean(direction * direction, axis=(1, 2))) * lax.rsqrt(
        jnp.mean(turned * turned, axis=(1, 2)) + SCALE_EPS
    )
    update = -step_size * factor[:, None, None] * turned
    return (first_new, second_new, update, factor)


def gelu_gate(gate_vals, up_vals):
    return jax.nn.gelu(gate_vals, approximate=False) * up_vals


def per_device(
    hidden_in,
    out_grad,
    attn_weight,
    mlp_weight,
    norm_gain,
    attn_first,
    attn_second,
    attn_left,
    attn_right,
    mlp_first,
    mlp_second,
    mlp_left,
    mlp_right,
    gain_first,
    gain_second,
    owner_rows,
    segment_ids,
    positions,
    valid,
    step,
    learn_rate,
    beta_first,
    beta_second,
):
    owners = lax.axis_size("dp")
    shards = lax.axis_size("tensor")
    own_rows = hidden_in.shape[0]
    group_rows = segment_ids.shape[0]
    offset = lax.axis_index("tensor") * own_rows
    heads_here = HEADS // shards
    sequences = group_rows // SEQ_LEN
    gain_rows = norm_gain.astype(jnp.float32)
    hidden_f = hidden_in.astype(jnp.float32)
    attn_stored, mlp_stored = (
        lax.all_gather(attn_weight, "dp", axis=1, tiled=True),
        lax.all_gather(mlp_weight, "dp", axis=1, tiled=True),
    )
    slot_ids = jnp.arange(owners, dtype=jnp.int32)
    inverse = jnp.sum(
        slot_ids[:, None] * (owner_rows[:, None] == slot_ids[None, :]).astype(jnp.int32), axis=0
    )
    attn_model = to_model(attn_stored, inverse, owners)
    mlp_model = to_model(mlp_stored, inverse, owners)
    qkv_local = attn_model[:3]
    out_local = attn_model[3]
    gate_up_local = mlp_model[:2]
    down_local = mlp_model[2]
    first_norm = layer_norm(hidden_f, gain_rows[0]).astype(jnp.bfloat16)
    first_all = lax.all_gather(first_norm, "tensor", axis=0, tiled=True)
    projected = jnp.einsum("td,kdc->ktc", first_all, qkv_local, preferred_element_type=jnp.float32)
    cos_table, sin_table = rope_tables(positions)
    head_shape = (group_rows, heads_here, HEAD_DIM)
    flat_shape = (group_rows, heads_here * HEAD_DIM)
    seq_shape = (sequences, SEQ_LEN, heads_here, HEAD_DIM)
    queries = (
        rotate(projected[0].reshape(head_shape), cos_table, sin_table)
        .astype(jnp.bfloat16)
        .reshape(seq_shape)
    )
    key_rows = (
        rotate(projected[1].reshape(head_shape), cos_table, sin_table)
        .astype(jnp.bfloat16)
        .reshape(seq_shape)
    )
    value_rows = projected[2].astype(jnp.bfloat16).reshape(seq_shape)
    seg_seq = segment_ids.reshape(sequences, SEQ_LEN)
    keep_seq = valid.reshape(sequences, SEQ_LEN)
    mixture, log_sums = lax.map(
        sequence_forward, (queries, key_rows, value_rows, seg_seq, keep_seq)
    )
    attended = mixture.reshape(flat_shape).astype(jnp.bfloat16)
    attn_branch = lax.psum_scatter(
        jnp.einsum("tc,dc->td", attended, out_local, preferred_element_type=jnp.float32),
        "tensor",
        scatter_dimension=0,
        tiled=True,
    )
    resid_own = hidden_f + attn_branch
    second_norm = layer_norm(resid_own, gain_rows[1]).astype(jnp.bfloat16)
    second_all = lax.all_gather(second_norm, "tensor", axis=0, tiled=True)
    gate_up = jnp.einsum(
        "td,kdf->ktf", second_all, gate_up_local, preferred_element_type=jnp.float32
    )
    gated_vals, gated_back = jax.vjp(gelu_gate, gate_up[0], gate_up[1])
    activated = gated_vals.astype(jnp.bfloat16)
    mlp_branch = lax.psum_scatter(
        jnp.einsum("tf,df->td", activated, down_local, preferred_element_type=jnp.float32),
        "tensor",
        scatter_dimension=0,
        tiled=True,
    )
    result = resid_own + mlp_branch
    output = result.astype(jnp.bfloat16)
    keep_own = lax.dynamic_slice_in_dim(valid, offset, own_rows, 0).astype(jnp.float32)[:, None]
    stat_terms = jnp.stack(
        [
            jnp.sum(keep_own),
            jnp.sum(keep_own * attn_branch * attn_branch),
            jnp.sum(keep_own * resid_own * resid_own),
            jnp.sum(keep_own * mlp_branch * mlp_branch),
            jnp.sum(keep_own * result * result),
        ]
    )
    stat_sums = lax.psum(stat_terms, ("dp", "tensor"))
    grad_all = lax.all_gather(out_grad, "tensor", axis=0, tiled=True)
    hidden_grad = jnp.einsum("td,df->tf", grad_all, down_local, preferred_element_type=jnp.float32)
    down_wgrad = jnp.einsum("td,tf->df", grad_all, activated, preferred_element_type=jnp.float32)
    gate_grad, up_grad = gated_back(hidden_grad)
    gate_up_grad = jnp.stack([gate_grad, up_grad]).astype(jnp.bfloat16)
    gate_up_wgrad = jnp.einsum(
        "td,ktf->kdf", second_all, gate_up_grad, preferred_element_type=jnp.float32
    )
    second_grad = lax.psum_scatter(
        jnp.einsum("ktf,kdf->td", gate_up_grad, gate_up_local, preferred_element_type=jnp.float32),
        "tensor",
        scatter_dimension=0,
        tiled=True,
    )
    norm_two_out, norm_two_back = jax.vjp(layer_norm, resid_own, gain_rows[1])
    resid_part, gain_two_grad = norm_two_back(second_grad)
    resid_grad = out_grad.astype(jnp.float32) + resid_part
    resid_grad_all = lax.all_gather(resid_grad.astype(jnp.bfloat16), "tensor", axis=0, tiled=True)
    mixed_grad = jnp.einsum(
        "td,dc->tc", resid_grad_all, out_local, preferred_element_type=jnp.float32
    ).astype(jnp.bfloat16)
    out_wgrad = jnp.einsum(
        "td,tc->dc", resid_grad_all, attended, preferred_element_type=jnp.float32
    )
    query_grad, key_grad, value_grad = lax.map(
        sequence_backward,
        (queries, key_rows, value_rows, seg_seq, keep_seq, log_sums, mixed_grad.reshape(seq_shape)),
    )
    qkv_grad = jnp.stack(
        [
            rotate_back(query_grad.reshape(head_shape), cos_table, sin_table).reshape(flat_shape),
            rotate_back(key_grad.reshape(head_shape), cos_table, sin_table).reshape(flat_shape),
            value_grad.reshape(flat_shape),
        ]
    ).astype(jnp.bfloat16)
    qkv_wgrad = jnp.einsum("td,ktc->kdc", first_all, qkv_grad, preferred_element_type=jnp.float32)
    first_grad = lax.psum_scatter(
        jnp.einsum("ktc,kdc->td", qkv_grad, qkv_local, preferred_element_type=jnp.float32),
        "tensor",
        scatter_dimension=0,
        tiled=True,
    )
    norm_one_out, norm_one_back = jax.vjp(layer_norm, hidden_f, gain_rows[0])
    input_part, gain_one_grad = norm_one_back(first_grad)
    input_grad = (resid_grad + input_part).astype(jnp.bfloat16)
    attn_part = to_owner(jnp.concatenate([qkv_wgrad, out_wgrad[None]], axis=0), owner_rows, owners)
    mlp_part = to_owner(
        jnp.concatenate([gate_up_wgrad, down_wgrad[None]], axis=0), owner_rows, owners
    )
    attn_grad, mlp_grad = (
        lax.psum_scatter(attn_part, "dp", scatter_dimension=1, tiled=True),
        lax.psum_scatter(mlp_part, "dp", scatter_dimension=1, tiled=True),
    )
    gain_part = jnp.stack([gain_one_grad, gain_two_grad])
    gain_grad = lax.psum(gain_part, ("dp", "tensor"))
    step_count = step.astype(jnp.float32)
    step_size = (
        learn_rate
        * jnp.sqrt(1.0 - jnp.power(beta_second, step_count))
        / (1.0 - jnp.power(beta_first, step_count))
    )
    attn_first_new, attn_second_new, attn_update, attn_scale = soap_block(
        attn_grad,
        attn_first,
        attn_second,
        attn_left,
        attn_right,
        step_size,
        beta_first,
        beta_second,
    )
    mlp_first_new, mlp_second_new, mlp_update, mlp_scale = soap_block(
        mlp_grad, mlp_first, mlp_second, mlp_left, mlp_right, step_size, beta_first, beta_second
    )
    gain_first_new = beta_first * gain_first + (1.0 - beta_first) * gain_grad
    gain_second_new = beta_second * gain_second + (1.0 - beta_second) * gain_grad * gain_grad
    gain_update = -step_size * gain_first_new / (jnp.sqrt(gain_second_new) + ADAM_EPS)
    root_means = jnp.sqrt(stat_sums[1:] / (stat_sums[0] * D))
    norm_scale = jnp.concatenate([attn_scale, mlp_scale], axis=0).reshape(7, 1, 1)
    return (
        output,
        input_grad,
        attn_grad,
        mlp_grad,
        gain_grad,
        attn_first_new,
        attn_second_new,
        mlp_first_new,
        mlp_second_new,
        gain_first_new,
        gain_second_new,
        attn_update,
        mlp_update,
        gain_update,
        norm_scale,
        root_means,
    )


def solution(mesh):
    return jax.shard_map(
        per_device,
        mesh=mesh,
        in_specs=(
            P(("dp", "tensor"), None),
            P(("dp", "tensor"), None),
            P(None, "dp", "tensor"),
            P(None, "dp", "tensor"),
            P(),
            P(None, "dp", "tensor"),
            P(None, "dp", "tensor"),
            P(None, "dp", "tensor"),
            P(None, "dp", "tensor"),
            P(None, "dp", "tensor"),
            P(None, "dp", "tensor"),
            P(None, "dp", "tensor"),
            P(None, "dp", "tensor"),
            P(),
            P(),
            P(),
            P("dp"),
            P("dp"),
            P("dp"),
            P(),
            P(),
            P(),
            P(),
        ),
        out_specs=(
            P(("dp", "tensor"), None),
            P(("dp", "tensor"), None),
            P(None, "dp", "tensor"),
            P(None, "dp", "tensor"),
            P(),
            P(None, "dp", "tensor"),
            P(None, "dp", "tensor"),
            P(None, "dp", "tensor"),
            P(None, "dp", "tensor"),
            P(),
            P(),
            P(None, "dp", "tensor"),
            P(None, "dp", "tensor"),
            P(),
            P(None, "dp", "tensor"),
            P(),
        ),
        check_vma=False,
    )
```

profile of v0, /device:TPU:0, one launch (start us, length us, event | category | flops | bytes accessed | tf_op | source)
XLA Modules:
  0.0 1533.4 jit_solution(12198340850637608766)
XLA Ops:
  20.2 20.4 %all-gather.7.cloned.1.call-done = bf16[4,1024,256]{2,1,0:T(8,128)(2,1)} async-done(((bf16[4,128,256]{2,1,0:T(8,128)(2,1)}), bf16[4,1024,256]{2,1,0:T(8,128)(2,1)}) %all-gather.7.cloned.1.call-update) | async-done | bytes 2097168 | tf_op jit(solution)/shard_map/all_gather | solution.py:212
  48.7 74.9 %all-gather.9.cloned.1.call-done = bf16[2048,1024]{1,0:T(8,128)(2,1)} async-done(((bf16[512,1024]{1,0:T(8,128)(2,1)}), bf16[2048,1024]{1,0:T(8,128)(2,1)}) %all-gather.9.cloned.1.call-update) | async-done | bytes 4194320 | tf_op jit(solution)/shard_map/all_gather | solution.py:226
  143.4 51.9 %while.60 = (s32[]{:T(128)}, bf16[2,1024,4,64]{3,2,1,0:T(4,128)(2,1)}, f32[2,2,4,512]{3,2,1,0:T(4,128)S(1)}, bf16[2,1024,4,64]{1,3,2,0:T(8,128)(2,1)}, s32[2,102...) while((s32[]{:T(128)}, ...), condition=%wide.region_8.9_spmd.clone, body=%wide.region_3.8_spmd.sunk.clone | while | flops 564133376 | bytes 41292332 | solution.py:245
  146.7 19.8 %while.59 = (s32[]{:T(128)}, bf16[2,512,4,64]{1,3,2,0:T(8,128)(2,1)}, f32[2,4,512]{2,1,0:T(4,128)S(1)}, s32[2]{0:T(128)S(1)}, s32[1024]{0:T(1024)S(1)}, /*index=...) while((s32[]{:T(128)}, ...), condition=%wide.region_7.7_spmd, body=%wide.region_4.6_spmd.sunk | while | flops 564133376 | bytes 35475748 | solution.py:98
  172.5 19.8 %while.59 = (s32[]{:T(128)}, bf16[2,512,4,64]{1,3,2,0:T(8,128)(2,1)}, f32[2,4,512]{2,1,0:T(4,128)S(1)}, s32[2]{0:T(128)S(1)}, s32[1024]{0:T(1024)S(1)}, /*index=...) while((s32[]{:T(128)}, ...), condition=%wide.region_7.7_spmd, body=%wide.region_4.6_spmd.sunk | while | flops 564133376 | bytes 35475748 | solution.py:98
  205.5 142.5 %reduce-scatter.7.cloned.1.call-done = f32[512,1024]{1,0:T(8,128)} async-done(((f32[2048,1024]{1,0:T(8,128)}), f32[512,1024]{1,0:T(8,128)}) %reduce-scatter.7.cloned.1.call-update) | async-done | bytes 2097168 | tf_op jit(solution)/shard_map/reduce_scatter | solution.py:249
  352.5 34.8 %all-gather.11.cloned.1.call-done = bf16[3,1024,656]{1,2,0:T(8,128)(2,1)} async-done(((bf16[3,128,656]{1,2,0:T(8,128)(2,1)}), bf16[3,1024,656]{1,2,0:T(8,128)(2,1)}) %all-gather.11.cloned.1.call-update) | async-done | bytes 4030480 | tf_op jit(solution)/shard_map/all_gather | solution.py:213
  403.6 66.5 %all-gather.13.cloned.1.call-done = bf16[2048,1024]{1,0:T(8,128)(2,1)} async-done(((bf16[512,1024]{1,0:T(8,128)(2,1)}), bf16[2048,1024]{1,0:T(8,128)(2,1)}) %all-gather.13.cloned.1.call-update) | async-done | bytes 4194320 | tf_op jit(solution)/shard_map/all_gather | solution.py:257
  499.5 51.3 %all-gather.15.cloned.1.call-done = bf16[2048,1024]{1,0:T(8,128)(2,1)} async-done(((bf16[512,1024]{1,0:T(8,128)(2,1)}), bf16[2048,1024]{1,0:T(8,128)(2,1)}) %all-gather.15.cloned.1.call-update) | async-done | bytes 4194320 | tf_op jit(solution)/shard_map/all_gather | solution.py:282
  594.0 102.1 %reduce-scatter.9.cloned.1.call-done = f32[512,1024]{1,0:T(8,128)} async-done(((f32[2048,1024]{1,0:T(8,128)}), f32[512,1024]{1,0:T(8,128)}) %reduce-scatter.9.cloned.1.call-update) | async-done | bytes 2097168 | tf_op jit(solution)/shard_map/reduce_scatter | solution.py:263
  696.1 147.6 %reduce-scatter.11.cloned.1.call-done = f32[512,1024]{1,0:T(8,128)} async-done(((f32[2048,1024]{1,0:T(8,128)}), f32[512,1024]{1,0:T(8,128)}) %reduce-scatter.11.cloned.1.call-update) | async-done | bytes 2097168 | tf_op jit(solution)/shard_map/reduce_scatter | solution.py:290
  894.3 40.0 %all-gather.17.cloned.1.call-done = bf16[2048,1024]{1,0:T(8,128)(2,1)} async-done(((bf16[512,1024]{1,0:T(8,128)(2,1)}), bf16[2048,1024]{1,0:T(8,128)(2,1)}) %all-gather.17.cloned.1.call-update) | async-done | bytes 4194320 | tf_op jit(solution)/shard_map/all_gather | solution.py:299
  944.5 269.8 %while.62 = (s32[]{:T(128)}, f32[2,1024,4,64]{3,2,1,0:T(4,128)}, f32[2,1024,4,64]{1,0,3,2:T(2,128)}, bf16[2,1024,4,64]{1,3,2,0:T(8,128)(2,1)}, bf16[2,1024,4,64]...) while((s32[]{:T(128)}, f32[2,1024,4,64]{3,2,1,0:T(4,128)}, ...), condition=%wide.region_20.21_spmd.clone, body=%wide.region_16.20_spmd.sunk.clone | while | flops 1399856640 | bytes 152171168 | solution.py:306
  948.9 104.7 %while.61 = (s32[]{:T(128)}, f32[1024,4,64]{0,2,1:T(8,128)}, f32[1024,4,64]{0,2,1:T(8,128)}, f32[2,512,4,64]{1,3,2,0:T(8,128)}, s32[2]{0:T(128)S(1)}, /*index=5*...) while((s32[]{:T(128)}, f32[1024,4,64]{0,2,1:T(8,128)}, ...), condition=%wide.region_19.19_spmd.clone, body=%wide.region_17.18_spmd.clone.sunk | while | flops 1399856640 | bytes 136393040 | solution.py:138
  963.5 19.0 %fusion.289 = f32[1024,4,64]{0,2,1:T(8,128)} fusion(f32[4,512,1024]{2,1,0:T(8,128)} %fusion.286, f32[4,512,1024]{2,1,0:T(8,128)} %copy-done.1, f32[4,512]{1,0:T(4,128)S(1)} %dynamic-slice_bitcast_fusion.20, pred[512,1024]{1,0:T(8,128)(4,1)S(1)} %fusion.288, f32[1024,4,64]{0,2,1:T(8,128)} %get-tuple-element.967, pred[]{:T(512)S(6)} %compare.3, ...), kind=kOutput, calls=%fused_computation.53.clone.1 | convolution fusion | flops 292031488 | bytes 36978692 | tf_op jit(solution)/shard_map/while/body/eval_jaxpr/while/body/eval_jaxpr/hqk,qhe->khe/dot_general | solution.py:129
  982.5 18.1 %fusion.291 = f32[2,512,4,64]{1,3,2,0:T(8,128)} fusion(f32[2,512,4,64]{1,3,2,0:T(8,128)} %get-tuple-element.969, s32[]{:T(128)S(6)} %copy.252, bf16[1024,4,64]{0,2,1:T(8,128)(2,1)S(1)} %get-tuple-element.991, f32[4,512,1024]{2,1,0:T(8,128)} %fusion.286, f32[4,512,1024]{2,1,0:T(8,128)} %copy-done.1, f32[4,512]{1,0:T(4,128)S(1)} %dynamic-slice_bitcast_fusion.20, ...), kind=kOutput, calls=%fused_computation.56.clone.1 | convolution fusion | flops 291507200 | bytes 35667972 | tf_op jit(solution)/shard_map/while/body/eval_jaxpr/while/body/eval_jaxpr/hqk,khe->qhe/dot_general | solution.py:126
  1016.5 19.2 %fusion.289 = f32[1024,4,64]{0,2,1:T(8,128)} fusion(f32[4,512,1024]{2,1,0:T(8,128)} %fusion.286, f32[4,512,1024]{2,1,0:T(8,128)} %copy-done.1, f32[4,512]{1,0:T(4,128)S(1)} %dynamic-slice_bitcast_fusion.20, pred[512,1024]{1,0:T(8,128)(4,1)S(1)} %fusion.288, f32[1024,4,64]{0,2,1:T(8,128)} %get-tuple-element.967, pred[]{:T(512)S(6)} %compare.3, ...), kind=kOutput, calls=%fused_computation.53.clone.1 | convolution fusion | flops 292031488 | bytes 36978692 | tf_op jit(solution)/shard_map/while/body/eval_jaxpr/while/body/eval_jaxpr/hqk,qhe->khe/dot_general | solution.py:129
  1055.9 18.7 %dynamic_update_slice.56 = f32[2,1024,4,64]{1,0,3,2:T(2,128)} dynamic-update-slice(f32[2,1024,4,64]{1,0,3,2:T(2,128)} %get-tuple-element.1054, f32[1,1024,4,64]{1,0,3,2:T(1,128)S(1)} %copy.233, s32[]{:T(128)S(6)} %copy.276, s32[]{:T(128)} %constant.121.clone.1..sunk.6, s32[]{:T(128)} %constant.121.clone.1..sunk.6, s32[]{:T(128)} %constant.121.clone.1..sunk.6) | dynamic-update-slice | bytes 2097156 | tf_op jit(solution)/shard_map/while/body/jit(dynamic_update_index_in_dim)/dynamic_update_slice | solution.py:245
  1083.5 104.2 %while.61 = (s32[]{:T(128)}, f32[1024,4,64]{0,2,1:T(8,128)}, f32[1024,4,64]{0,2,1:T(8,128)}, f32[2,512,4,64]{1,3,2,0:T(8,128)}, s32[2]{0:T(128)S(1)}, /*index=5*...) while((s32[]{:T(128)}, f32[1024,4,64]{0,2,1:T(8,128)}, ...), condition=%wide.region_19.19_spmd.clone, body=%wide.region_17.18_spmd.clone.sunk | while | flops 1399856640 | bytes 136393040 | solution.py:138
  1097.9 19.0 %fusion.289 = f32[1024,4,64]{0,2,1:T(8,128)} fusion(f32[4,512,1024]{2,1,0:T(8,128)} %fusion.286, f32[4,512,1024]{2,1,0:T(8,128)} %copy-done.1, f32[4,512]{1,0:T(4,128)S(1)} %dynamic-slice_bitcast_fusion.20, pred[512,1024]{1,0:T(8,128)(4,1)S(1)} %fusion.288, f32[1024,4,64]{0,2,1:T(8,128)} %get-tuple-element.967, pred[]{:T(512)S(6)} %compare.3, ...), kind=kOutput, calls=%fused_computation.53.clone.1 | convolution fusion | flops 292031488 | bytes 36978692 | tf_op jit(solution)/shard_map/while/body/eval_jaxpr/while/body/eval_jaxpr/hqk,qhe->khe/dot_general | solution.py:129
  1150.6 19.2 %fusion.289 = f32[1024,4,64]{0,2,1:T(8,128)} fusion(f32[4,512,1024]{2,1,0:T(8,128)} %fusion.286, f32[4,512,1024]{2,1,0:T(8,128)} %copy-done.1, f32[4,512]{1,0:T(4,128)S(1)} %dynamic-slice_bitcast_fusion.20, pred[512,1024]{1,0:T(8,128)(4,1)S(1)} %fusion.288, f32[1024,4,64]{0,2,1:T(8,128)} %get-tuple-element.967, pred[]{:T(512)S(6)} %compare.3, ...), kind=kOutput, calls=%fused_computation.53.clone.1 | convolution fusion | flops 292031488 | bytes 36978692 | tf_op jit(solution)/shard_map/while/body/eval_jaxpr/while/body/eval_jaxpr/hqk,qhe->khe/dot_general | solution.py:129
  1190.0 18.7 %dynamic_update_slice.56 = f32[2,1024,4,64]{1,0,3,2:T(2,128)} dynamic-update-slice(f32[2,1024,4,64]{1,0,3,2:T(2,128)} %get-tuple-element.1054, f32[1,1024,4,64]{1,0,3,2:T(1,128)S(1)} %copy.233, s32[]{:T(128)S(6)} %copy.276, s32[]{:T(128)} %constant.121.clone.1..sunk.6, s32[]{:T(128)} %constant.121.clone.1..sunk.6, s32[]{:T(128)} %constant.121.clone.1..sunk.6) | dynamic-update-slice | bytes 2097156 | tf_op jit(solution)/shard_map/while/body/jit(dynamic_update_index_in_dim)/dynamic_update_slice | solution.py:245
  1336.2 139.4 %reduce-scatter.13.cloned.1.call-done = f32[512,1024]{1,0:T(8,128)} async-done(((f32[2048,1024]{1,0:T(8,128)}), f32[512,1024]{1,0:T(8,128)}) %reduce-scatter.13.cloned.1.call-update) | async-done | bytes 2097168 | tf_op jit(solution)/shard_map/reduce_scatter | solution.py:318
  1480.3 41.1 %all-reduce = (f32[2,1024]{1,0:T(2,128)S(1)}, f32[5]{0:T(128)S(1)}) all-reduce(f32[2,1024]{1,0:T(2,128)S(1)} %pad_maximum_fusion.14, f32[5]{0:T(128)S(1)} %stack.49), channel_id=1, replica_groups=mesh['dp'=8,'tensor'=4] {'dp','tensor'}, use_global_device_ids=true, to_apply=%region_28.29 | all-reduce | flops 2053 | bytes 16424 | tf_op jit(solution)/shard_map/psum | solution.py:336
  (439 shorter events, 507.6 us)
Async XLA Ops:
  7.2 1323.4 %copy-start = (f32[4,256,256]{2,1,0:T(8,128)S(1)}, f32[4,256,256]{2,1,0:T(8,128)}, u32[]{:S(2)}) copy-start(f32[4,256,256]{2,1,0:T(8,128)} %param.39) | copy-start | bytes 3145732
  7.2 33.4 %all-gather.7.cloned.1.call-start = ((), (), s32[]{:S(2)}) async-start(), calls=%async_computation.6 | async-start | bytes 2359296 | tf_op jit(solution)/shard_map/all_gather | solution.py:212
  8.0 115.6 %all-gather.9.cloned.1.call-start = ((), (), s32[]{:S(2)}) async-start(), calls=%async_computation.7 | async-start | bytes 5242880 | tf_op jit(solution)/shard_map/all_gather | solution.py:226
  16.3 331.7 %reduce-scatter.7.cloned.1.call-start = ((), (), s32[]{:S(2)}) async-start(), calls=%async_computation.8 | async-start | bytes 10485760 | tf_op jit(solution)/shard_map/reduce_scatter | solution.py:249
  204.9 145.6 %copy-start.50 = (f32[1,1024]{1,0:T(1,128)S(1)}, f32[1,1024]{1,0:T(1,128)}, u32[]{:S(2)}) copy-start(f32[1,1024]{1,0:T(1,128)} %get-tuple-element.494) | copy-start | bytes 12292
  204.9 182.4 %all-gather.11.cloned.1.call-start = ((), (), s32[]{:S(2)}) async-start(), calls=%async_computation.9 | async-start | bytes 4534272 | tf_op jit(solution)/shard_map/all_gather | solution.py:213
  205.5 264.6 %all-gather.13.cloned.1.call-start = ((), (), s32[]{:S(2)}) async-start(), calls=%async_computation.10 | async-start | bytes 5242880 | tf_op jit(solution)/shard_map/all_gather | solution.py:257
  351.9 198.9 %all-gather.15.cloned.1.call-start = ((), (), s32[]{:S(2)}) async-start(), calls=%async_computation.12 | async-start | bytes 5242880 | tf_op jit(solution)/shard_map/all_gather | solution.py:282
  352.4 343.7 %reduce-scatter.9.cloned.1.call-start = ((), (), s32[]{:S(2)}) async-start(), calls=%async_computation.11 | async-start | bytes 10485760 | tf_op jit(solution)/shard_map/reduce_scatter | solution.py:263
  499.4 344.3 %reduce-scatter.11.cloned.1.call-start = ((), (), s32[]{:S(2)}) async-start(), calls=%async_computation.13 | async-start | bytes 10485760 | tf_op jit(solution)/shard_map/reduce_scatter | solution.py:290
  592.6 341.7 %all-gather.17.cloned.1.call-start = ((), (), s32[]{:S(2)}) async-start(), calls=%async_computation.14 | async-start | bytes 5242880 | tf_op jit(solution)/shard_map/all_gather | solution.py:299
  852.7 436.7 %reduce-scatter.17.cloned.1.call-start = ((), (), s32[]{:S(2)}) async-start(), calls=%async_computation.17 | async-start | bytes 9068544 | tf_op jit(solution)/shard_map/reduce_scatter | solution.py:333
  894.3 434.7 %reduce-scatter.15.cloned.1.call-start = ((), (), s32[]{:S(2)}) async-start(), calls=%async_computation.16 | async-start | bytes 4718592 | tf_op jit(solution)/shard_map/reduce_scatter | solution.py:332
  1278.6 197.0 %reduce-scatter.13.cloned.1.call-start = ((), (), s32[]{:S(2)}) async-start(), calls=%async_computation.15 | async-start | bytes 10485760 | tf_op jit(solution)/shard_map/reduce_scatter | solution.py:318
  1313.4 162.3 %copy-start.2 = (bf16[512,1024]{1,0:T(8,128)(2,1)S(1)}, bf16[512,1024]{1,0:T(8,128)(2,1)}, u32[]{:S(2)}) copy-start(bf16[512,1024]{1,0:T(8,128)(2,1)} %param.31) | copy-start | bytes 3145732
  1313.4 162.3 %copy-start.47 = (f32[1,1024]{1,0:T(1,128)S(1)}, f32[1,1024]{1,0:T(1,128)}, u32[]{:S(2)}) copy-start(f32[1,1024]{1,0:T(1,128)} %copy-done.46) | copy-start | bytes 12292
  1313.4 162.3 %copy-start.49 = (f32[512]{0:T(512)S(1)}, f32[512]{0:T(512)}, u32[]{:S(2)}) copy-start(f32[512]{0:T(512)} %copy-done.48) | copy-start | bytes 6148
  1330.6 147.1 %copy-start.56 = (f32[512]{0:T(512)S(1)}, f32[512]{0:T(512)}, u32[]{:S(2)}) copy-start(f32[512]{0:T(512)} %copy-done.55) | copy-start | bytes 6148
  1330.6 147.1 %copy-start.52 = (f32[512]{0:T(512)S(1)}, f32[512]{0:T(512)}, u32[]{:S(2)}) copy-start(f32[512]{0:T(512)} %copy-done.51) | copy-start | bytes 6148
  1332.6 147.7 %copy-start.57 = (f32[1024]{0:T(1024)S(1)}, f32[1024]{0:T(1024)}, u32[]{:S(2)}) copy-start(f32[1024]{0:T(1024)} %get-tuple-element.358) | copy-start | bytes 12292
  1332.6 189.5 %copy-start.59 = (f32[2,1024]{1,0:T(2,128)S(1)}, f32[2,1024]{1,0:T(2,128)}, u32[]{:S(2)}) copy-start(f32[2,1024]{1,0:T(2,128)} %param.45) | copy-start | bytes 24580
  1332.6 189.5 %copy-start.60 = (f32[2,1024]{1,0:T(2,128)S(1)}, f32[2,1024]{1,0:T(2,128)}, u32[]{:S(2)}) copy-start(f32[2,1024]{1,0:T(2,128)} %param.44) | copy-start | bytes 24580
  1332.6 190.1 %copy-start.14 = (bf16[512,1024]{1,0:T(8,128)(2,1)S(1)}, bf16[512,1024]{1,0:T(8,128)(2,1)}, u32[]{:S(2)}) copy-start(bf16[512,1024]{1,0:T(8,128)(2,1)} %param.32) | copy-start | bytes 3145732
  1332.6 190.1 %copy-start.54 = (f32[512]{0:T(512)S(1)}, f32[512]{0:T(512)}, u32[]{:S(2)}) copy-start(f32[512]{0:T(512)} %copy-done.53) | copy-start | bytes 6148
  (75 other events, 864.9 us)
Sparse Core Ops, SparseCore 0:
  10.0 30.6 all-gather.6
  42.8 80.7 all-gather.8
  205.0 142.9 reduce-scatter.6
  349.7 37.4 all-gather.10
  389.2 80.7 all-gather.12
  471.4 79.2 all-gather.14
  553.1 142.9 reduce-scatter.8
  698.5 145.1 reduce-scatter.10
  852.8 81.4 all-gather.16
  938.3 69.0 reduce-scatter.16
  1278.7 50.1 reduce-scatter.14
  1331.1 144.4 reduce-scatter.12
where the time goes:
time: 1550 us; the launch traced here: 1530 us
  waiting for transfers between devices  834 us (54%)
  matrix products  332 us (21%)
  local copies, waits for them, and re-layouts  191 us (12%)
  other arithmetic  102 us (7%)
  blocking collectives  41.1 us (3%)
  between operations  18.7 us (1%)
    reduce_scatter x1, waiting for transfers between devices, per_device(): lax.psum_scatter(jnp.einsum('ktf,kdf->td', gate_up_grad, gate_up_local, p...  148 us
    reduce_scatter x1, waiting for transfers between devices, per_device(): lax.psum_scatter(jnp.einsum('tc,dc->td', attended, out_local, preferred_e...  143 us
    reduce_scatter x1, waiting for transfers between devices, per_device(): lax.psum_scatter(jnp.einsum('ktc,kdc->td', qkv_grad, qkv_local, preferred...  139 us
    reduce_scatter x1, waiting for transfers between devices, per_device(): lax.psum_scatter(jnp.einsum('tf,df->td', activated, down_local, preferred...  102 us
    dot_general x4, matrix products, one_block(): jnp.einsum('hqk,qhe->khe', raw_grad, query_block, preferred_element_type=...  76.5 us
    all_gather x1, waiting for transfers between devices, per_device(): first_all = lax.all_gather(first_norm, 'tensor', axis=0, tiled=True)  74.9 us
    dot_general x4, matrix products, one_block(): jnp.einsum('hqk,khe->qhe', raw_grad, key_rows, preferred_element_type=jnp...  71.7 us
    all_gather x1, waiting for transfers between devices, per_device(): second_all = lax.all_gather(second_norm, 'tensor', axis=0, tiled=True)  66.5 us
  transfers between devices with their start and end apart: 12, of which 11 were waited for; matrix products, arithmetic and copies ran while one was open for 34% of the time, Pallas kernels for 0%

commit v1 on v0

v1 whole, which is shorter than its diff:
```python
import functools
import math

import jax
import jax.numpy as jnp
from jax import lax
from jax.experimental import pallas as pl
from jax.experimental.pallas import tpu as pltpu
from jax.sharding import PartitionSpec as P

HEAD_DIM = 64
SEQ_LEN = 1024
NORM_EPS = 1e-05
ROPE_BASE = 160000.0
ADAM_EPS = 1e-08
SCALE_EPS = 1e-06
PRECISE = lax.Precision.HIGHEST
BF = jnp.bfloat16
F32 = jnp.float32
ANY = pl.ANY


def dot(a,b,ca,cb):
    return lax.dot_general(a,b,(((ca,),(cb,)),((),())),preferred_element_type=F32)

def turn(x, cos, sin, lower):
    w=x.shape[1]
    sw=jnp.where(lower, pltpu.roll(x, w-32, 1), pltpu.roll(x, 32, 1))
    return x*cos+sw*sin

def lower_lanes(rows, cols):
    return lax.broadcasted_iota(jnp.int32,(rows,cols),1)%64<32

def wide(t, n):
    return t if n==1 else jnp.concatenate([t]*n,axis=1)

def fwd_attn_kernel(perm, a1, hid, gain, cos, sin, kseg, qseg, keep, wp,
                    q_out, k_out, v_out, o_out, lse_out, resid_out, a2_out, stat_out,
                    W, acc, bias, osc, sem, *, T, KV, C, R, S, SLAB, QB):
    s=pl.program_id(0)
    def fetch(step, slot):
        for r in range(R):
            pltpu.make_async_copy(wp.at[r, step], W.at[slot, :, pl.ds(pl.multiple_of(perm[r]*SLAB,SLAB),SLAB), :], sem.at[slot]).start()
    slot=lax.rem(s,2)
    @pl.when(s==0)
    def _():
        fetch(0,0)
        row=lax.broadcasted_iota(jnp.int32,(KV,T),0); col=lax.broadcasted_iota(jnp.int32,(KV,T),1)
        ok=(kseg[...]==qseg[...])|(row==col)
        bias[...]=jnp.where(ok,0.0,-1e30)
        acc[...]=jnp.zeros_like(acc)
    @pl.when(s+1<S)
    def _(): fetch(s+1,1-slot)
    pltpu.make_async_copy(W.at[slot],W.at[slot],sem.at[slot]).wait()
    n=C//128
    low_q=lower_lanes(T,C); low_k=lower_lanes(KV,C)
    cw=wide(cos[...],n); sw=wide(sin[...],n)
    q=dot(a1[:T,:],W[slot,0],1,0)
    q_out[0]=(turn(q,cw[:T],sw[:T],low_q).astype(BF)*BF(1/math.sqrt(HEAD_DIM))).astype(BF)
    k=dot(a1[...],W[slot,1],1,0)
    k_out[0]=turn(k,cw,sw,low_k).astype(BF)
    v_out[0]=dot(a1[...],W[slot,2],1,0).astype(BF)
    for p in range(n):
        kp=k_out[0,:,p*128:(p+1)*128]; vp=v_out[0,:,p*128:(p+1)*128]
        for b in range(T//QB):
            qp=q_out[0,b*QB:(b+1)*QB,p*128:(p+1)*128]
            half=lax.broadcasted_iota(jnp.int32,qp.shape,1)<64
            parts=[]
            for h in range(2):
                qm=jnp.where(half if h==0 else ~half,qp,jnp.zeros_like(qp))
                st=dot(kp,qm,1,1)+bias[:,b*QB:(b+1)*QB]
                m=jnp.max(st,axis=0,keepdims=True)
                e=jnp.exp(st-m)
                l=jnp.sum(e,axis=0,keepdims=True)
                ot=dot(vp,e.astype(BF),0,0)
                parts.append(ot[h*64:(h+1)*64]*(1.0/l))
                lse_out[0,pl.ds(2*p+h,1),b*QB:(b+1)*QB]=m+jnp.log(l)
            op=jnp.concatenate(parts,axis=0)
            osc[b*QB:(b+1)*QB,p*128:(p+1)*128]=op.T.astype(BF)
    o_out[0]=osc[...]
    acc[...]+=dot(osc[...],W[slot,3],1,1)
    @pl.when(s==S-1)
    def _():
        at=acc[...]
        rs=hid[...].astype(F32)+at
        resid_out[...]=rs
        mu=jnp.mean(rs,axis=1,keepdims=True); ce=rs-mu
        var=jnp.mean(ce*ce,axis=1,keepdims=True)
        a2_out[...]=(ce*lax.rsqrt(var+NORM_EPS)*gain[...]).astype(BF)
        kp=keep[...]
        s1=jnp.sum(kp*at*at,axis=0,keepdims=True); s2=jnp.sum(kp*rs*rs,axis=0,keepdims=True)
        stat_out[...]=jnp.concatenate([s1,s2],axis=0)

def full(shape):
    nd=len(shape)
    return pl.BlockSpec(shape,lambda *a:(0,)*nd)

def fwd_attn(perm,a1,hid,gain,cos,sin,kseg,qseg,keep,wp,QB=512):
    R,S,_,SLAB,C=wp.shape
    KV,D=a1.shape; T=hid.shape[0]; HG=C//HEAD_DIM
    sb=lambda rows:pl.BlockSpec((1,rows,C),lambda s,p:(s,0,0))
    gs=pltpu.PrefetchScalarGridSpec(num_scalar_prefetch=1,grid=(S,),
        in_specs=[full((KV,D)),full((T,D)),full((1,D)),full((KV,128)),full((KV,128)),full((KV,1)),full((1,T)),full((T,1)),pl.BlockSpec(memory_space=ANY)],
        out_specs=[sb(T),sb(KV),sb(KV),sb(T),pl.BlockSpec((1,HG,T),lambda s,p:(s,0,0)),full((T,D)),full((T,D)),full((2,D))],
        scratch_shapes=[pltpu.VMEM((2,4,D,C),BF),pltpu.VMEM((T,D),F32),pltpu.VMEM((KV,T),F32),pltpu.VMEM((T,C),BF),pltpu.SemaphoreType.DMA((2,))])
    sd=jax.ShapeDtypeStruct
    fl=2*(2*KV+2*T)*D*D+4*T*KV*D
    return pl.pallas_call(functools.partial(fwd_attn_kernel,T=T,KV=KV,C=C,R=R,S=S,SLAB=SLAB,QB=min(QB,T)),grid_spec=gs,
        out_shape=[sd((S,T,C),BF),sd((S,KV,C),BF),sd((S,KV,C),BF),sd((S,T,C),BF),sd((S,HG,T),F32),sd((T,D),F32),sd((T,D),BF),sd((2,D),F32)],
        cost_estimate=pl.CostEstimate(flops=fl,transcendentals=T*KV*D//HEAD_DIM,bytes_accessed=24<<20),name="attn_fwd")(perm,a1,hid,gain,cos,sin,kseg,qseg,keep,wp)

def gelu_parts(x):
    phi=0.5*(1.0+lax.erf(x*(1.0/math.sqrt(2.0))))
    den=jnp.exp(-0.5*x*x)*(1.0/math.sqrt(2.0*math.pi))
    return phi,den

def mlp_kernel(perm, slots, a2, g, resid, gain, keep, wp,
               out, dres_out, dresb_out, dresT_out, gg_out, stat_out, d0, d1,
               W, stg, hT, dgT, duT, y, da, sem, osem, *, T, D, HC, R, S, SLAB, TB):
    s=pl.program_id(0)
    slot=lax.rem(s,2)
    def fetch(step, sl):
        for r in range(R):
            pltpu.make_async_copy(wp.at[r, step], W.at[sl, :, :, pl.ds(pl.multiple_of(perm[r]*SLAB,SLAB),SLAB)], sem.at[sl]).start()
    @pl.when(s==0)
    def _(): fetch(0,0)
    @pl.when(s+1<S)
    def _(): fetch(s+1,1-slot)
    pltpu.make_async_copy(W.at[slot],W.at[slot],sem.at[slot]).wait()
    for b in range(T//TB):
        lo,hi=b*TB,(b+1)*TB
        ga=dot(W[slot,0],a2[lo:hi,:],1,1)
        up=dot(W[slot,1],a2[lo:hi,:],1,1)
        dh=dot(W[slot,2],g[lo:hi,:],1,1)
        phi,den=gelu_parts(ga)
        ge=ga*phi
        hT[:,lo:hi]=(ge*up).astype(BF)
        dgT[:,lo:hi]=(dh*up*(phi+ga*den)).astype(BF)
        duT[:,lo:hi]=(dh*ge).astype(BF)
    yc=dot(hT[...],W[slot,2],0,0)
    dc=dot(dgT[...],W[slot,0],0,0)+dot(duT[...],W[slot,1],0,0)
    @pl.when(s==0)
    def _():
        y[...]=yc; da[...]=dc
    @pl.when(s>0)
    def _():
        y[...]+=yc; da[...]+=dc
    @pl.when(s>=2)
    def _(): pltpu.make_async_copy(stg.at[slot],stg.at[slot],osem.at[slot]).wait()
    stg[slot,0]=dot(dgT[...],a2[...],1,0).astype(BF)
    stg[slot,1]=dot(duT[...],a2[...],1,0).astype(BF)
    stg[slot,2]=dot(hT[...],g[...],1,0).astype(BF)
    for r in range(R):
        dst=(d0,d1)[r%2]
        pltpu.make_async_copy(stg.at[slot,:,:,pl.ds(pl.multiple_of(perm[R+r]*SLAB,SLAB),SLAB)], dst.at[r//2, slots[s]], osem.at[slot]).start()
    @pl.when(s==S-1)
    def _():
        br=y[...]; rs=resid[...]; gf=g[...].astype(F32)
        res=rs+br
        out[...]=res.astype(BF)
        kp=keep[...]
        s1=jnp.sum(kp*br*br,axis=0,keepdims=True); s2=jnp.sum(kp*res*res,axis=0,keepdims=True)
        stat_out[...]=jnp.concatenate([s1,s2],axis=0)
        mu=jnp.mean(rs,axis=1,keepdims=True); ce=rs-mu
        rstd=lax.rsqrt(jnp.mean(ce*ce,axis=1,keepdims=True)+NORM_EPS)
        xh=ce*rstd
        d=da[...]
        gg_out[...]=jnp.sum(d*xh,axis=0,keepdims=True)
        e=d*gain[...]
        dr=gf+rstd*(e-jnp.mean(e,axis=1,keepdims=True)-xh*jnp.mean(e*xh,axis=1,keepdims=True))
        dres_out[...]=dr
        db=dr.astype(BF)
        dresb_out[...]=db
        dresT_out[...]=dr.T.astype(BF)
        for sl in range(min(S,2)):
            pltpu.make_async_copy(stg.at[sl],stg.at[sl],osem.at[sl]).wait()

def mlp(perm2,slots,a2,g,resid,gain,keep,wp,TB=256):
    R,S,_,HC,SLAB=wp.shape
    T,D=a2.shape
    A=pl.BlockSpec(memory_space=ANY)
    gs=pltpu.PrefetchScalarGridSpec(num_scalar_prefetch=2,grid=(S,),
        in_specs=[full((T,D)),full((T,D)),full((T,D)),full((1,D)),full((T,1)),A],
        out_specs=[full((T,D)),full((T,D)),full((T,D)),full((D,T)),full((1,D)),full((2,D)),A,A],
        scratch_shapes=[pltpu.VMEM((2,3,HC,D),BF),pltpu.VMEM((2,3,HC,D),BF)]+[pltpu.VMEM((HC,T),BF)]*3+[pltpu.VMEM((T,D),F32)]*2+[pltpu.SemaphoreType.DMA((2,)),pltpu.SemaphoreType.DMA((2,))])
    sd=jax.ShapeDtypeStruct
    piece=sd((R//2,S,3,HC,SLAB),BF)
    return pl.pallas_call(functools.partial(mlp_kernel,T=T,D=D,HC=HC,R=R,S=S,SLAB=SLAB,TB=min(TB,T)),grid_spec=gs,
        out_shape=[sd((T,D),BF),sd((T,D),F32),sd((T,D),BF),sd((D,T),BF),sd((1,D),F32),sd((2,D),F32),piece,piece],
        cost_estimate=pl.CostEstimate(flops=18*T*D*HC*S,transcendentals=2*T*HC*S,bytes_accessed=40<<20),name="mlp_both")(perm2,slots,a2,g,resid,gain,keep,wp)

def bwd_attn_kernel(perm, dres, cos, sin, kseg, qseg, q_in, k_in, v_in, lse_in, wp,
                    dq_out, dk_out, dv_out, W, bias, dob, dqs, dks, sem, *, T, KV, C, R, S, SLAB, S0, N):
    s=pl.program_id(0)
    slot=lax.rem(s,2)
    def fetch(step, sl):
        for r in range(R):
            pltpu.make_async_copy(wp.at[r, S0+step, 3], W.at[sl, pl.ds(pl.multiple_of(perm[r]*SLAB,SLAB),SLAB), :], sem.at[sl]).start()
    @pl.when(s==0)
    def _():
        fetch(0,0)
        row=lax.broadcasted_iota(jnp.int32,(KV,T),0); col=lax.broadcasted_iota(jnp.int32,(KV,T),1)
        ok=(kseg[...]==qseg[...])|(row==col)
        bias[...]=jnp.where(ok,0.0,-1e30)
    @pl.when(s+1<N)
    def _(): fetch(s+1,1-slot)
    pltpu.make_async_copy(W.at[slot],W.at[slot],sem.at[slot]).wait()
    n=C//128
    dob[...]=dot(dres[...],W[slot],1,0).astype(BF)
    for p in range(n):
        kp=k_in[0,:,p*128:(p+1)*128]; vp=v_in[0,:,p*128:(p+1)*128]
        qp=q_in[0,:,p*128:(p+1)*128]; dp_=dob[:,p*128:(p+1)*128]
        half=lax.broadcasted_iota(jnp.int32,qp.shape,1)<64
        parts=[]
        dvs=None
        for h in range(2):
            mk=half if h==0 else ~half
            qm=jnp.where(mk,qp,jnp.zeros_like(qp)); dm=jnp.where(mk,dp_,jnp.zeros_like(dp_))
            pt=jnp.exp(dot(kp,qm,1,1)+bias[...]-lse_in[0,2*p+h:2*p+h+1,:])
            dpt=dot(vp,dm,1,1)
            delta=jnp.sum(pt*dpt,axis=0,keepdims=True)
            ds=(pt*(dpt-delta)).astype(BF)
            dv=dot(pt.astype(BF),dm,1,0); dk=dot(ds,qm,1,0)
            dqt=dot(kp,ds,0,0)
            parts.append(dqt[h*64:(h+1)*64])
            if h==0: dva,dka=dv,dk
            else: dva,dka=dva+dv,dka+dk
        dqs[:,p*128:(p+1)*128]=jnp.concatenate(parts,axis=0).T*(1.0/math.sqrt(HEAD_DIM))
        dks[:,p*128:(p+1)*128]=dka
        dv_out[0,:,p*128:(p+1)*128]=dva.astype(BF)
    cw=wide(cos[...],n); sw=wide(sin[...],n)
    dq_out[0]=turn(dqs[...],cw[:T],-sw[:T],lower_lanes(T,C)).astype(BF)
    dk_out[0]=turn(dks[...],cw,-sw,lower_lanes(KV,C)).astype(BF)

def bwd_attn(perm,dres,cos,sin,kseg,qseg,q,k,v,lse,wp,S0=0,N=None):
    R,S,_,SLAB,C=wp.shape
    T,D=dres.shape; KV=k.shape[1]; HG=C//HEAD_DIM
    N=S if N is None else N
    ib=lambda rows:pl.BlockSpec((1,rows,C),lambda s,p:(s+S0,0,0))
    ob=lambda rows:pl.BlockSpec((1,rows,C),lambda s,p:(s,0,0))
    gs=pltpu.PrefetchScalarGridSpec(num_scalar_prefetch=1,grid=(N,),
        in_specs=[full((T,D)),full((KV,128)),full((KV,128)),full((KV,1)),full((1,T)),ib(T),ib(KV),ib(KV),pl.BlockSpec((1,HG,T),lambda s,p:(s+S0,0,0)),pl.BlockSpec(memory_space=ANY)],
        out_specs=[ob(T),ob(KV),ob(KV)],
        scratch_shapes=[pltpu.VMEM((2,D,C),BF),pltpu.VMEM((KV,T),F32),pltpu.VMEM((T,C),BF),pltpu.VMEM((T,C),F32),pltpu.VMEM((KV,C),F32),pltpu.SemaphoreType.DMA((2,))])
    sd=jax.ShapeDtypeStruct
    fl=(2*T*D*C+10*T*KV*C)*N
    return pl.pallas_call(functools.partial(bwd_attn_kernel,T=T,KV=KV,C=C,R=R,S=S,SLAB=SLAB,S0=S0,N=N),grid_spec=gs,
        out_shape=[sd((N,T,C),BF),sd((N,KV,C),BF),sd((N,KV,C),BF)],
        cost_estimate=pl.CostEstimate(flops=fl*4,transcendentals=T*KV*N*C//HEAD_DIM,bytes_accessed=(8<<20)*N//S+(2<<20)),name="attn_bwd")(perm,dres,cos,sin,kseg,qseg,q,k,v,lse,wp)

def grad_attn_kernel(perm, slots, a1T, dresT, xhat, o_in, dq_in, dk_in, dv_in, wp,
                     da_own, da_far, gg_out, d0, d1, W, stg, acc, sem, osem, *, T, KV, C, R, S, SLAB):
    s=pl.program_id(0)
    slot=lax.rem(s,2)
    def fetch(step, sl):
        for r in range(R):
            pltpu.make_async_copy(wp.at[r, step, pl.ds(0,3)], W.at[sl, :, pl.ds(pl.multiple_of(perm[r]*SLAB,SLAB),SLAB), :], sem.at[sl]).start()
    @pl.when(s==0)
    def _(): fetch(0,0)
    @pl.when(s+1<S)
    def _(): fetch(s+1,1-slot)
    @pl.when(s>=2)
    def _(): pltpu.make_async_copy(stg.at[slot],stg.at[slot],osem.at[slot]).wait()
    stg[slot,0]=dot(a1T[:,:T],dq_in[0],1,0).astype(BF)
    stg[slot,1]=dot(a1T[...],dk_in[0],1,0).astype(BF)
    stg[slot,2]=dot(a1T[...],dv_in[0],1,0).astype(BF)
    stg[slot,3]=dot(dresT[...],o_in[0],1,0).astype(BF)
    for r in range(R):
        dst=(d0,d1)[r%2]
        pltpu.make_async_copy(stg.at[slot,:,pl.ds(pl.multiple_of(perm[R+r]*SLAB,SLAB),SLAB),:], dst.at[r//2, slots[s]], osem.at[slot]).start()
    pltpu.make_async_copy(W.at[slot],W.at[slot],sem.at[slot]).wait()
    c=dot(dk_in[0],W[slot,1],1,1)+dot(dv_in[0],W[slot,2],1,1)
    cq=dot(dq_in[0],W[slot,0],1,1)
    @pl.when(s==0)
    def _():
        acc[...]=c
        acc[:T,:]=acc[:T,:]+cq
    @pl.when(s>0)
    def _():
        acc[...]=acc[...]+c
        acc[:T,:]=acc[:T,:]+cq
    @pl.when(s==S-1)
    def _():
        gg_out[...]=jnp.sum(acc[...]*xhat[...].astype(F32),axis=0,keepdims=True)
        da_own[...]=acc[:T,:]
        da_far[...]=acc[T:,:].astype(BF)
        for sl in range(min(S,2)):
            pltpu.make_async_copy(stg.at[sl],stg.at[sl],osem.at[sl]).wait()

def grad_attn(perm2,slots,a1T,dresT,xhat,o,dq,dk,dv,wp):
    R,S,_,SLAB,C=wp.shape
    D,T=dresT.shape; KV=dk.shape[1]
    A=pl.BlockSpec(memory_space=ANY)
    ib=lambda rows:pl.BlockSpec((1,rows,C),lambda s,p,q:(s,0,0))
    gs=pltpu.PrefetchScalarGridSpec(num_scalar_prefetch=2,grid=(S,),
        in_specs=[full((D,KV)),full((D,T)),full((KV,D)),ib(T),ib(T),ib(KV),ib(KV),A],
        out_specs=[full((T,D)),full((KV-T,D)),full((1,D)),A,A],
        scratch_shapes=[pltpu.VMEM((2,3,D,C),BF),pltpu.VMEM((2,4,D,C),BF),pltpu.VMEM((KV,D),F32),pltpu.SemaphoreType.DMA((2,)),pltpu.SemaphoreType.DMA((2,))])
    sd=jax.ShapeDtypeStruct
    piece=sd((R//2,S,4,SLAB,C),BF)
    return pl.pallas_call(functools.partial(grad_attn_kernel,T=T,KV=KV,C=C,R=R,S=S,SLAB=SLAB),grid_spec=gs,
        out_shape=[sd((T,D),F32),sd((KV-T,D),BF),sd((1,D),F32),piece,piece],
        cost_estimate=pl.CostEstimate(flops=2*D*D*(2*T+2*KV+2*KV+T),transcendentals=0,bytes_accessed=30<<20),name="attn_grad")(perm2,slots,a1T,dresT,xhat,o,dq,dk,dv,wp)


def ring_order(count):
    return list(range(0, count, 2)) + list(range(1, count, 2))[::-1]


def swap_dp(value, bit, owners):
    return lax.ppermute(value, "dp", [(i, i ^ bit) for i in range(owners)])


def to_ring_pred(value, shards):
    ring = ring_order(shards)
    return lax.ppermute(
        value, "tensor", [(ring[p], ring[(p - 1) % shards]) for p in range(shards)]
    )


def add_low(one, two):
    return (one.astype(F32) + two.astype(F32)).astype(BF)


def halve(pieces, bits, owners):
    for bit in bits:
        live = sorted(bits[bits.index(bit):], reverse=True)
        axis = live.index(bit)
        send = lax.index_in_dim(pieces, 1, axis, keepdims=False)
        keep = lax.index_in_dim(pieces, 0, axis, keepdims=False)
        pieces = add_low(keep, swap_dp(send, bit, owners))
    return pieces


def reduce_pieces(even, odd, cut, owners, shards):
    mine = add_low(even, swap_dp(odd, 1, owners))
    bits = [1 << b for b in range(1, owners.bit_length() - 1)]
    mine = mine.reshape((2,) * len(bits) + mine.shape[1:])
    low = halve(mine[..., :cut, :], bits[::-1], owners)
    high = halve(mine[..., cut:, :], bits, owners)
    both = jnp.concatenate([low, high], axis=-2)
    moving = both[shards - 1]
    for left in range(shards - 2, -1, -1):
        moving = to_ring_pred(moving, shards)
        moving = moving.astype(F32) + both[left].astype(F32)
        if left:
            moving = moving.astype(BF)
    return moving


def all_sum(value, owners, shards):
    for axis, count in (("dp", owners), ("tensor", shards)):
        step = 1
        while step < count:
            value = value + lax.ppermute(value, axis, [(i, i ^ step) for i in range(count)])
            step *= 2
    return value


def soap_block(grad_block, first, second, left, right, step_size, beta_one, beta_two):
    half_turn = jnp.einsum("kab,kac->kbc", left, grad_block, precision=PRECISE)
    rotated = jnp.einsum("kbc,kce->kbe", half_turn, right, precision=PRECISE)
    first_new = beta_one * first + (1.0 - beta_one) * rotated
    second_new = beta_two * second + (1.0 - beta_two) * rotated * rotated
    direction = first_new / (jnp.sqrt(second_new) + ADAM_EPS)
    back_half = jnp.einsum("kab,kbe->kae", left, direction, precision=PRECISE)
    turned = jnp.einsum("kae,kce->kac", back_half, right, precision=PRECISE)
    factor = jnp.sqrt(jnp.mean(direction * direction, axis=(1, 2))) * lax.rsqrt(
        jnp.mean(turned * turned, axis=(1, 2)) + SCALE_EPS
    )
    update = -step_size * factor[:, None, None] * turned
    return (first_new, second_new, update, factor)


def per_device(
    hidden_in, out_grad, attn_weight, mlp_weight, norm_gain,
    attn_first, attn_second, attn_left, attn_right,
    mlp_first, mlp_second, mlp_left, mlp_right,
    gain_first, gain_second, owner_rows, segment_ids, positions, valid,
    step, learn_rate, beta_first, beta_second,
):
    owners = lax.axis_size("dp")
    shards = lax.axis_size("tensor")
    dp_index = lax.axis_index("dp")
    place = lax.axis_index("tensor")
    rows, width = hidden_in.shape
    slab = attn_weight.shape[1]
    hid_cols = mlp_weight.shape[2]
    span = SEQ_LEN // rows
    within = place % span
    base = place - within
    gain_rows = norm_gain.astype(F32)

    def from_peer(value, ahead):
        pairs = [(g + (w + ahead) % span, g + w) for g in range(0, shards, span) for w in range(span)]
        return lax.ppermute(value, "tensor", pairs)

    def sequence_rows(column):
        return jnp.concatenate(
            [lax.dynamic_slice_in_dim(column, (base + (within + d) % span) * rows, rows, 0) for d in range(span)]
        )

    both = ("dp", "tensor")
    attn_all = lax.all_gather(attn_weight, both, axis=0, tiled=False).reshape((owners, shards) + attn_weight.shape)
    mlp_turned = jnp.swapaxes(mlp_weight, 1, 2)
    mlp_all = lax.all_gather(mlp_turned, both, axis=0, tiled=False).reshape((owners, shards) + mlp_turned.shape)

    slot_ids = jnp.arange(owners, dtype=jnp.int32)
    rel_owner = jnp.sum(
        jnp.where((slot_ids[:, None] ^ dp_index) == slot_ids[None, :], owner_rows[None, :], 0), axis=1
    )
    ring = ring_order(shards)
    ring_place = jnp.array([ring.index(z) for z in range(shards)], jnp.int32)
    my_place = jnp.sum(jnp.where(jnp.arange(shards) == place, ring_place, 0))
    slots = (my_place - ring_place) % shards
    attn_perm = jnp.concatenate([owner_rows, rel_owner]).astype(jnp.int32)
    joined = 128 // slab if slab < 128 else 1
    if joined == 1:
        mlp_perm = attn_perm
    else:
        inverse = jnp.sum(jnp.where(owner_rows[None, :] == slot_ids[:, None], slot_ids[None, :], 0), axis=1)
        mlp_all = jnp.take(mlp_all, inverse, axis=0).reshape((owners // joined, joined) + mlp_all.shape[1:])
        mlp_all = jnp.moveaxis(mlp_all, 1, 4)
        mlp_all = mlp_all.reshape(mlp_all.shape[:4] + (joined * slab,))
        blocks = jnp.arange(owners // joined, dtype=jnp.int32)
        mlp_perm = jnp.concatenate([blocks, blocks])

    hidden_seq = jnp.concatenate([hidden_in] + [from_peer(hidden_in, d) for d in range(1, span)]).astype(F32)
    centred = hidden_seq - jnp.mean(hidden_seq, axis=-1, keepdims=True)
    rstd = lax.rsqrt(jnp.mean(centred * centred, axis=-1, keepdims=True) + NORM_EPS)
    xhat = centred * rstd
    first_norm = (xhat * gain_rows[0]).astype(BF)
    xhat_low = xhat.astype(BF)

    seg = sequence_rows(segment_ids)
    keep_seq = sequence_rows(valid)
    pos = sequence_rows(positions)
    half_dim = HEAD_DIM // 2
    frequency = jnp.exp(jnp.arange(half_dim, dtype=F32) * (-2.0 * math.log(ROPE_BASE) / HEAD_DIM))
    angles = pos.astype(F32)[:, None] * frequency[None, :]
    cos_half, sin_half = jnp.cos(angles), jnp.sin(angles)
    cos_table = jnp.concatenate([cos_half] * 4, axis=1)
    sin_table = jnp.concatenate([-sin_half, sin_half] * 2, axis=1)
    key_seg = jnp.where(keep_seq > 0, seg, -1)[:, None]
    query_seg = seg[None, :rows]
    keep_own = keep_seq[:rows].astype(F32)[:, None]

    queries, keys, values, attended, log_sums, resid, second_norm, stat_a = fwd_attn(
        attn_perm, first_norm, hidden_in, gain_rows[1:2], cos_table, sin_table, key_seg, query_seg, keep_own, attn_all
    )
    output, dresid, dres_low, dres_turned, gain_two, stat_m, mlp_even, mlp_odd = mlp(
        mlp_perm, slots, second_norm, out_grad, resid, gain_rows[1:2], keep_own, mlp_all
    )
    if joined > 1:
        merged = jnp.stack([mlp_even, mlp_odd], axis=1).reshape((owners // joined,) + mlp_even.shape[1:])
        merged = merged.reshape(merged.shape[:-1] + (joined, slab))
        merged = jnp.moveaxis(merged, -2, 1).reshape((owners,) + mlp_even.shape[1:-1] + (slab,))
        merged = jnp.take(merged, rel_owner, axis=0)
        mlp_even, mlp_odd = merged[0::2], merged[1::2]
    mlp_cut = -(-hid_cols // 32) * 16
    mlp_sum = reduce_pieces(mlp_even, mlp_odd, mlp_cut, owners, shards)
    mlp_grad = jnp.swapaxes(mlp_sum, 1, 2)

    parts = [
        bwd_attn(attn_perm, dres_low, cos_table, sin_table, key_seg, query_seg, queries, keys, values, log_sums, attn_all, S0=s, N=1)
        for s in range(shards)
    ]
    dq, dk, dv = (jnp.concatenate([p[i] for p in parts]) for i in range(3))
    first_turned = first_norm.T
    da_own, da_far, gain_one, attn_even, attn_odd = grad_attn(
        attn_perm, slots, first_turned, dres_turned, xhat_low, attended, dq, dk, dv, attn_all
    )
    first_grad = da_own
    for d in range(1, span):
        pairs = [(g + w, g + (w + d) % span) for g in range(0, shards, span) for w in range(span)]
        first_grad = first_grad + lax.ppermute(da_far[(d - 1) * rows : d * rows], "tensor", pairs).astype(F32)
    attn_grad = reduce_pieces(attn_even, attn_odd, slab // 2, owners, shards)

    scaled = first_grad * gain_rows[0]
    own_hat = xhat[:rows]
    input_part = rstd[:rows] * (
        scaled
        - jnp.mean(scaled, axis=-1, keepdims=True)
        - own_hat * jnp.mean(scaled * own_hat, axis=-1, keepdims=True)
    )
    input_grad = (dresid + input_part).astype(BF)

    sums = jnp.concatenate([jnp.sum(stat_a, axis=1), jnp.sum(stat_m, axis=1), jnp.sum(keep_own)[None]])
    small = jnp.concatenate([gain_one, gain_two, jnp.pad(sums, (0, width - 5))[None]], axis=0)
    small = all_sum(small, owners, shards)
    gain_grad = small[:2]
    stat_sums = small[2]

    step_count = step.astype(F32)
    step_size = (
        learn_rate
        * jnp.sqrt(1.0 - jnp.power(beta_second, step_count))
        / (1.0 - jnp.power(beta_first, step_count))
    )
    attn_first_new, attn_second_new, attn_update, attn_scale = soap_block(
        attn_grad, attn_first, attn_second, attn_left, attn_right, step_size, beta_first, beta_second
    )
    mlp_first_new, mlp_second_new, mlp_update, mlp_scale = soap_block(
        mlp_grad, mlp_first, mlp_second, mlp_left, mlp_right, step_size, beta_first, beta_second
    )
    gain_first_new = beta_first * gain_first + (1.0 - beta_first) * gain_grad
    gain_second_new = beta_second * gain_second + (1.0 - beta_second) * gain_grad * gain_grad
    gain_update = -step_size * gain_first_new / (jnp.sqrt(gain_second_new) + ADAM_EPS)
    root_means = jnp.sqrt(stat_sums[:4] / (stat_sums[4] * width))
    norm_scale = jnp.concatenate([attn_scale, mlp_scale], axis=0).reshape(7, 1, 1)
    return (
        output, input_grad, attn_grad, mlp_grad, gain_grad,
        attn_first_new, attn_second_new, mlp_first_new, mlp_second_new,
        gain_first_new, gain_second_new, attn_update, mlp_update, gain_update,
        norm_scale, root_means,
    )


def solution(mesh):
    rows = P(("dp", "tensor"), None)
    block = P(None, "dp", "tensor")
    return jax.shard_map(
        per_device,
        mesh=mesh,
        in_specs=(rows, rows, block, block, P()) + (block,) * 8 + (P(),) * 3 + (P("dp"),) * 3 + (P(),) * 4,
        out_specs=(rows, rows, block, block, P(), block, block, block, block, P(), P(), block, block, P(), block, P()),
        check_vma=False,
    )
```

time: 1550 us -> 530 us (0.34)
  waiting for transfers between devices: 834 us -> 265 us
  matrix products: 332 us -> 23.1 us
  local copies, waits for them, and re-layouts: 191 us -> 10.2 us
  Pallas kernels: 0 us -> 139 us
  other arithmetic: 102 us -> 45.4 us
  blocking collectives: 41.1 us -> 0 us
  starting transfers between devices: 0.49 us -> 23.1 us
    reduce_scatter x6 -> x0, waiting for transfers between devices: 544 us -> none  [the longest x1 148 us: per_device(): lax.psum_scatter(jnp.einsum('ktf,kdf->td', gate_up_grad, gate_up_local, p...]
    dot_general x40 -> x0, matrix products: 304 us -> none  [the longest x4 76.5 us: one_block(): jnp.einsum('hqk,qhe->khe', raw_grad, query_block, preferred_element_type=...]
    all_gather x6 -> x2, waiting for transfers between devices: 288 us -> 127 us  [the longest x1 83.9 us: per_device(): lax.all_gather(mlp_turned, both, axis=0, tiled=False)]
    pallas_call x0 -> x7, Pallas kernels: none -> 139 us  [the longest x4 47 us: bwd_attn(): pl.pallas_call(functools.partial(bwd_attn_kernel, T=T, KV=KV, C=C, R=R, S...]
    ppermute x0 -> x23, waiting for transfers between devices: none -> 137 us  [the longest x10 67.1 us: swap_dp(): return lax.ppermute(value, 'dp', [(i, i ^ bit) for i in range(owners)])]
    dynamic_update_slice x12 -> x0, local copies, waits for them, and re-layouts: 51.9 us -> none  [per_device(): lax.map(sequence_forward, (queries, key_rows, value_rows, seg_seq, keep_s...]
    psum x1 -> x0, blocking collectives: 41.1 us -> none  [per_device(): gain_grad = lax.psum(gain_part, ('dp', 'tensor'))]
    another operation x14 -> x0, other arithmetic: 29.6 us -> none  [the longest x2 25.6 us: per_device(): gate_up_grad = jnp.stack([gate_grad, up_grad]).astype(jnp.bfloat16)]
  transfers between devices with their start and end apart: 12 -> 25, of which waited for: 11 -> 19; matrix products, arithmetic and copies ran while one was open for 34% -> 10% of each run, Pallas kernels for 0% -> 14%
where the time goes in v1:
time: 530 us; the launch traced here: 525 us
  waiting for transfers between devices  265 us (50%)
  Pallas kernels  139 us (26%)
  other arithmetic  45.4 us (9%)
  starting transfers between devices  23.1 us (4%)
  matrix products  23.1 us (4%)
  between operations  18.5 us (3%)
  local copies, waits for them, and re-layouts  10.2 us (2%)
    all_gather x1, waiting for transfers between devices, per_device(): lax.all_gather(mlp_turned, both, axis=0, tiled=False)  83.9 us
    ppermute x10, waiting for transfers between devices, swap_dp(): return lax.ppermute(value, 'dp', [(i, i ^ bit) for i in range(owners)])  67.1 us
    pallas_call x4, Pallas kernels, bwd_attn(): pl.pallas_call(functools.partial(bwd_attn_kernel, T=T, KV=KV, C=C, R=R, S...  47 us
    all_gather x1, waiting for transfers between devices, per_device(): lax.all_gather(attn_weight, both, axis=0, tiled=False)  43.3 us
    ppermute x6, waiting for transfers between devices, to_ring_pred(): lax.ppermute(value, 'tensor', [(ring[p], ring[(p - 1) % shards]) for p in...  42.4 us
    pallas_call x1, Pallas kernels, mlp(): pl.pallas_call(functools.partial(mlp_kernel, T=T, D=D, HC=HC, R=R, S=S, S...  40.4 us
    pallas_call x1, Pallas kernels, fwd_attn(): pl.pallas_call(functools.partial(fwd_attn_kernel, T=T, KV=KV, C=C, R=R, S...  29.4 us
    pallas_call x1, Pallas kernels, grad_attn(): pl.pallas_call(functools.partial(grad_attn_kernel, T=T, KV=KV, C=C, R=R,...  22.5 us
  transfers between devices with their start and end apart: 25, of which 19 were waited for; matrix products, arithmetic and copies ran while one was open for 10% of the time, Pallas kernels for 14%

profile of v1, /device:TPU:0, one launch (start us, length us, event | category | flops | bytes accessed | tf_op | source)
XLA Modules:
  0.0 525.0 jit_solution(6409094060309935388)
XLA Ops:
  26.1 14.6 %collective-permute-done = bf16[512,1024]{1,0:T(8,128)(2,1)S(1)} collective-permute-done((bf16[512,1024]{1,0:T(8,128)(2,1)}, bf16[512,1024]{1,0:T(8,128)(2,1)S(1)}, u32[]{:S(2)}, u32[]{:S(2)}) %collective-permute-start) | collective-permute-done | bytes 1048608 | tf_op jit(solution)/shard_map/ppermute | solution.py:396
  41.8 4.5 fusion.43
  46.3 3.9 copy.93.a1T
  50.2 43.3 %all-gather.5.cloned.1.call-done = bf16[128,128,256]{2,1,0:T(8,128)(2,1)} async-done(((bf16[4,128,256]{2,1,0:T(8,128)(2,1)}), bf16[128,128,256]{2,1,0:T(8,128)(2,1)}) %all-gather.5.cloned.1.call-update) | async-done | bytes 8388624 | tf_op jit(solution)/shard_map/all_gather | solution.py:404
  93.5 29.4 %attn_fwd.1 = (bf16[4,512,256]{2,1,0:T(8,128)(2,1)}, bf16[4,1024,256]{2,1,0:T(8,128)(2,1)}, bf16[4,1024,256]{2,1,0:T(8,128)(2,1)}, bf16[4,512,256]{2,1,0:T(8,128...) custom-call(s32[16]{0:T(128)} %pad_add_fusion.1.perm, ...), custom_call_target="tpu_custom_call" | custom-call | flops 8589934592 | bytes 25165824 | tf_op jit(solution)/shard_map/attn_fwd/pallas_call | solution.py:108
  122.9 83.9 %all-gather.7.cloned.1.call-done = bf16[96,656,128]{2,1,0:T(8,128)(2,1)} async-done(((bf16[3,656,128]{2,1,0:T(8,128)(2,1)}), bf16[96,656,128]{2,1,0:T(8,128)(2,1)}) %all-gather.7.cloned.1.call-update) | async-done | bytes 16121872 | tf_op jit(solution)/shard_map/all_gather | solution.py:406
  206.9 40.4 %mlp_both.1 = (bf16[512,1024]{1,0:T(8,128)(2,1)}, f32[512,1024]{1,0:T(8,128)}, bf16[512,1024]{1,0:T(8,128)(2,1)}, bf16[1024,512]{1,0:T(8,128)(2,1)}, f32[1,1024]...) custom-call(s32[16]{0:T(128)} %pad_add_fusion.1.perm, ...), custom_call_target="tpu_custom_call" | custom-call | flops 24763170816 | bytes 41943040 | tf_op jit(solution)/shard_map/mlp_both/pallas_call | solution.py:188
  247.3 11.5 %attn_bwd.7 = (bf16[1,512,256]{2,1,0:T(8,128)(2,1)}, bf16[1,1024,256]{2,1,0:T(8,128)(2,1)}, bf16[1,1024,256]{2,1,0:T(8,128)(2,1)}) custom-call(s32[16]{0:T(128)} %pad_add_fusion.1.perm, bf16[512,1024]{1,0:T(8,128)(2,1)} %get-tuple-element.55.dres, f32[1024,128]{1,0:T(8,128)} %pad_maximum_fusion.4.cos, f32[1024,128]{1,0:T(8,128)} %pad_maximum_fusion.5.sin, ...), custom_call_target="tpu_custom_call" | custom-call | flops 6442450944 | bytes 4194304 | tf_op jit(solution)/shard_map/attn_bwd/pallas_call | solution.py:247
  258.8 11.8 %attn_bwd.6 = (bf16[1,512,256]{2,1,0:T(8,128)(2,1)}, bf16[1,1024,256]{2,1,0:T(8,128)(2,1)}, bf16[1,1024,256]{2,1,0:T(8,128)(2,1)}) custom-call(s32[16]{0:T(128)} %pad_add_fusion.1.perm, bf16[512,1024]{1,0:T(8,128)(2,1)} %get-tuple-element.55.dres, f32[1024,128]{1,0:T(8,128)} %pad_maximum_fusion.4.cos, f32[1024,128]{1,0:T(8,128)} %pad_maximum_fusion.5.sin, ...), custom_call_target="tpu_custom_call" | custom-call | flops 6442450944 | bytes 4194304 | tf_op jit(solution)/shard_map/attn_bwd/pallas_call | solution.py:247
  270.9 11.5 %attn_bwd.5 = (bf16[1,512,256]{2,1,0:T(8,128)(2,1)}, bf16[1,1024,256]{2,1,0:T(8,128)(2,1)}, bf16[1,1024,256]{2,1,0:T(8,128)(2,1)}) custom-call(s32[16]{0:T(128)} %pad_add_fusion.1.perm, bf16[512,1024]{1,0:T(8,128)(2,1)} %get-tuple-element.55.dres, f32[1024,128]{1,0:T(8,128)} %pad_maximum_fusion.4.cos, f32[1024,128]{1,0:T(8,128)} %pad_maximum_fusion.5.sin, ...), custom_call_target="tpu_custom_call" | custom-call | flops 6442450944 | bytes 4194304 | tf_op jit(solution)/shard_map/attn_bwd/pallas_call | solution.py:247
  282.5 12.1 %attn_bwd.4 = (bf16[1,512,256]{2,1,0:T(8,128)(2,1)}, bf16[1,1024,256]{2,1,0:T(8,128)(2,1)}, bf16[1,1024,256]{2,1,0:T(8,128)(2,1)}) custom-call(s32[16]{0:T(128)} %pad_add_fusion.1.perm, bf16[512,1024]{1,0:T(8,128)(2,1)} %get-tuple-element.55.dres, f32[1024,128]{1,0:T(8,128)} %pad_maximum_fusion.4.cos, f32[1024,128]{1,0:T(8,128)} %pad_maximum_fusion.5.sin, ...), custom_call_target="tpu_custom_call" | custom-call | flops 6442450944 | bytes 4194304 | tf_op jit(solution)/shard_map/attn_bwd/pallas_call | solution.py:247
  300.8 22.5 %attn_grad.1 = (f32[512,1024]{1,0:T(8,128)}, bf16[512,1024]{1,0:T(8,128)(2,1)}, f32[1,1024]{1,0:T(1,128)}, bf16[4,4,4,128,256]{4,3,2,1,0:T(8,128)(2,1)}, bf16[4,4,4,128,256]{4,3,2,1,0:T(8,128)(2,1)}) custom-call(s32[16]{0:T(128)} %pad_add_fusion.1.perm, s32[4]{0:T(128)} %and_select_fusion.slots, bf16[1024,1024]{1,0:T(8,128)(2,1)} %copy.93.a1T, ...), custom_call_target="tpu_custom_call" | custom-call | flops 11811160064 | bytes 31457280 | tf_op jit(solution)/shard_map/attn_grad/pallas_call | solution.py:301
  325.7 4.9 collective-permute-done.18
  350.7 5.2 add_convert_fusion.1
  358.3 5.1 add_convert_fusion
  365.2 12.2 %collective-permute-done.3 = bf16[2,4,4,64,256]{4,3,2,1,0:T(8,128)(2,1)S(1)} collective-permute-done((bf16[2,4,4,64,256]{4,3,2,1,0:T(8,128)(2,1)S(1)}, bf16[2,4,4,64,256]{4,3,2,1,0:T(8,128)(2,1)S(1)}, u32[]{:S(2)}, u32[]{:S(2)}) %collective-permute-start.3) | collective-permute-done | bytes 1048608 | tf_op jit(solution)/shard_map/ppermute | solution.py:311
  377.4 6.4 %collective-permute-done.5 = bf16[2,4,4,64,256]{4,3,2,1,0:T(8,128)(2,1)S(1)} collective-permute-done((bf16[2,4,4,64,256]{4,3,2,1,0:T(8,128)(2,1)S(1)}, bf16[2,4,4,64,256]{4,3,2,1,0:T(8,128)(2,1)S(1)}, u32[]{:S(2)}, u32[]{:S(2)}) %collective-permute-start.5) | collective-permute-done | bytes 1048608 | tf_op jit(solution)/shard_map/ppermute | solution.py:311
  388.3 43.9 %collective-permute-done.4 = bf16[4,4,64,256]{3,2,1,0:T(8,128)(2,1)S(1)} collective-permute-done((bf16[4,4,64,256]{3,2,1,0:T(8,128)(2,1)S(1)}, bf16[4,4,64,256]{3,2,1,0:T(8,128)(2,1)S(1)}, u32[]{:S(2)}, u32[]{:S(2)}) %collective-permute-start.4) | collective-permute-done | bytes 524320 | tf_op jit(solution)/shard_map/ppermute | solution.py:311
  443.1 8.4 %collective-permute-done.8 = bf16[4,128,256]{2,1,0:T(8,128)(2,1)S(1)} collective-permute-done((bf16[4,128,256]{2,1,0:T(8,128)(2,1)S(1)}, bf16[4,128,256]{2,1,0:T(8,128)(2,1)S(1)}, u32[]{:S(2)}, u32[]{:S(2)}) %collective-permute-start.8) | collective-permute-done | bytes 262176 | tf_op jit(solution)/shard_map/ppermute | solution.py:316
  460.3 9.5 %collective-permute-done.15 = bf16[3,656,128]{2,1,0:T(8,128)(2,1)S(1)} collective-permute-done((bf16[3,656,128]{2,1,0:T(8,128)(2,1)S(1)}, bf16[3,656,128]{2,1,0:T(8,128)(2,1)S(1)}, u32[]{:S(2)}, u32[]{:S(2)}) %collective-permute-start.15) | collective-permute-done | bytes 503840 | tf_op jit(solution)/shard_map/ppermute | solution.py:316
  472.9 12.2 %collective-permute-done.16 = bf16[3,656,128]{2,1,0:T(8,128)(2,1)S(1)} collective-permute-done((bf16[3,656,128]{2,1,0:T(8,128)(2,1)S(1)}, bf16[3,656,128]{2,1,0:T(8,128)(2,1)S(1)}, u32[]{:S(2)}, u32[]{:S(2)}) %collective-permute-start.16) | collective-permute-done | bytes 503840 | tf_op jit(solution)/shard_map/ppermute | solution.py:316
  487.8 7.7 %collective-permute-done.17 = bf16[3,656,128]{2,1,0:T(8,128)(2,1)S(1)} collective-permute-done((bf16[3,656,128]{2,1,0:T(8,128)(2,1)S(1)}, bf16[3,656,128]{2,1,0:T(8,128)(2,1)S(1)}, u32[]{:S(2)}, u32[]{:S(2)}) %collective-permute-start.17) | collective-permute-done | bytes 503840 | tf_op jit(solution)/shard_map/ppermute | solution.py:316
  498.1 11.5 %multiply_reduce_fusion.2 = (f32[3]{0:T(128)S(1)}, f32[3,128,656]{1,2,0:T(8,128)S(1)}, f32[3,128,656]{1,2,0:T(8,128)S(1)}) fusion(f32[]{:T(128)S(6)} %sub.53, f32[3,128,656]{1,2,0:T(8,128)S(1)} %copy-done.6, f32[]{:T(128)S(6)} %copy.115, f32[]{:T(128)S(6)} %sub.52, f32[3,128,656]{1,2,0:T(8,128)S(1)} %copy-done.7, f32[]{:T(128)S(6)} %copy.114, ...), kind=kOutput, calls=%fused_computation.61 | convolution fusion | flops 1985759232 | bytes 10202140 | tf_op jit(solution)/shard_map/kbc,kce->kbe/dot_general | solution.py:362
  510.9 5.3 %multiply_reduce_fusion.1 = (f32[3]{0:T(128)S(1)}, f32[3,128,656]{1,2,0:T(8,128)S(1)}) fusion(f32[3,656,128]{2,1,0:T(8,128)S(1)} %fusion.42, f32[3,656,656]{2,1,0:T(8,128)S(1)} %bitcast.137), kind=kOutput, calls=%fused_computation.60 | convolution fusion | flops 1983492096 | bytes 7179276 | tf_op jit(solution)/shard_map/kae,kce->kac/dot_general | solution.py:367
  (205 shorter events, 84.7 us)
Async XLA Ops:
  7.2 86.3 %all-gather.5.cloned.1.call-start = ((), (), s32[]{:S(2)}) async-start(), calls=%async_computation | async-start | bytes 8650752 | tf_op jit(solution)/shard_map/all_gather | solution.py:404
  7.9 198.9 %all-gather.7.cloned.1.call-start = ((), (), s32[]{:S(2)}) async-start(), calls=%async_computation.1 | async-start | bytes 16625664 | tf_op jit(solution)/shard_map/all_gather | solution.py:406
  8.7 32.1 %collective-permute-start = (bf16[512,1024]{1,0:T(8,128)(2,1)}, bf16[512,1024]{1,0:T(8,128)(2,1)S(1)}, u32[]{:S(2)}, u32[]{:S(2)}) collective-permute-start(bf16[512,1024]{1,0:T(8,128)(2,1)} %hid.1), channel_id=1, source_target_pairs={{1,0},{0,1},{3,2},{2,3},{5,4},{4,5},{7,6},{6,7},{9,8},{8,9},{11,10... | collective-permute-start | bytes 3145736 | tf_op jit(solution)/shard_map/ppermute | solution.py:396
  270.6 87.7 %collective-permute-start.10 = (bf16[4,4,3,656,128]{4,3,2,1,0:T(8,128)(2,1)}, bf16[4,4,3,656,128]{4,3,2,1,0:T(8,128)(2,1)}, u32[]{:S(2)}, u32[]{:S(2)}) collective-permute-start(bf16[4,4,3,656,128]{4,3,2,1,0:T(8,128)(2,1)} %get-tuple-element.77), channel_id=1, source_target_pairs={{0,4},{4,0},{8,12},{12,8},{16,20},{20,16},{24,28},{28,24},{1,5},{5... | collective-permute-start | bytes 24182792 | tf_op jit(solution)/shard_map/ppermute | solution.py:311
  323.3 27.3 %collective-permute-start.2 = (bf16[4,4,4,128,256]{4,3,2,1,0:T(8,128)(2,1)}, bf16[4,4,4,128,256]{4,3,2,1,0:T(8,128)(2,1)}, u32[]{:S(2)}, u32[]{:S(2)}) collective-permute-start(bf16[4,4,4,128,256]{4,3,2,1,0:T(8,128)(2,1)} %get-tuple-element.75), channel_id=1, source_target_pairs={{0,4},{4,0},{8,12},{12,8},{16,20},{20,16},{24,28},{28,24},{1,5},{5... | collective-permute-start | bytes 12582920 | tf_op jit(solution)/shard_map/ppermute | solution.py:311
  325.4 5.2 collective-permute-start.18
  331.3 3.8 collective-permute-start.19
  335.8 3.8 collective-permute-start.20
  343.4 4.9 collective-permute-start.22
  347.7 40.0 %collective-permute-start.1 = (bf16[512,1024]{1,0:T(8,128)(2,1)}, bf16[512,1024]{1,0:T(8,128)(2,1)S(1)}, u32[]{:S(2)}, u32[]{:S(2)}) collective-permute-start(bf16[512,1024]{1,0:T(8,128)(2,1)} %get-tuple-element.73), channel_id=1, source_target_pairs={{0,1},{1,0},{2,3},{3,2},{4,5},{5,4},{6,7},{7,6},{8,9},{9,8},{10,11... | collective-permute-start | bytes 3145736 | tf_op jit(solution)/shard_map/ppermute | solution.py:476
  356.0 21.4 %collective-permute-start.3 = (bf16[2,4,4,64,256]{4,3,2,1,0:T(8,128)(2,1)S(1)}, bf16[2,4,4,64,256]{4,3,2,1,0:T(8,128)(2,1)S(1)}, u32[]{:S(2)}, u32[]{:S(2)}) collective-permute-start(bf16[2,4,4,64,256]{4,3,2,1,0:T(8,128)(2,1)S(1)} %slice_bitcast_fusion.6), channel_id=1, source_target_pairs={{0,16},{4,20},{8,24},{12,28},{16,0},{20,4},{24,8},{28,12},{1,17},{... | collective-permute-start | bytes 3145736 | tf_op jit(solution)/shard_map/ppermute | solution.py:311
  357.6 26.2 %collective-permute-start.5 = (bf16[2,4,4,64,256]{4,3,2,1,0:T(8,128)(2,1)S(1)}, bf16[2,4,4,64,256]{4,3,2,1,0:T(8,128)(2,1)S(1)}, u32[]{:S(2)}, u32[]{:S(2)}) collective-permute-start(bf16[2,4,4,64,256]{4,3,2,1,0:T(8,128)(2,1)S(1)} %slice_bitcast_fusion.4), channel_id=1, source_target_pairs={{0,8},{4,12},{8,0},{12,4},{16,24},{20,28},{24,16},{28,20},{1,9},{5... | collective-permute-start | bytes 3145736 | tf_op jit(solution)/shard_map/ppermute | solution.py:311
  363.7 71.8 %collective-permute-start.13 = (bf16[2,4,3,320,128]{4,3,2,1,0:T(8,128)(2,1)S(1)}, bf16[2,4,3,320,128]{4,3,2,1,0:T(8,128)(2,1)S(1)}, u32[]{:S(2)}, u32[]{:S(2)}) collective-permute-start(bf16[2,4,3,320,128]{4,3,2,1,0:T(8,128)(2,1)S(1)} %slice_bitcast_fusion.2), channel_id=1, source_target_pairs={{0,8},{4,12},{8,0},{12,4},{16,24},{20,28},{24,16},{28,20},{1,9},{5... | collective-permute-start | bytes 5898248 | tf_op jit(solution)/shard_map/ppermute | solution.py:311
  384.8 53.7 %collective-permute-start.11 = (bf16[2,4,3,336,128]{4,3,2,1,0:T(8,128)(2,1)S(1)}, bf16[2,4,3,336,128]{4,3,2,1,0:T(8,128)(2,1)S(1)}, u32[]{:S(2)}, u32[]{:S(2)}) collective-permute-start(bf16[2,4,3,336,128]{4,3,2,1,0:T(8,128)(2,1)S(1)} %slice_bitcast_fusion), channel_id=1, source_target_pairs={{0,16},{4,20},{8,24},{12,28},{16,0},{20,4},{24,8},{28,12},{1,17},{... | collective-permute-start | bytes 6193160 | tf_op jit(solution)/shard_map/ppermute | solution.py:311
  385.5 46.6 %collective-permute-start.4 = (bf16[4,4,64,256]{3,2,1,0:T(8,128)(2,1)S(1)}, bf16[4,4,64,256]{3,2,1,0:T(8,128)(2,1)S(1)}, u32[]{:S(2)}, u32[]{:S(2)}) collective-permute-start(bf16[4,4,64,256]{3,2,1,0:T(8,128)(2,1)S(1)} %slice_bitcast_fusion.14), channel_id=1, source_target_pairs={{0,8},{4,12},{8,0},{12,4},{16,24},{20,28},{24,16},{28,20},{1,9},{5... | collective-permute-start | bytes 1572872 | tf_op jit(solution)/shard_map/ppermute | solution.py:311
  387.0 46.6 %collective-permute-start.6 = (bf16[4,4,64,256]{3,2,1,0:T(8,128)(2,1)S(1)}, bf16[4,4,64,256]{3,2,1,0:T(8,128)(2,1)S(1)}, u32[]{:S(2)}, u32[]{:S(2)}) collective-permute-start(bf16[4,4,64,256]{3,2,1,0:T(8,128)(2,1)S(1)} %slice_bitcast_fusion.12), channel_id=1, source_target_pairs={{0,16},{4,20},{8,24},{12,28},{16,0},{20,4},{24,8},{28,12},{1,17},{... | collective-permute-start | bytes 1572872 | tf_op jit(solution)/shard_map/ppermute | solution.py:311
  433.8 9.1 %collective-permute-start.7 = (bf16[4,128,256]{2,1,0:T(8,128)(2,1)S(1)}, bf16[4,128,256]{2,1,0:T(8,128)(2,1)S(1)}, u32[]{:S(2)}, u32[]{:S(2)}) collective-permute-start(bf16[4,128,256]{2,1,0:T(8,128)(2,1)S(1)} %fusion.30), channel_id=1, source_target_pairs={{0,1},{2,0},{3,2},{1,3},{4,5},{6,4},{7,6},{5,7},{8,9},{10,8},{11,1... | collective-permute-start | bytes 786440 | tf_op jit(solution)/shard_map/ppermute | solution.py:316
  436.2 17.8 %collective-permute-start.14 = (bf16[4,3,320,128]{3,2,1,0:T(8,128)(2,1)S(1)}, bf16[4,3,320,128]{3,2,1,0:T(8,128)(2,1)S(1)}, u32[]{:S(2)}, u32[]{:S(2)}) collective-permute-start(bf16[4,3,320,128]{3,2,1,0:T(8,128)(2,1)S(1)} %slice_bitcast_fusion.10), channel_id=1, source_target_pairs={{0,16},{4,20},{8,24},{12,28},{16,0},{20,4},{24,8},{28,12},{1,17},{... | collective-permute-start | bytes 2949128 | tf_op jit(solution)/shard_map/ppermute | solution.py:311
  439.2 16.1 %collective-permute-start.12 = (bf16[4,3,336,128]{3,2,1,0:T(8,128)(2,1)S(1)}, bf16[4,3,336,128]{3,2,1,0:T(8,128)(2,1)S(1)}, u32[]{:S(2)}, u32[]{:S(2)}) collective-permute-start(bf16[4,3,336,128]{3,2,1,0:T(8,128)(2,1)S(1)} %slice_bitcast_fusion.8), channel_id=1, source_target_pairs={{0,8},{4,12},{8,0},{12,4},{16,24},{20,28},{24,16},{28,20},{1,9},{5... | collective-permute-start | bytes 3096584 | tf_op jit(solution)/shard_map/ppermute | solution.py:311
  443.0 8.5 %collective-permute-start.8 = (bf16[4,128,256]{2,1,0:T(8,128)(2,1)S(1)}, bf16[4,128,256]{2,1,0:T(8,128)(2,1)S(1)}, u32[]{:S(2)}, u32[]{:S(2)}) collective-permute-start(bf16[4,128,256]{2,1,0:T(8,128)(2,1)S(1)} %fusion.19), channel_id=1, source_target_pairs={{0,1},{2,0},{3,2},{1,3},{4,5},{6,4},{7,6},{5,7},{8,9},{10,8},{11,1... | collective-permute-start | bytes 786440 | tf_op jit(solution)/shard_map/ppermute | solution.py:316
  451.6 7.9 %collective-permute-start.9 = (bf16[4,128,256]{2,1,0:T(8,128)(2,1)S(1)}, bf16[4,128,256]{2,1,0:T(8,128)(2,1)S(1)}, u32[]{:S(2)}, u32[]{:S(2)}) collective-permute-start(bf16[4,128,256]{2,1,0:T(8,128)(2,1)S(1)} %fusion.18), channel_id=1, source_target_pairs={{0,1},{2,0},{3,2},{1,3},{4,5},{6,4},{7,6},{5,7},{8,9},{10,8},{11,1... | collective-permute-start | bytes 786440 | tf_op jit(solution)/shard_map/ppermute | solution.py:316
  455.5 14.3 %collective-permute-start.15 = (bf16[3,656,128]{2,1,0:T(8,128)(2,1)S(1)}, bf16[3,656,128]{2,1,0:T(8,128)(2,1)S(1)}, u32[]{:S(2)}, u32[]{:S(2)}) collective-permute-start(bf16[3,656,128]{2,1,0:T(8,128)(2,1)S(1)} %fusion.23), channel_id=1, source_target_pairs={{0,1},{2,0},{3,2},{1,3},{4,5},{6,4},{7,6},{5,7},{8,9},{10,8},{11,1... | collective-permute-start | bytes 1511432 | tf_op jit(solution)/shard_map/ppermute | solution.py:316
  469.9 15.2 %collective-permute-start.16 = (bf16[3,656,128]{2,1,0:T(8,128)(2,1)S(1)}, bf16[3,656,128]{2,1,0:T(8,128)(2,1)S(1)}, u32[]{:S(2)}, u32[]{:S(2)}) collective-permute-start(bf16[3,656,128]{2,1,0:T(8,128)(2,1)S(1)} %fusion.13), channel_id=1, source_target_pairs={{0,1},{2,0},{3,2},{1,3},{4,5},{6,4},{7,6},{5,7},{8,9},{10,8},{11,1... | collective-permute-start | bytes 1511432 | tf_op jit(solution)/shard_map/ppermute | solution.py:316
  485.3 10.1 %collective-permute-start.17 = (bf16[3,656,128]{2,1,0:T(8,128)(2,1)S(1)}, bf16[3,656,128]{2,1,0:T(8,128)(2,1)S(1)}, u32[]{:S(2)}, u32[]{:S(2)}) collective-permute-start(bf16[3,656,128]{2,1,0:T(8,128)(2,1)S(1)} %fusion.12), channel_id=1, source_target_pairs={{0,1},{2,0},{3,2},{1,3},{4,5},{6,4},{7,6},{5,7},{8,9},{10,8},{11,1... | collective-permute-start | bytes 1511432 | tf_op jit(solution)/shard_map/ppermute | solution.py:316
  (43 other events, 1200.1 us)
Sparse Core Ops, SparseCore 0:
  11.0 82.5 all-gather.4
  96.4 110.4 all-gather.6

commit v2 on v1

v2 whole, which is shorter than its diff:
```python
import functools
import math

import jax
import jax.numpy as jnp
from jax import lax
from jax.experimental import pallas as pl
from jax.experimental.pallas import tpu as pltpu
from jax.sharding import PartitionSpec as P

HEAD_DIM = 64
SEQ_LEN = 1024
NORM_EPS = 1e-05
ROPE_BASE = 160000.0
ADAM_EPS = 1e-08
SCALE_EPS = 1e-06
PRECISE = lax.Precision.HIGHEST
BF = jnp.bfloat16
F32 = jnp.float32
ANY = pl.ANY


def dot(a,b,ca,cb):
    return lax.dot_general(a,b,(((ca,),(cb,)),((),())),preferred_element_type=F32)

def turn(x, cos, sin, lower):
    w=x.shape[1]
    sw=jnp.where(lower, pltpu.roll(x, w-32, 1), pltpu.roll(x, 32, 1))
    return x*cos+sw*sin

def lower_lanes(rows, cols):
    return lax.broadcasted_iota(jnp.int32,(rows,cols),1)%64<32

def wide(t, n):
    return t if n==1 else jnp.concatenate([t]*n,axis=1)

def fetch_pieces(refs, metas, perm, step, copy):
    for ref, meta in zip(refs, metas):
        if meta is None:
            for r in range(ref.shape[0]):
                copy(ref.at[r, step], perm[r])
        else:
            r, first, count, total = meta
            if count == total:
                copy(ref.at[step], perm[r])
            else:
                @pl.when((step >= first) & (step < first + count))
                def _(ref=ref, r=r, first=first):
                    copy(ref.at[jnp.clip(step - first, 0, ref.shape[0] - 1)], perm[r])

def fwd_attn_kernel(perm, a1, hid, gain, cos, sin, kseg, qseg, keep, *rest, T, KV, C, metas, S, SLAB, QB, S0, N):
    wps = rest[:len(metas)]
    rest = rest[len(metas):]
    if S0:
        acc_in, rest = rest[0], rest[6:]
    q_out, k_out, v_out, o_out, lse_out = rest[:5]
    if S0+N==S:
        resid_out, a2_out, stat_out, acc = rest[5:9]
    else:
        acc = rest[5]
    W, bias, osc, sem = rest[-4:]
    s=pl.program_id(0)
    def fetch(step, slot):
        fetch_pieces(wps, metas, perm, S0+step, lambda src, blk: pltpu.make_async_copy(src, W.at[slot, :, pl.ds(pl.multiple_of(blk*SLAB,SLAB),SLAB), :], sem.at[slot]).start())
    slot=lax.rem(s,2)
    @pl.when(s==0)
    def _():
        fetch(0,0)
        row=lax.broadcasted_iota(jnp.int32,(KV,T),0); col=lax.broadcasted_iota(jnp.int32,(KV,T),1)
        ok=(kseg[...]==qseg[...])|(row==col)
        bias[...]=jnp.where(ok,0.0,-1e30)
        acc[...]=acc_in[...] if S0 else jnp.zeros_like(acc)
    @pl.when(s+1<N)
    def _(): fetch(s+1,1-slot)
    pltpu.make_async_copy(W.at[slot],W.at[slot],sem.at[slot]).wait()
    n=C//128
    low_q=lower_lanes(T,C); low_k=lower_lanes(KV,C)
    cw=wide(cos[...],n); sw=wide(sin[...],n)
    q=dot(a1[:T,:],W[slot,0],1,0)
    q_out[0]=(turn(q,cw[:T],sw[:T],low_q).astype(BF)*BF(1/math.sqrt(HEAD_DIM))).astype(BF)
    k=dot(a1[...],W[slot,1],1,0)
    k_out[0]=turn(k,cw,sw,low_k).astype(BF)
    v_out[0]=dot(a1[...],W[slot,2],1,0).astype(BF)
    for p in range(n):
        kp=k_out[0,:,p*128:(p+1)*128]; vp=v_out[0,:,p*128:(p+1)*128]
        for b in range(T//QB):
            qp=q_out[0,b*QB:(b+1)*QB,p*128:(p+1)*128]
            half=lax.broadcasted_iota(jnp.int32,qp.shape,1)<64
            parts=[]
            for h in range(2):
                qm=jnp.where(half if h==0 else ~half,qp,jnp.zeros_like(qp))
                st=dot(kp,qm,1,1)+bias[:,b*QB:(b+1)*QB]
                m=jnp.max(st,axis=0,keepdims=True)
                e=jnp.exp(st-m)
                l=jnp.sum(e,axis=0,keepdims=True)
                ot=dot(vp,e.astype(BF),0,0)
                parts.append(ot[h*64:(h+1)*64]*(1.0/l))
                lse_out[0,pl.ds(2*p+h,1),b*QB:(b+1)*QB]=m+jnp.log(l)
            op=jnp.concatenate(parts,axis=0)
            osc[b*QB:(b+1)*QB,p*128:(p+1)*128]=op.T.astype(BF)
    o_out[0]=osc[...]
    acc[...]+=dot(osc[...],W[slot,3],1,1)
    if S0+N<S:
        return
    @pl.when(s==N-1)
    def _():
        at=acc[...]
        rs=hid[...].astype(F32)+at
        resid_out[...]=rs
        mu=jnp.mean(rs,axis=1,keepdims=True); ce=rs-mu
        var=jnp.mean(ce*ce,axis=1,keepdims=True)
        a2_out[...]=(ce*lax.rsqrt(var+NORM_EPS)*gain[...]).astype(BF)
        kp=keep[...]
        s1=jnp.sum(kp*at*at,axis=0,keepdims=True); s2=jnp.sum(kp*rs*rs,axis=0,keepdims=True)
        stat_out[...]=jnp.concatenate([s1,s2],axis=0)

def full(shape):
    nd=len(shape)
    return pl.BlockSpec(shape,lambda *a:(0,)*nd)

def fwd_attn(perm,a1,hid,gain,cos,sin,kseg,qseg,keep,pieces,S0=0,N=None,carry=(),QB=512):
    wps,metas,S,SLAB,C=pieces
    N=S if N is None else N
    KV,D=a1.shape; T=hid.shape[0]; HG=C//HEAD_DIM
    A=pl.BlockSpec(memory_space=ANY)
    sb=lambda rows:pl.BlockSpec((1,rows,C),lambda s,p:(s+S0,0,0))
    sd=jax.ShapeDtypeStruct
    last=S0+N==S
    tail=[sd((T,D),F32),sd((T,D),BF),sd((2,D),F32)] if last else [sd((T,D),F32)]
    gs=pltpu.PrefetchScalarGridSpec(num_scalar_prefetch=1,grid=(N,),
        in_specs=[full((KV,D)),full((T,D)),full((1,D)),full((KV,128)),full((KV,128)),full((KV,1)),full((1,T)),full((T,1))]+[A]*len(wps)+([full((T,D))]+[A]*5 if S0 else []),
        out_specs=[sb(T),sb(KV),sb(KV),sb(T),pl.BlockSpec((1,HG,T),lambda s,p:(s+S0,0,0))]+[full(t.shape) for t in tail],
        scratch_shapes=([pltpu.VMEM((T,D),F32)] if last else [])+[pltpu.VMEM((2,4,D,C),BF),pltpu.VMEM((KV,T),F32),pltpu.VMEM((T,C),BF),pltpu.SemaphoreType.DMA((2,))])
    return pl.pallas_call(functools.partial(fwd_attn_kernel,T=T,KV=KV,C=C,metas=metas,S=S,SLAB=SLAB,QB=min(QB,T),S0=S0,N=N),grid_spec=gs,
        out_shape=[sd((S,T,C),BF),sd((S,KV,C),BF),sd((S,KV,C),BF),sd((S,T,C),BF),sd((S,HG,T),F32)]+tail,
        input_output_aliases={10+len(wps)+i:i for i in range(5)} if S0 else {},
        cost_estimate=pl.CostEstimate(flops=1,transcendentals=0,bytes_accessed=1),name="attn_fwd")(perm,a1,hid,gain,cos,sin,kseg,qseg,keep,*wps,*((carry[5],)+tuple(carry[:5]) if S0 else ()))

def gelu_parts(x):
    phi=0.5*(1.0+lax.erf(x*(1.0/math.sqrt(2.0))))
    den=jnp.exp(-0.5*x*x)*(1.0/math.sqrt(2.0*math.pi))
    return phi,den

def mlp_kernel(perm, slots, a2, g, resid, gain, keep, *rest, T, D, HC, R, metas, S, SLAB, TB, S0, N):
    wps = rest[:len(metas)]
    rest = rest[len(metas):]
    if S0:
        y_in, da_in = rest[:2]
        rest = rest[2:]
    if S0+N==S:
        out, dres_out, dresb_out, dresT_out, gg_out, stat_out = rest[:6]
        rest = rest[6:]
        d0, d1, y, da = rest[:4]
    else:
        y, da, d0, d1 = rest[:4]
    W, stg, hT, dgT, duT, sem, osem = rest[4:]
    s=pl.program_id(0)
    slot=lax.rem(s,2)
    def fetch(step, sl):
        fetch_pieces(wps, metas, perm, S0+step, lambda src, blk: pltpu.make_async_copy(src, W.at[sl, :, :, pl.ds(pl.multiple_of(blk*SLAB,SLAB),SLAB)], sem.at[sl]).start())
    @pl.when(s==0)
    def _(): fetch(0,0)
    @pl.when(s+1<N)
    def _(): fetch(s+1,1-slot)
    pltpu.make_async_copy(W.at[slot],W.at[slot],sem.at[slot]).wait()
    for b in range(T//TB):
        lo,hi=b*TB,(b+1)*TB
        ga=dot(W[slot,0],a2[lo:hi,:],1,1)
        up=dot(W[slot,1],a2[lo:hi,:],1,1)
        dh=dot(W[slot,2],g[lo:hi,:],1,1)
        phi,den=gelu_parts(ga)
        ge=ga*phi
        hT[:,lo:hi]=(ge*up).astype(BF)
        dgT[:,lo:hi]=(dh*up*(phi+ga*den)).astype(BF)
        duT[:,lo:hi]=(dh*ge).astype(BF)
    yc=dot(hT[...],W[slot,2],0,0)
    dc=dot(dgT[...],W[slot,0],0,0)+dot(duT[...],W[slot,1],0,0)
    @pl.when(s==0)
    def _():
        y[...]=yc+y_in[...] if S0 else yc
        da[...]=dc+da_in[...] if S0 else dc
    @pl.when(s>0)
    def _():
        y[...]+=yc; da[...]+=dc
    @pl.when(s>=2)
    def _(): pltpu.make_async_copy(stg.at[slot],stg.at[slot],osem.at[slot]).wait()
    stg[slot,0]=dot(dgT[...],a2[...],1,0).astype(BF)
    stg[slot,1]=dot(duT[...],a2[...],1,0).astype(BF)
    stg[slot,2]=dot(hT[...],g[...],1,0).astype(BF)
    for r in range(R):
        dst=(d0,d1)[r%2]
        pltpu.make_async_copy(stg.at[slot,:,:,pl.ds(pl.multiple_of(perm[R+r]*SLAB,SLAB),SLAB)], dst.at[r//2, slots[S0+s]-S0], osem.at[slot]).start()
    if S0+N==S:
        @pl.when(s==N-1)
        def _():
            br=y[...]; rs=resid[...]; gf=g[...].astype(F32)
            res=rs+br
            out[...]=res.astype(BF)
            kp=keep[...]
            s1=jnp.sum(kp*br*br,axis=0,keepdims=True); s2=jnp.sum(kp*res*res,axis=0,keepdims=True)
            stat_out[...]=jnp.concatenate([s1,s2],axis=0)
            mu=jnp.mean(rs,axis=1,keepdims=True); ce=rs-mu
            rstd=lax.rsqrt(jnp.mean(ce*ce,axis=1,keepdims=True)+NORM_EPS)
            xh=ce*rstd
            d=da[...]
            gg_out[...]=jnp.sum(d*xh,axis=0,keepdims=True)
            e=d*gain[...]
            dr=gf+rstd*(e-jnp.mean(e,axis=1,keepdims=True)-xh*jnp.mean(e*xh,axis=1,keepdims=True))
            dres_out[...]=dr
            db=dr.astype(BF)
            dresb_out[...]=db
            dresT_out[...]=dr.T.astype(BF)
    @pl.when(s==N-1)
    def _():
        for sl in range(min(N,2)):
            pltpu.make_async_copy(stg.at[sl],stg.at[sl],osem.at[sl]).wait()

def mlp(perm2,slots,a2,g,resid,gain,keep,pieces,S0=0,N=None,carry=(),TB=256):
    wps,metas,S,SLAB,HC=pieces
    N=S if N is None else N
    R=perm2.shape[0]//2
    T,D=a2.shape
    A=pl.BlockSpec(memory_space=ANY)
    sd=jax.ShapeDtypeStruct
    last=S0+N==S
    outs=[sd((T,D),BF),sd((T,D),F32),sd((T,D),BF),sd((D,T),BF),sd((1,D),F32),sd((2,D),F32)] if last else [sd((T,D),F32)]*2
    gs=pltpu.PrefetchScalarGridSpec(num_scalar_prefetch=2,grid=(N,),
        in_specs=[full((T,D)),full((T,D)),full((T,D)),full((1,D)),full((T,1))]+[A]*len(wps)+[full((T,D))]*len(carry),
        out_specs=[full(o.shape) for o in outs]+[A,A],
        scratch_shapes=([pltpu.VMEM((T,D),F32)]*2 if last else [])+[pltpu.VMEM((2,3,HC,D),BF),pltpu.VMEM((2,3,HC,D),BF)]+[pltpu.VMEM((HC,T),BF)]*3+[pltpu.SemaphoreType.DMA((2,)),pltpu.SemaphoreType.DMA((2,))])
    piece=sd((R//2,N,3,HC,SLAB),BF)
    return pl.pallas_call(functools.partial(mlp_kernel,T=T,D=D,HC=HC,R=R,metas=metas,S=S,SLAB=SLAB,TB=min(TB,T),S0=S0,N=N),grid_spec=gs,
        out_shape=outs+[piece,piece],
        cost_estimate=pl.CostEstimate(flops=1,transcendentals=0,bytes_accessed=1),name="mlp_both")(perm2,slots,a2,g,resid,gain,keep,*wps,*carry)

def bwd_attn_kernel(perm, dres, cos, sin, kseg, qseg, q_in, k_in, v_in, lse_in, *rest, T, KV, C, metas, S, SLAB, S0, N):
    wps = rest[:len(metas)]
    dq_out, dk_out, dv_out, W, bias, dob, dqs, dks, sem = rest[-9:]
    s=pl.program_id(0)
    slot=lax.rem(s,2)
    def fetch(step, sl):
        fetch_pieces(wps, metas, perm, S0+step, lambda src, blk: pltpu.make_async_copy(src.at[3], W.at[sl, pl.ds(pl.multiple_of(blk*SLAB,SLAB),SLAB), :], sem.at[sl]).start())
    @pl.when(s==0)
    def _():
        fetch(0,0)
        row=lax.broadcasted_iota(jnp.int32,(KV,T),0); col=lax.broadcasted_iota(jnp.int32,(KV,T),1)
        ok=(kseg[...]==qseg[...])|(row==col)
        bias[...]=jnp.where(ok,0.0,-1e30)
    @pl.when(s+1<N)
    def _(): fetch(s+1,1-slot)
    pltpu.make_async_copy(W.at[slot],W.at[slot],sem.at[slot]).wait()
    n=C//128
    dob[...]=dot(dres[...],W[slot],1,0).astype(BF)
    for p in range(n):
        kp=k_in[0,:,p*128:(p+1)*128]; vp=v_in[0,:,p*128:(p+1)*128]
        qp=q_in[0,:,p*128:(p+1)*128]; dp_=dob[:,p*128:(p+1)*128]
        half=lax.broadcasted_iota(jnp.int32,qp.shape,1)<64
        parts=[]
        dvs=None
        for h in range(2):
            mk=half if h==0 else ~half
            qm=jnp.where(mk,qp,jnp.zeros_like(qp)); dm=jnp.where(mk,dp_,jnp.zeros_like(dp_))
            pt=jnp.exp(dot(kp,qm,1,1)+bias[...]-lse_in[0,2*p+h:2*p+h+1,:])
            dpt=dot(vp,dm,1,1)
            delta=jnp.sum(pt*dpt,axis=0,keepdims=True)
            ds=(pt*(dpt-delta)).astype(BF)
            dv=dot(pt.astype(BF),dm,1,0); dk=dot(ds,qm,1,0)
            dqt=dot(kp,ds,0,0)
            parts.append(dqt[h*64:(h+1)*64])
            if h==0: dva,dka=dv,dk
            else: dva,dka=dva+dv,dka+dk
        dqs[:,p*128:(p+1)*128]=jnp.concatenate(parts,axis=0).T*(1.0/math.sqrt(HEAD_DIM))
        dks[:,p*128:(p+1)*128]=dka
        dv_out[0,:,p*128:(p+1)*128]=dva.astype(BF)
    cw=wide(cos[...],n); sw=wide(sin[...],n)
    dq_out[0]=turn(dqs[...],cw[:T],-sw[:T],lower_lanes(T,C)).astype(BF)
    dk_out[0]=turn(dks[...],cw,-sw,lower_lanes(KV,C)).astype(BF)

def bwd_attn(perm,dres,cos,sin,kseg,qseg,q,k,v,lse,pieces,S0=0,N=None,carry=()):
    wps,metas,S,SLAB,C=pieces
    T,D=dres.shape; KV=k.shape[1]; HG=C//HEAD_DIM
    N=S if N is None else N
    ib=lambda rows:pl.BlockSpec((1,rows,C),lambda s,p:(s+S0,0,0))
    gs=pltpu.PrefetchScalarGridSpec(num_scalar_prefetch=1,grid=(N,),
        in_specs=[full((T,D)),full((KV,128)),full((KV,128)),full((KV,1)),full((1,T)),ib(T),ib(KV),ib(KV),pl.BlockSpec((1,HG,T),lambda s,p:(s+S0,0,0))]+[pl.BlockSpec(memory_space=ANY)]*(len(wps)+len(carry)),
        out_specs=[ib(T),ib(KV),ib(KV)],
        scratch_shapes=[pltpu.VMEM((2,D,C),BF),pltpu.VMEM((KV,T),F32),pltpu.VMEM((T,C),BF),pltpu.VMEM((T,C),F32),pltpu.VMEM((KV,C),F32),pltpu.SemaphoreType.DMA((2,))])
    sd=jax.ShapeDtypeStruct
    fl=(2*T*D*C+10*T*KV*C)*N
    return pl.pallas_call(functools.partial(bwd_attn_kernel,T=T,KV=KV,C=C,metas=metas,S=S,SLAB=SLAB,S0=S0,N=N),grid_spec=gs,
        out_shape=[sd((S,T,C),BF),sd((S,KV,C),BF),sd((S,KV,C),BF)],
        input_output_aliases={10+len(wps)+i:i for i in range(len(carry))},
        cost_estimate=pl.CostEstimate(flops=1,transcendentals=0,bytes_accessed=1),name="attn_bwd")(perm,dres,cos,sin,kseg,qseg,q,k,v,lse,*wps,*carry)

def grad_attn_kernel(perm, slots, a1T, dresT, xhat, o_in, dq_in, dk_in, dv_in, *rest, T, KV, C, R, metas, S, SLAB):
    wps = rest[:len(metas)]
    da_own, da_far, gg_out, d0, d1, W, stg, acc, sem, osem = rest[len(metas):]
    s=pl.program_id(0)
    slot=lax.rem(s,2)
    def fetch(step, sl):
        fetch_pieces(wps, metas, perm, step, lambda src, blk: pltpu.make_async_copy(src.at[pl.ds(0,3)], W.at[sl, :, pl.ds(pl.multiple_of(blk*SLAB,SLAB),SLAB), :], sem.at[sl]).start())
    @pl.when(s==0)
    def _(): fetch(0,0)
    @pl.when(s+1<S)
    def _(): fetch(s+1,1-slot)
    @pl.when(s>=2)
    def _(): pltpu.make_async_copy(stg.at[slot],stg.at[slot],osem.at[slot]).wait()
    stg[slot,0]=dot(a1T[:,:T],dq_in[0],1,0).astype(BF)
    stg[slot,1]=dot(a1T[...],dk_in[0],1,0).astype(BF)
    stg[slot,2]=dot(a1T[...],dv_in[0],1,0).astype(BF)
    stg[slot,3]=dot(dresT[...],o_in[0],1,0).astype(BF)
    for r in range(R):
        dst=(d0,d1)[r%2]
        pltpu.make_async_copy(stg.at[slot,:,pl.ds(pl.multiple_of(perm[R+r]*SLAB,SLAB),SLAB),:], dst.at[r//2, slots[s]], osem.at[slot]).start()
    pltpu.make_async_copy(W.at[slot],W.at[slot],sem.at[slot]).wait()
    c=dot(dk_in[0],W[slot,1],1,1)+dot(dv_in[0],W[slot,2],1,1)
    cq=dot(dq_in[0],W[slot,0],1,1)
    @pl.when(s==0)
    def _():
        acc[...]=c
        acc[:T,:]=acc[:T,:]+cq
    @pl.when(s>0)
    def _():
        acc[...]=acc[...]+c
        acc[:T,:]=acc[:T,:]+cq
    @pl.when(s==S-1)
    def _():
        gg_out[...]=jnp.sum(acc[...]*xhat[...].astype(F32),axis=0,keepdims=True)
        da_own[...]=acc[:T,:]
        da_far[...]=acc[T:,:].astype(BF)
        for sl in range(min(S,2)):
            pltpu.make_async_copy(stg.at[sl],stg.at[sl],osem.at[sl]).wait()

def grad_attn(perm2,slots,a1T,dresT,xhat,o,dq,dk,dv,pieces):
    wps,metas,S,SLAB,C=pieces
    R=perm2.shape[0]//2
    D,T=dresT.shape; KV=dk.shape[1]
    A=pl.BlockSpec(memory_space=ANY)
    ib=lambda rows:pl.BlockSpec((1,rows,C),lambda s,p,q:(s,0,0))
    gs=pltpu.PrefetchScalarGridSpec(num_scalar_prefetch=2,grid=(S,),
        in_specs=[full((D,KV)),full((D,T)),full((KV,D)),ib(T),ib(T),ib(KV),ib(KV)]+[A]*len(wps),
        out_specs=[full((T,D)),full((KV-T,D)),full((1,D)),A,A],
        scratch_shapes=[pltpu.VMEM((2,3,D,C),BF),pltpu.VMEM((2,4,D,C),BF),pltpu.VMEM((KV,D),F32),pltpu.SemaphoreType.DMA((2,)),pltpu.SemaphoreType.DMA((2,))])
    sd=jax.ShapeDtypeStruct
    piece=sd((R//2,S,4,SLAB,C),BF)
    return pl.pallas_call(functools.partial(grad_attn_kernel,T=T,KV=KV,C=C,R=R,metas=metas,S=S,SLAB=SLAB),grid_spec=gs,
        out_shape=[sd((T,D),F32),sd((KV-T,D),BF),sd((1,D),F32),piece,piece],
        cost_estimate=pl.CostEstimate(flops=1,transcendentals=0,bytes_accessed=1),name="attn_grad")(perm2,slots,a1T,dresT,xhat,o,dq,dk,dv,*wps)

def split3(x):
    hi=x.astype(BF)
    return hi,(x-hi.astype(F32)).astype(BF)

def dot3(a,b,ca,cb):
    ah,al=a; bh,bl=b
    return dot(ah,bh,ca,cb)+(dot(ah,bl,ca,cb)+dot(al,bh,ca,cb))

def soap_kernel(sc, g_in, first, second, left, right, *rest, turned):
    f_out, s_out, u_out, n_out = rest[-4:]
    step,b1,b2=sc[0],sc[1],sc[2]
    ql=split3(left[0]); qr=split3(right[0])
    if turned:
        x=dot3(split3(g_in[0]),ql,1,0)
        r=dot3(split3(x),qr,0,0).T
    else:
        x=dot3(ql,split3(g_in[0]),0,0)
        r=dot3(split3(x),qr,1,0)
    fn=b1*first[0]+(1.0-b1)*r
    sn=b2*second[0]+(1.0-b2)*r*r
    f_out[0]=fn; s_out[0]=sn
    n=fn/(jnp.sqrt(sn)+ADAM_EPS)
    if turned:
        t=dot3(split3(dot3(qr,split3(n),1,0)),ql,1,1)
    else:
        t=dot3(split3(dot3(ql,split3(n),1,0)),qr,1,1)
    size=n.shape[0]*n.shape[1]
    fac=jnp.sqrt(jnp.sum(n*n,keepdims=True)*(1.0/size))*lax.rsqrt(jnp.sum(t*t,keepdims=True)*(1.0/size)+SCALE_EPS)
    u_out[0]=(-step*fac)*t
    n_out[0]=jnp.broadcast_to(fac,(8,128))

def soap(scalars,g,first,second,left,right,turned,K0=0,N=None,carry=()):
    K=first.shape[0]
    N=K if N is None else N
    b=lambda x:pl.BlockSpec((1,)+x.shape[1:],lambda k,s:(k+K0,0,0))
    sd=jax.ShapeDtypeStruct
    o=sd(first.shape,F32)
    outs=[o,o,o,sd((K,8,128),F32)]
    gs=pltpu.PrefetchScalarGridSpec(num_scalar_prefetch=1,grid=(N,),
        in_specs=[b(x) for x in (g,first,second,left,right)]+[pl.BlockSpec(memory_space=ANY)]*len(carry),out_specs=[b(x) for x in outs])
    return pl.pallas_call(functools.partial(soap_kernel,turned=turned),grid_spec=gs,out_shape=outs,
        input_output_aliases={6+i:i for i in range(len(carry))},
        cost_estimate=pl.CostEstimate(flops=1,transcendentals=0,bytes_accessed=1),
        name="soap_"+("mlp" if turned else "attn"))(scalars,g,first,second,left,right,*carry)


def ring_order(count):
    return list(range(0, count, 2)) + list(range(1, count, 2))[::-1]


def swap_dp(value, bit, owners):
    return lax.ppermute(value, "dp", [(i, i ^ bit) for i in range(owners)])


def to_ring_pred(value, shards):
    ring = ring_order(shards)
    return lax.ppermute(
        value, "tensor", [(ring[p], ring[(p - 1) % shards]) for p in range(shards)]
    )


def to_ring_succ(value, shards):
    ring = ring_order(shards)
    return lax.ppermute(
        value, "tensor", [(ring[p], ring[(p + 1) % shards]) for p in range(shards)]
    )


def along_line(value, steps, shards):
    ring = ring_order(shards)
    return lax.ppermute(
        value, "tensor", [(ring[p], ring[(p + steps) % shards]) for p in range(shards)]
    )


def add_low(one, two):
    return (one.astype(F32) + two.astype(F32)).astype(BF)


def halve(pieces, bits, owners):
    for bit in bits:
        live = sorted(bits[bits.index(bit):], reverse=True)
        axis = live.index(bit)
        send = lax.index_in_dim(pieces, 1, axis, keepdims=False)
        keep = lax.index_in_dim(pieces, 0, axis, keepdims=False)
        pieces = add_low(keep, swap_dp(send, bit, owners))
    return pieces


def reduce_pieces(even, odd, cut, owners, shards):
    mine = add_low(even, swap_dp(odd, 1, owners))
    bits = [1 << b for b in range(1, owners.bit_length() - 1)]
    mine = mine.reshape((2,) * len(bits) + mine.shape[1:])
    low = halve(mine[..., :cut, :], bits[::-1], owners)
    high = halve(mine[..., cut:, :], bits, owners)
    both = jnp.concatenate([low, high], axis=-2)
    moving = both[shards - 1]
    for left in range(shards - 2, -1, -1):
        moving = to_ring_pred(moving, shards)
        moving = moving.astype(F32) + both[left].astype(F32)
        if left:
            moving = moving.astype(BF)
    return moving


def all_sum(value, owners, shards):
    for axis, count in (("dp", owners), ("tensor", shards)):
        step = 1
        while step < count:
            value = value + lax.ppermute(value, axis, [(i, i ^ step) for i in range(count)])
            step *= 2
    return value


def after(value, *earlier):
    return lax.optimization_barrier((value,) + earlier)[0]


def add_all(*values):
    total = values[0].astype(F32)
    for value in values[1:]:
        total = total + value.astype(F32)
    return total


def gather_stack(stacked, owners):
    half = stacked.shape[0] // 2
    by_x, by_y = swap_dp(stacked, 2, owners), swap_dp(stacked, 4, owners)
    return by_x, by_y, swap_dp(by_x[:half], 4, owners), swap_dp(by_y[half:], 2, owners)


def to_core(arrays, owners):
    return [swap_dp(a, 1, owners) for a in arrays]


def with_partner(arrays, metas, owners):
    return arrays + [swap_dp(a, 1, owners) for a in arrays], metas + tuple((m[0] + 1,) + m[1:] for m in metas)


def cross_sends(even, core, half):
    low = add_all(even[3, :half], core[3, :half]).astype(BF)
    high = add_all(even[3, half:], core[3, half:]).astype(BF)
    return low, high


def side_sends(even, core, from_y, from_x, half):
    to_x = jnp.concatenate(
        [add_all(even[1, :half], core[1, :half], from_y), add_all(even[1, half:], core[1, half:])]
    ).astype(BF)
    to_y = jnp.concatenate(
        [add_all(even[2, :half], core[2, :half]), add_all(even[2, half:], core[2, half:], from_x)]
    ).astype(BF)
    return to_x, to_y


def own_part(even, core, from_x, from_y, slot):
    return add_all(even[0, slot], core[0, slot], from_x[slot], from_y[slot])


def ring_sum(even, core, from_x, from_y, shards):
    moving = None
    for slot in list(range(1, shards)) + [0]:
        part = own_part(even, core, from_x, from_y, slot)
        if moving is not None:
            part = part + to_ring_succ(moving, shards).astype(F32)
        moving = part.astype(BF)
    return part


def per_device(
    hidden_in, out_grad, attn_weight, mlp_weight, norm_gain,
    attn_first, attn_second, attn_left, attn_right,
    mlp_first, mlp_second, mlp_left, mlp_right,
    gain_first, gain_second, owner_rows, segment_ids, positions, valid,
    step, learn_rate, beta_first, beta_second,
):
    owners = lax.axis_size("dp")
    shards = lax.axis_size("tensor")
    dp_index = lax.axis_index("dp")
    place = lax.axis_index("tensor")
    rows, width = hidden_in.shape
    slab = attn_weight.shape[1]
    hid_cols = mlp_weight.shape[2]
    span = SEQ_LEN // rows
    within = place % span
    base = place - within
    half = shards // 2
    gain_rows = norm_gain.astype(F32)

    def from_peer(value, ahead):
        pairs = [(g + (w + ahead) % span, g + w) for g in range(0, shards, span) for w in range(span)]
        return lax.ppermute(value, "tensor", pairs)

    def sequence_rows(column):
        return jnp.concatenate(
            [lax.dynamic_slice_in_dim(column, (base + (within + d) % span) * rows, rows, 0) for d in range(span)]
        )

    joined = 128 // slab if slab < 128 else 1
    fast = owners == 8 and joined == 1 and shards == 4 and span == 2
    both = ("dp", "tensor")
    mlp_turned = jnp.swapaxes(mlp_weight, 1, 2)
    if not fast:
        attn_all = lax.all_gather(attn_weight, both, axis=0, tiled=False).reshape((owners, shards) + attn_weight.shape)
        mlp_all = lax.all_gather(mlp_turned, both, axis=0, tiled=False).reshape((owners, shards) + mlp_turned.shape)

    slot_ids = jnp.arange(owners, dtype=jnp.int32)
    rel_owner = jnp.sum(
        jnp.where((slot_ids[:, None] ^ dp_index) == slot_ids[None, :], owner_rows[None, :], 0), axis=1
    )
    ring = ring_order(shards)
    ring_place = jnp.array([ring.index(z) for z in range(shards)], jnp.int32)
    my_place = jnp.sum(jnp.where(jnp.arange(shards) == place, ring_place, 0))
    slots = (my_place - ring_place) % shards
    attn_perm = jnp.concatenate([rel_owner if fast else owner_rows, rel_owner]).astype(jnp.int32)
    if fast:
        slots = jnp.arange(shards, dtype=jnp.int32)
    if joined == 1:
        mlp_perm = attn_perm
    else:
        inverse = jnp.sum(jnp.where(owner_rows[None, :] == slot_ids[:, None], slot_ids[None, :], 0), axis=1)
        mlp_all = jnp.take(mlp_all, inverse, axis=0).reshape((owners // joined, joined) + mlp_all.shape[1:])
        mlp_all = jnp.moveaxis(mlp_all, 1, 4)
        mlp_all = mlp_all.reshape(mlp_all.shape[:4] + (joined * slab,))
        blocks = jnp.arange(owners // joined, dtype=jnp.int32)
        mlp_perm = jnp.concatenate([blocks, blocks])

    seg = sequence_rows(segment_ids)
    keep_seq = sequence_rows(valid)
    pos = sequence_rows(positions)
    half_dim = HEAD_DIM // 2
    frequency = jnp.exp(jnp.arange(half_dim, dtype=F32) * (-2.0 * math.log(ROPE_BASE) / HEAD_DIM))
    angles = pos.astype(F32)[:, None] * frequency[None, :]
    cos_half, sin_half = jnp.cos(angles), jnp.sin(angles)
    cos_table = jnp.concatenate([cos_half] * 4, axis=1)
    sin_table = jnp.concatenate([-sin_half, sin_half] * 2, axis=1)
    key_seg = jnp.where(keep_seq > 0, seg, -1)[:, None]
    query_seg = seg[None, :rows]
    keep_own = keep_seq[:rows].astype(F32)[:, None]

    def normalize_first(far_rows):
        hidden_seq = jnp.concatenate([hidden_in] + far_rows).astype(F32)
        centred = hidden_seq - jnp.mean(hidden_seq, axis=-1, keepdims=True)
        rstd = lax.rsqrt(jnp.mean(centred * centred, axis=-1, keepdims=True) + NORM_EPS)
        xhat = centred * rstd
        first_norm = (xhat * gain_rows[0]).astype(BF)
        return first_norm, first_norm.T, xhat.astype(BF), xhat[:rows], rstd[:rows]

    back_args = (cos_table, sin_table, key_seg, query_seg)
    if fast:
        line = [attn_weight] + [None] * 3
        for t in (1, 3, 2):
            line[t] = along_line(attn_weight, t, shards)
        mlp_line = [mlp_turned] + [None] * 3
        mlp_x, mlp_y, mlp_z = [None] * 4, [None] * 4, [None] * 4
        mlp_x[0], mlp_y[0] = swap_dp(mlp_turned, 2, owners), swap_dp(mlp_turned, 4, owners)
        line, mlp_x[0], mlp_y[0] = lax.optimization_barrier((line, mlp_x[0], mlp_y[0]))
        far_rows = from_peer(after(hidden_in, line[2]), 1)
        stacked = jnp.stack(line)
        by_x, by_y = swap_dp(stacked, 2, owners), swap_dp(stacked, 4, owners)
        by_x, by_y, far_rows = lax.optimization_barrier((by_x, by_y, far_rows))
        across = [swap_dp(by_x[:half], 4, owners), swap_dp(by_y[half:], 2, owners)]
        turn = after(mlp_turned, far_rows)
        for t in (1, 3, 2):
            mlp_line[t] = along_line(turn, t, shards)
        normal = normalize_first([far_rows])
        across, normal, mlp_line[1] = lax.optimization_barrier((across, normal, mlp_line[1]))
        first_norm, first_turned, xhat_low, own_hat, own_rstd = normal
        arrays = [stacked, by_x, by_y, *across]
        metas = tuple((r, f, n, shards) for r, f, n in ((0, 0, shards), (2, 0, shards), (4, 0, shards), (6, 0, half), (6, half, half)))
        attn_pieces = (*with_partner(arrays, metas, owners), shards, slab, attn_weight.shape[2])
        mlp_x[1], mlp_y[1] = swap_dp(mlp_line[1], 2, owners), swap_dp(mlp_line[1], 4, owners)
        mlp_z[0] = swap_dp(after(mlp_x[0], mlp_line[1]), 4, owners)
    else:
        far_rows = [from_peer(hidden_in, d) for d in range(1, span)]
        attn_pieces = ([attn_all], (None,), shards, slab, attn_weight.shape[2])
        first_norm, first_turned, xhat_low, own_hat, own_rstd = normalize_first(far_rows)
    fwd_args = (attn_perm, first_norm, hidden_in, gain_rows[1:2], cos_table, sin_table, key_seg, query_seg, keep_own)
    if fast:
        carry = fwd_attn(*fwd_args, attn_pieces, S0=0, N=half)
        set_0 = [mlp_line[0], mlp_x[0], mlp_y[0], mlp_z[0]]
        set_1 = [mlp_line[1], mlp_x[1], mlp_y[1]]
        set_0, set_1, mlp_line[3], carry = lax.optimization_barrier((set_0, set_1, mlp_line[3], tuple(carry)))
        mlp_z[1] = swap_dp(set_1[2], 2, owners)
        mlp_x[3], mlp_y[3] = swap_dp(mlp_line[3], 2, owners), swap_dp(mlp_line[3], 4, owners)
        core_0, core_1 = to_core(set_0, owners), to_core(set_1, owners)
        out = fwd_attn(*fwd_args, attn_pieces, S0=half, N=half, carry=carry)
        set_3 = [mlp_line[3], mlp_x[3], mlp_y[3]]
        core_0, core_1, far_z, set_3, mlp_line[2], out = lax.optimization_barrier((core_0, core_1, mlp_z[1], set_3, mlp_line[2], tuple(out)))
        queries, keys, values, attended, log_sums, resid, second_norm, stat_a = out
        set_1, core_1 = set_1 + [far_z], core_1 + to_core([far_z], owners)
        core_1, second_norm, set_3, mlp_line[2] = lax.optimization_barrier((core_1, second_norm, set_3, mlp_line[2]))

        def mlp_pieces(*slots_of):
            arrays, metas = [], []
            for slot, got in slots_of:
                arrays += [a[None] for a in got]
                metas += [(r, slot, 1, shards) for r in (0, 2, 4, 6, 1, 3, 5, 7)]
            return arrays, tuple(metas), shards, slab, hid_cols

        mlp_z[3] = swap_dp(set_3[1], 4, owners)
        set_2 = [mlp_line[2], swap_dp(mlp_line[2], 2, owners), swap_dp(mlp_line[2], 4, owners)]
        core_3 = to_core(set_3, owners)
        mlp_args = (mlp_perm, slots, second_norm, out_grad, resid, gain_rows[1:2], keep_own)
        out = mlp(*mlp_args, mlp_pieces((0, set_0 + core_0), (1, set_1 + core_1)), S0=0, N=half)
        far_z, core_3, set_2, out = lax.optimization_barrier((mlp_z[3], core_3, set_2, tuple(out)))
        set_3, core_3 = set_3 + [far_z], core_3 + to_core([far_z], owners)
        far_z = swap_dp(set_2[2], 2, owners)
        core_2 = to_core(set_2, owners)
        set_2, core_2 = set_2 + [far_z], core_2 + to_core([far_z], owners)
        *carry, even_a, odd_a = out
        core_a = swap_dp(odd_a, 1, owners)
        low, high = cross_sends(even_a, core_a, 1)
        low, high, core_2, core_3, carry = lax.optimization_barrier((low, high, core_2, core_3, carry))
        from_y, from_x = swap_dp(low, 4, owners), swap_dp(high, 2, owners)
        out = mlp(*mlp_args, mlp_pieces((2, set_2 + core_2), (3, set_3 + core_3)), S0=half, N=half, carry=carry)
        from_y, from_x, *out = lax.optimization_barrier((from_y, from_x, *out))
        output, dresid, dres_low, dres_turned, gain_two, stat_m, even_b, odd_b = out
        core_b = swap_dp(odd_b, 1, owners)
        to_x, to_y = side_sends(even_a, core_a, from_y, from_x, 1)
        to_x, to_y, dres_low = lax.optimization_barrier((to_x, to_y, dres_low))
        back_x, back_y = swap_dp(to_x, 2, owners), swap_dp(to_y, 4, owners)
        fwd_kept = (queries, keys, values, log_sums, attn_pieces)
        grads = bwd_attn(attn_perm, dres_low, *back_args, *fwd_kept, S0=0, N=half)
        back_x, back_y, core_b, *grads = lax.optimization_barrier((back_x, back_y, core_b, *grads))
        low, high = cross_sends(even_b, core_b, 1)
        ring_1 = own_part(even_a, core_a, back_x, back_y, 1).astype(BF)
        low, high, ring_1, dres_low = lax.optimization_barrier((low, high, ring_1, dres_low))
        from_y, from_x = swap_dp(low, 4, owners), swap_dp(high, 2, owners)
        ring_1 = to_ring_succ(ring_1, shards)
        grads = bwd_attn(attn_perm, dres_low, *back_args, *fwd_kept, S0=half, N=half, carry=tuple(grads))
        from_y, from_x, ring_1, *grads = lax.optimization_barrier((from_y, from_x, ring_1, *grads))
        to_x, to_y = side_sends(even_b, core_b, from_y, from_x, 1)
        to_x, to_y, dres_turned = lax.optimization_barrier((to_x, to_y, dres_turned))
        from_x, from_y = swap_dp(to_x, 2, owners), swap_dp(to_y, 4, owners)
        out = grad_attn(attn_perm, slots, first_turned, dres_turned, xhat_low, attended, *grads, attn_pieces)
        from_x, from_y, *out = lax.optimization_barrier((from_x, from_y, *out))
        da_own, da_far, gain_one, attn_even, attn_odd = out
    else:
        queries, keys, values, attended, log_sums, resid, second_norm, stat_a = fwd_attn(*fwd_args, attn_pieces)
        output, dresid, dres_low, dres_turned, gain_two, stat_m, mlp_even, mlp_odd = mlp(
            mlp_perm, slots, second_norm, out_grad, resid, gain_rows[1:2], keep_own,
            ([mlp_all], (None,), shards, mlp_all.shape[-1], hid_cols),
        )
        if joined > 1:
            merged = jnp.stack([mlp_even, mlp_odd], axis=1).reshape((owners // joined,) + mlp_even.shape[1:])
            merged = merged.reshape(merged.shape[:-1] + (joined, slab))
            merged = jnp.moveaxis(merged, -2, 1).reshape((owners,) + mlp_even.shape[1:-1] + (slab,))
            merged = jnp.take(merged, rel_owner, axis=0)
            mlp_even, mlp_odd = merged[0::2], merged[1::2]
        mlp_sum = reduce_pieces(mlp_even, mlp_odd, -(-hid_cols // 32) * 16, owners, shards)
        grads = bwd_attn(attn_perm, dres_low, *back_args, queries, keys, values, log_sums, attn_pieces)
        da_own, da_far, gain_one, attn_even, attn_odd = grad_attn(
            attn_perm, slots, first_turned, dres_turned, xhat_low, attended, *grads, attn_pieces
        )
    def send_back(da_far):
        got = []
        for d in range(1, span):
            pairs = [(g + w, g + (w + d) % span) for g in range(0, shards, span) for w in range(span)]
            got.append(lax.ppermute(da_far[(d - 1) * rows : d * rows], "tensor", pairs))
        return got

    def swap_line(value, bit):
        return lax.ppermute(value, "tensor", [(i, i ^ bit) for i in range(shards)])

    def finish_input(da_back):
        first_grad = add_all(da_own, *da_back)
        scaled = first_grad * gain_rows[0]
        input_part = own_rstd * (
            scaled
            - jnp.mean(scaled, axis=-1, keepdims=True)
            - own_hat * jnp.mean(scaled * own_hat, axis=-1, keepdims=True)
        )
        return (dresid + input_part).astype(BF)

    step_count = step.astype(F32)
    step_size = (
        learn_rate
        * jnp.sqrt(1.0 - jnp.power(beta_second, step_count))
        / (1.0 - jnp.power(beta_first, step_count))
    )
    scalars = jnp.stack([step_size, beta_first, beta_second])

    def flip(value):
        return jnp.swapaxes(value, 1, 2)

    def soap_mlp(total, *part):
        return soap(scalars, total, flip(mlp_first), flip(mlp_second), mlp_left, mlp_right, True, *part)

    sums = jnp.concatenate([jnp.sum(stat_a, axis=1), jnp.sum(stat_m, axis=1), jnp.sum(keep_own)[None]])
    small = jnp.concatenate([gain_one, gain_two, jnp.pad(sums, (0, width - 5))[None]], axis=0)
    if fast:
        attn_core = swap_dp(attn_odd, 1, owners)
        da_back = send_back(da_far)
        small = small + swap_dp(small, 1, owners)
        small, attn_core = lax.optimization_barrier((small, attn_core))
        ring_2 = (own_part(even_b, core_b, from_x, from_y, 0) + ring_1.astype(F32)).astype(BF)
        ring_2 = to_ring_succ(ring_2, shards)
        low, high = cross_sends(attn_even, attn_core, half)
        cross_y, cross_x = swap_dp(low, 4, owners), swap_dp(high, 2, owners)
        small = (small + swap_dp(small, 2, owners)) + (swap_dp(small, 4, owners) + swap_dp(small, 6, owners))
        small, cross_x, cross_y = lax.optimization_barrier((small, cross_x, cross_y))
        to_x, to_y = side_sends(attn_even, attn_core, cross_y, cross_x, half)
        to_x, to_y, ring_2, da_back, small = lax.optimization_barrier((to_x, to_y, ring_2, da_back, small))
        attn_x, attn_y = swap_dp(to_x, 2, owners), swap_dp(to_y, 4, owners)
        ring_3 = (own_part(even_b, core_b, from_x, from_y, 1) + ring_2.astype(F32)).astype(BF)
        ring_3 = to_ring_succ(ring_3, shards)
        small = (small + swap_line(small, 1)) + (swap_line(small, 2) + swap_line(small, 3))
        input_grad = finish_input(da_back)
        small, attn_x, attn_y, ring_3, input_grad = lax.optimization_barrier((small, attn_x, attn_y, ring_3, input_grad))
        moving = own_part(attn_even, attn_core, attn_x, attn_y, 1).astype(BF)
        mlp_sum = own_part(even_a, core_a, back_x, back_y, 0) + ring_3.astype(F32)
        mlp_new = ()
        for slot in range(1, shards):
            moving, mlp_sum = lax.optimization_barrier((moving, mlp_sum))
            moving = to_ring_succ(moving, shards)
            mlp_new = soap_mlp(mlp_sum, slot - 1, 1, mlp_new)
            moving, mlp_new = lax.optimization_barrier((moving, tuple(mlp_new)))
            moving = moving.astype(F32) + own_part(attn_even, attn_core, attn_x, attn_y, (slot + 1) % shards)
            if slot + 1 < shards:
                moving = moving.astype(BF)
        attn_sum = moving
    else:
        attn_sum = reduce_pieces(attn_even, attn_odd, slab // 2, owners, shards)
        small = all_sum(small, owners, shards)
        mlp_new = soap_mlp(mlp_sum)
        input_grad = finish_input(send_back(da_far))
    gain_grad = small[:2]
    stat_sums = small[2]

    attn_grad = attn_sum
    attn_first_new, attn_second_new, attn_update, attn_scale = soap(
        scalars, attn_sum, attn_first, attn_second, attn_left, attn_right, False
    )
    mlp_grad, mlp_first_new, mlp_second_new, mlp_update = (flip(v) for v in (mlp_sum, *mlp_new[:3]))
    mlp_scale = mlp_new[3]
    gain_first_new = beta_first * gain_first + (1.0 - beta_first) * gain_grad
    gain_second_new = beta_second * gain_second + (1.0 - beta_second) * gain_grad * gain_grad
    gain_update = -step_size * gain_first_new / (jnp.sqrt(gain_second_new) + ADAM_EPS)
    root_means = jnp.sqrt(stat_sums[:4] / (stat_sums[4] * width))
    norm_scale = jnp.concatenate([attn_scale[:, :1, :1], mlp_scale[:, :1, :1]], axis=0)
    return (
        output, input_grad, attn_grad, mlp_grad, gain_grad,
        attn_first_new, attn_second_new, mlp_first_new, mlp_second_new,
        gain_first_new, gain_second_new, attn_update, mlp_update, gain_update,
        norm_scale, root_means,
    )


def solution(mesh):
    rows = P(("dp", "tensor"), None)
    block = P(None, "dp", "tensor")
    return jax.shard_map(
        per_device,
        mesh=mesh,
        in_specs=(rows, rows, block, block, P()) + (block,) * 8 + (P(),) * 3 + (P("dp"),) * 3 + (P(),) * 4,
        out_specs=(rows, rows, block, block, P(), block, block, block, block, P(), P(), block, block, P(), block, P()),
        check_vma=False,
    )
```

time: 530 us -> 442 us (0.83)
  waiting for transfers between devices: 265 us -> 114 us
  starting transfers between devices: 23.1 us -> 64.6 us
  Pallas kernels: 139 us -> 176 us
  matrix products: 23.1 us -> 0 us
  between operations: 18.5 us -> 5.23 us
  other arithmetic: 45.4 us -> 56.3 us
  local copies, waits for them, and re-layouts: 10.2 us -> 19.9 us
    all_gather x2 -> x0, waiting for transfers between devices: 127 us -> none  [the longest x1 83.9 us: per_device(): lax.all_gather(mlp_turned, both, axis=0, tiled=False)]
    pallas_call x6 -> x10, Pallas kernels: 117 us -> 153 us  [the longest x2 50.5 us: mlp(): pl.pallas_call(functools.partial(mlp_kernel, T=T, D=D, HC=HC, R=R, metas=...]
    ppermute x10 -> x56, starting transfers between devices: 9.55 us -> 42.5 us  [swap_dp(): return lax.ppermute(value, 'dp', [(i, i ^ bit) for i in range(owners)])]
    dot_general x8 -> x0, matrix products: 23.1 us -> none  [the longest x2 12.7 us: soap_block(): rotated = jnp.einsum('kbc,kce->kbe', half_turn, right, precision=PRECISE)]
    ppermute x1, waiting for transfers between devices: 14.6 us -> 0.57 us  [from_peer(): return lax.ppermute(value, 'tensor', pairs)]
    add x6 -> x8, other arithmetic: 1.48 us -> 15 us  [the longest x3 9.83 us: add_all(): total = total + value.astype(F32)]
    ppermute x12 -> x16, starting transfers between devices: 10.4 us -> 22 us  [the longest x6 8.47 us: along_line(): lax.ppermute(value, 'tensor', [(ring[p], ring[(p + steps) % shards]) for...]
    convert_element_type x15 -> x7, other arithmetic: 19.7 us -> 10.7 us  [the longest x2 2.39 us: per_device(): moving = moving.astype(BF)]
  transfers between devices with their start and end apart: 25 -> 73, of which waited for: 19 -> 22; matrix products, arithmetic and copies ran while one was open for 10% -> 11% of each run, Pallas kernels for 14% -> 39%
where the time goes in v2:
time: 442 us; the launch traced here: 436 us
  Pallas kernels  176 us (40%)
  waiting for transfers between devices  114 us (26%)
  starting transfers between devices  64.6 us (15%)
  other arithmetic  56.3 us (13%)
  local copies, waits for them, and re-layouts  19.9 us (5%)
  between operations  5.23 us (1%)
    ppermute x56, waiting for transfers between devices, swap_dp(): return lax.ppermute(value, 'dp', [(i, i ^ bit) for i in range(owners)])  62.3 us
    pallas_call x2, Pallas kernels, mlp(): pl.pallas_call(functools.partial(mlp_kernel, T=T, D=D, HC=HC, R=R, metas=...  50.5 us
    ppermute x56, starting transfers between devices, swap_dp(): return lax.ppermute(value, 'dp', [(i, i ^ bit) for i in range(owners)])  42.5 us
    pallas_call x2, Pallas kernels, bwd_attn(): pl.pallas_call(functools.partial(bwd_attn_kernel, T=T, KV=KV, C=C, metas=...  38.1 us
    pallas_call x2, Pallas kernels, fwd_attn(): pl.pallas_call(functools.partial(fwd_attn_kernel, T=T, KV=KV, C=C, metas=...  36.5 us
    ppermute x6, waiting for transfers between devices, along_line(): lax.ppermute(value, 'tensor', [(ring[p], ring[(p + steps) % shards]) for...  34.7 us
    pallas_call x4, Pallas kernels, soap(): pl.pallas_call(functools.partial(soap_kernel, turned=turned), grid_spec=g...  28.3 us
    pallas_call x1, Pallas kernels, grad_attn(): pl.pallas_call(functools.partial(grad_attn_kernel, T=T, KV=KV, C=C, R=R,...  22.8 us
  transfers between devices with their start and end apart: 73, of which 22 were waited for; matrix products, arithmetic and copies ran while one was open for 11% of the time, Pallas kernels for 39%

profile of v2, /device:TPU:0, one launch (start us, length us, event | category | flops | bytes accessed | tf_op | source)
XLA Modules:
  0.0 435.9 jit_solution(10670752036010875361)
XLA Ops:
  10.8 5.7 %collective-permute-done.1 = bf16[4,128,256]{2,1,0:T(8,128)(2,1)S(1)} collective-permute-done((bf16[4,128,256]{2,1,0:T(8,128)(2,1)}, bf16[4,128,256]{2,1,0:T(8,128)(2,1)S(1)}, u32[]{:S(2)}, u32[]{:S(2)}) %collective-permute-start.1) | collective-permute-done | bytes 262176 | tf_op jit(solution)/shard_map/ppermute | solution.py:420
  16.5 4.9 %collective-permute-done = bf16[4,128,256]{2,1,0:T(8,128)(2,1)S(1)} collective-permute-done((bf16[4,128,256]{2,1,0:T(8,128)(2,1)}, bf16[4,128,256]{2,1,0:T(8,128)(2,1)S(1)}, u32[]{:S(2)}, u32[]{:S(2)}) %collective-permute-start) | collective-permute-done | bytes 262176 | tf_op jit(solution)/shard_map/ppermute | solution.py:420
  21.5 9.3 %collective-permute-done.2 = bf16[4,128,256]{2,1,0:T(8,128)(2,1)S(1)} collective-permute-done((bf16[4,128,256]{2,1,0:T(8,128)(2,1)}, bf16[4,128,256]{2,1,0:T(8,128)(2,1)S(1)}, u32[]{:S(2)}, u32[]{:S(2)}) %collective-permute-start.2) | collective-permute-done | bytes 262176 | tf_op jit(solution)/shard_map/ppermute | solution.py:420
  39.1 17.9 %collective-permute-done.6.rest_2_ = bf16[4,4,128,256]{3,2,1,0:T(8,128)(2,1)S(1)} collective-permute-done((bf16[4,4,128,256]{3,2,1,0:T(8,128)(2,1)S(1)}, bf16[4,4,128,256]{3,2,1,0:T(8,128)(2,1)S(1)}, u32[]{:S(2)}, u32[]{:S(2)}) %collective-permute-start.6) | collective-permute-done | bytes 1048608 | tf_op jit(solution)/shard_map/ppermute | solution.py:401
  64.4 4.7 %collective-permute-done.10 = bf16[3,656,128]{2,1,0:T(8,128)(2,1)S(1)} collective-permute-done((bf16[3,656,128]{2,1,0:T(8,128)(2,1)}, bf16[3,656,128]{2,1,0:T(8,128)(2,1)S(1)}, u32[]{:S(2)}, u32[]{:S(2)}) %collective-permute-start.10) | collective-permute-done | bytes 503840 | tf_op jit(solution)/shard_map/ppermute | solution.py:420
  75.4 4.4 %collective-permute-done.8.rest_3_ = bf16[2,4,128,256]{3,2,1,0:T(8,128)(2,1)} collective-permute-done((bf16[2,4,128,256]{3,2,1,0:T(8,128)(2,1)S(1)}, bf16[2,4,128,256]{3,2,1,0:T(8,128)(2,1)}, u32[]{:S(2)}, u32[]{:S(2)}) %collective-permute-start.8) | collective-permute-done | bytes 524320 | tf_op jit(solution)/shard_map/ppermute | solution.py:401
  94.2 17.0 %attn_fwd.2 = (bf16[4,512,256]{2,1,0:T(8,128)(2,1)}, bf16[4,1024,256]{2,1,0:T(8,128)(2,1)}, bf16[4,1024,256]{2,1,0:T(8,128)(2,1)}, bf16[4,512,256]{2,1,0:T(8,128...) custom-call(s32[16]{0:T(128)} %pad_add_fusion.1.perm, bf16[1024,1024]{1,0:T(8,128)(2,1)} %get-tuple-element.243.a1, ...), custom_call_target="tpu_custom_call" | custom-call | flops 1 | bytes 1 | tf_op jit(solution)/shard_map/attn_fwd/pallas_call | solution.py:134
  111.2 10.1 %collective-permute-done.14 = bf16[3,656,128]{2,1,0:T(8,128)(2,1)S(1)} collective-permute-done((bf16[3,656,128]{2,1,0:T(8,128)(2,1)}, bf16[3,656,128]{2,1,0:T(8,128)(2,1)S(1)}, u32[]{:S(2)}, u32[]{:S(2)}) %collective-permute-start.14) | collective-permute-done | bytes 503840 | tf_op jit(solution)/shard_map/ppermute | solution.py:420
  129.5 19.5 %attn_fwd.3 = (bf16[4,512,256]{2,1,0:T(8,128)(2,1)}, bf16[4,1024,256]{2,1,0:T(8,128)(2,1)}, bf16[4,1024,256]{2,1,0:T(8,128)(2,1)}, bf16[4,512,256]{2,1,0:T(8,128...) custom-call(s32[16]{0:T(128)} %pad_add_fusion.1.perm, ...), custom_call_target="tpu_custom_call", output_to_operand_aliasing={{0}: (20, {}), {1}: (21, {}), {2}: (22, {}), {3}: (23, {}),... | custom-call | flops 1 | bytes 1 | tf_op jit(solution)/shard_map/attn_fwd/pallas_call | solution.py:134
  154.7 24.2 %mlp_both.2 = (f32[512,1024]{1,0:T(8,128)}, f32[512,1024]{1,0:T(8,128)}, bf16[4,2,3,656,128]{4,3,2,1,0:T(8,128)(2,1)}, bf16[4,2,3,656,128]{4,3,2,1,0:T(8,128)(2,1)}) custom-call(s32[16]{0:T(128)} %pad_add_fusion.1.perm, s32[4]{0:T(128)} %iota.22.slots, bf16[512,1024]{1,0:T(8,128)(2,1)} %get-tuple-element.287.a2, bf16[512,1024]{1,0:T(8,128)(2,1)} %g.3, ...), custom_call_target="tpu_custom_call" | custom-call | flops 1 | bytes 1 | tf_op jit(solution)/shard_map/mlp_both/pallas_call | solution.py:232
  181.4 11.9 %collective-permute-done.42 = bf16[3,656,128]{2,1,0:T(8,128)(2,1)S(1)} collective-permute-done((bf16[3,656,128]{2,1,0:T(8,128)(2,1)}, bf16[3,656,128]{2,1,0:T(8,128)(2,1)S(1)}, u32[]{:S(2)}, u32[]{:S(2)}) %collective-permute-start.42) | collective-permute-done | bytes 503840 | tf_op jit(solution)/shard_map/ppermute | solution.py:401
  202.8 26.3 %mlp_both.3 = (bf16[512,1024]{1,0:T(8,128)(2,1)}, f32[512,1024]{1,0:T(8,128)}, bf16[512,1024]{1,0:T(8,128)(2,1)}, bf16[1024,512]{1,0:T(8,128)(2,1)}, f32[1,1024]...) custom-call(s32[16]{0:T(128)} %pad_add_fusion.1.perm, ...), custom_call_target="tpu_custom_call" | custom-call | flops 1 | bytes 1 | tf_op jit(solution)/shard_map/mlp_both/pallas_call | solution.py:232
  234.2 19.2 %attn_bwd.2 = (bf16[4,512,256]{2,1,0:T(8,128)(2,1)}, bf16[4,1024,256]{2,1,0:T(8,128)(2,1)}, bf16[4,1024,256]{2,1,0:T(8,128)(2,1)}) custom-call(s32[16]{0:T(128)} %pad_add_fusion.1.perm, bf16[512,1024]{1,0:T(8,128)(2,1)} %get-tuple-element.354.dres, f32[1024,128]{1,0:T(8,128)} %pad_maximum_fusion.8.cos, f32[1024,128]{1,0:T(8,128)} %pad_maximum_fusion.9.sin, ...), custom_call_target="tpu_custom_call" | custom-call | flops 1 | bytes 1 | tf_op jit(solution)/shard_map/attn_bwd/pallas_call | solution.py:290
  253.4 3.9 collective-permute-done.47
  266.2 18.9 %attn_bwd.3 = (bf16[4,512,256]{2,1,0:T(8,128)(2,1)}, bf16[4,1024,256]{2,1,0:T(8,128)(2,1)}, bf16[4,1024,256]{2,1,0:T(8,128)(2,1)}) custom-call(s32[16]{0:T(128)} %pad_add_fusion.1.perm, bf16[512,1024]{1,0:T(8,128)(2,1)} %get-tuple-element.354.dres, f32[1024,128]{1,0:T(8,128)} %pad_maximum_fusion.8.cos, ...), custom_call_target="tpu_custom_call", output_to_operand_aliasing={{0}: (20, {}), {1}: (21, {}), {2}: (22, {})} | custom-call | flops 1 | bytes 1 | tf_op jit(solution)/shard_map/attn_bwd/pallas_call | solution.py:290
  295.5 22.8 %attn_grad.1 = (f32[512,1024]{1,0:T(8,128)}, bf16[512,1024]{1,0:T(8,128)(2,1)}, f32[1,1024]{1,0:T(1,128)}, bf16[4,4,4,128,256]{4,3,2,1,0:T(8,128)(2,1)}, bf16[4,4,4,128,256]{4,3,2,1,0:T(8,128)(2,1)}) custom-call(s32[16]{0:T(128)} %pad_add_fusion.1.perm, s32[4]{0:T(128)} %iota.24.slots, bf16[1024,1024]{1,0:T(8,128)(2,1)} %copy.94.a1T, ...), custom_call_target="tpu_custom_call" | custom-call | flops 1 | bytes 1 | tf_op jit(solution)/shard_map/attn_grad/pallas_call | solution.py:346
  338.7 7.3 %collective-permute-done.61 = bf16[2,4,128,256]{3,2,1,0:T(8,128)(2,1)S(1)} collective-permute-done((bf16[2,4,128,256]{3,2,1,0:T(8,128)(2,1)S(1)}, bf16[2,4,128,256]{3,2,1,0:T(8,128)(2,1)S(1)}, u32[]{:S(2)}, u32[]{:S(2)}) %collective-permute-start.61) | collective-permute-done | bytes 524320 | tf_op jit(solution)/shard_map/ppermute | solution.py:401
  349.1 7.9 %collective-permute-done.62 = bf16[3,656,128]{2,1,0:T(8,128)(2,1)S(1)} collective-permute-done((bf16[3,656,128]{2,1,0:T(8,128)(2,1)S(1)}, bf16[3,656,128]{2,1,0:T(8,128)(2,1)S(1)}, u32[]{:S(2)}, u32[]{:S(2)}) %collective-permute-start.62) | collective-permute-done | bytes 503840 | tf_op jit(solution)/shard_map/ppermute | solution.py:413
  369.5 8.2 %collective-permute-done.69 = bf16[3,656,128]{2,1,0:T(8,128)(2,1)S(1)} collective-permute-done((bf16[3,656,128]{2,1,0:T(8,128)(2,1)S(1)}, bf16[3,656,128]{2,1,0:T(8,128)(2,1)S(1)}, u32[]{:S(2)}, u32[]{:S(2)}) %collective-permute-start.69) | collective-permute-done | bytes 503840 | tf_op jit(solution)/shard_map/ppermute | solution.py:413
  377.7 9.2 %collective-permute-done.67 = bf16[4,4,128,256]{3,2,1,0:T(8,128)(2,1)S(1)} collective-permute-done((bf16[4,4,128,256]{3,2,1,0:T(8,128)(2,1)S(1)}, bf16[4,4,128,256]{3,2,1,0:T(8,128)(2,1)S(1)}, u32[]{:S(2)}, u32[]{:S(2)}) %collective-permute-start.67) | collective-permute-done | bytes 1048608 | tf_op jit(solution)/shard_map/ppermute | solution.py:401
  396.4 7.0 %soap_mlp.3 = (f32[3,656,128]{2,1,0:T(8,128)}, f32[3,656,128]{2,1,0:T(8,128)}, f32[3,656,128]{2,1,0:T(8,128)}, f32[3,8,128]{2,1,0:T(8,128)}) custom-call(f32[3]{0:T(128)} %pad_maximum_fusion.11.sc, f32[3,656,128]{2,1,0:T(8,128)} %fusion.5.g_in, f32[3,656,128]{2,1,0:T(8,128)} %bitcast.177, f32[3,656,128]{2,1,0:T(8,128)} %bitcast.180, f32[3,128,128]{2,1,0:T(8,128)} %left.6, ...), custom_call_target="tpu_custom_call" | custom-call | flops 1 | bytes 1 | tf_op jit(solution)/shard_map/soap_mlp/pallas_call | solution.py:390
  406.3 7.2 %soap_mlp.4 = (f32[3,656,128]{2,1,0:T(8,128)}, f32[3,656,128]{2,1,0:T(8,128)}, f32[3,656,128]{2,1,0:T(8,128)}, f32[3,8,128]{2,1,0:T(8,128)}) custom-call(f32[3]{0:T(128)} %pad_maximum_fusion.11.sc, f32[3,656,128]{2,1,0:T(8,128)} %fusion.5.g_in, f32[3,656,128]{2,1,0:T(8,128)} %bitcast.178, ...), custom_call_target="tpu_custom_call", output_to_operand_aliasing={{0}: (6, {}), {1}: (7, {}), {2}: (8, {}), {3}: (9, {})} | custom-call | flops 1 | bytes 1 | tf_op jit(solution)/shard_map/soap_mlp/pallas_call | solution.py:390
  417.4 7.0 %soap_mlp.5 = (f32[3,656,128]{2,1,0:T(8,128)}, f32[3,656,128]{2,1,0:T(8,128)}, f32[3,656,128]{2,1,0:T(8,128)}, f32[3,8,128]{2,1,0:T(8,128)}) custom-call(f32[3]{0:T(128)} %pad_maximum_fusion.11.sc, f32[3,656,128]{2,1,0:T(8,128)} %fusion.5.g_in, f32[3,656,128]{2,1,0:T(8,128)} %bitcast.179, ...), custom_call_target="tpu_custom_call", output_to_operand_aliasing={{0}: (6, {}), {1}: (7, {}), {2}: (8, {}), {3}: (9, {})} | custom-call | flops 1 | bytes 1 | tf_op jit(solution)/shard_map/soap_mlp/pallas_call | solution.py:390
  427.2 7.0 %soap_attn.1 = (f32[4,128,256]{2,1,0:T(8,128)}, f32[4,128,256]{2,1,0:T(8,128)}, f32[4,128,256]{2,1,0:T(8,128)}, f32[4,8,128]{2,1,0:T(8,128)}) custom-call(f32[3]{0:T(128)} %pad_maximum_fusion.11.sc, f32[4,128,256]{2,1,0:T(8,128)} %fusion.20.g_in, f32[4,128,256]{2,1,0:T(8,128)} %first.1, f32[4,128,256]{2,1,0:T(8,128)} %second.1, f32[4,128,128]{2,1,0:T(8,128)} %left.7, ...), custom_call_target="tpu_custom_call" | custom-call | flops 1 | bytes 1 | tf_op jit(solution)/shard_map/soap_attn/pallas_call | solution.py:390
  (317 shorter events, 149.2 us)
Async XLA Ops:
  0.6 30.1 %collective-permute-start.4 = (bf16[3,656,128]{2,1,0:T(8,128)(2,1)}, bf16[3,656,128]{2,1,0:T(8,128)(2,1)S(1)}, u32[]{:S(2)}, u32[]{:S(2)}) collective-permute-start(bf16[3,656,128]{2,1,0:T(8,128)(2,1)} %bitcast.186), channel_id=1, source_target_pairs={{0,16},{4,20},{8,24},{12,28},{16,0},{20,4},{24,8},{28,12},{1,17},{... | collective-permute-start | bytes 1511432 | tf_op jit(solution)/shard_map/ppermute | solution.py:401
  3.7 27.1 %collective-permute-start.3 = (bf16[3,656,128]{2,1,0:T(8,128)(2,1)}, bf16[3,656,128]{2,1,0:T(8,128)(2,1)S(1)}, u32[]{:S(2)}, u32[]{:S(2)}) collective-permute-start(bf16[3,656,128]{2,1,0:T(8,128)(2,1)} %bitcast.187), channel_id=1, source_target_pairs={{0,8},{4,12},{8,0},{12,4},{16,24},{20,28},{24,16},{28,20},{1,9},{5... | collective-permute-start | bytes 1511432 | tf_op jit(solution)/shard_map/ppermute | solution.py:401
  39.1 45.8 %collective-permute-start.15 = (bf16[4,4,128,256]{3,2,1,0:T(8,128)(2,1)S(1)}, bf16[4,4,128,256]{3,2,1,0:T(8,128)(2,1)}, u32[]{:S(2)}, u32[]{:S(2)}) collective-permute-start(bf16[4,4,128,256]{3,2,1,0:T(8,128)(2,1)S(1)} %pad_maximum_fusion.1.rest_0_), channel_id=1, source_target_pairs={{0,4},{4,0},{8,12},{12,8},{16,20},{20,16},{24,28},{28,24},{1,5},{5... | collective-permute-start | bytes 3145736 | tf_op jit(solution)/shard_map/ppermute | solution.py:401
  60.3 25.5 %collective-permute-start.16 = (bf16[4,4,128,256]{3,2,1,0:T(8,128)(2,1)S(1)}, bf16[4,4,128,256]{3,2,1,0:T(8,128)(2,1)}, u32[]{:S(2)}, u32[]{:S(2)}) collective-permute-start(bf16[4,4,128,256]{3,2,1,0:T(8,128)(2,1)S(1)} %collective-permute-done.5.rest_1_), channel_id=1, source_target_pairs={{0,4},{4,0},{8,12},{12,8},{16,20},{20,16},{24,28},{28,24},{1,5},{5... | collective-permute-start | bytes 3145736 | tf_op jit(solution)/shard_map/ppermute | solution.py:401
  60.4 26.9 %collective-permute-start.17 = (bf16[4,4,128,256]{3,2,1,0:T(8,128)(2,1)S(1)}, bf16[4,4,128,256]{3,2,1,0:T(8,128)(2,1)}, u32[]{:S(2)}, u32[]{:S(2)}) collective-permute-start(bf16[4,4,128,256]{3,2,1,0:T(8,128)(2,1)S(1)} %collective-permute-done.6.rest_2_), channel_id=1, source_target_pairs={{0,4},{4,0},{8,12},{12,8},{16,20},{20,16},{24,28},{28,24},{1,5},{5... | collective-permute-start | bytes 3145736 | tf_op jit(solution)/shard_map/ppermute | solution.py:401
  85.0 37.5 %collective-permute-start.30 = (bf16[3,656,128]{2,1,0:T(8,128)(2,1)}, bf16[3,656,128]{2,1,0:T(8,128)(2,1)S(1)}, u32[]{:S(2)}, u32[]{:S(2)}) collective-permute-start(bf16[3,656,128]{2,1,0:T(8,128)(2,1)} %bitcast.189), channel_id=1, source_target_pairs={{0,3},{2,1},{3,0},{1,2},{4,7},{6,5},{7,4},{5,6},{8,11},{10,9},{11,... | collective-permute-start | bytes 1511432 | tf_op jit(solution)/shard_map/ppermute | solution.py:420
  85.8 35.5 %collective-permute-start.14 = (bf16[3,656,128]{2,1,0:T(8,128)(2,1)}, bf16[3,656,128]{2,1,0:T(8,128)(2,1)S(1)}, u32[]{:S(2)}, u32[]{:S(2)}) collective-permute-start(bf16[3,656,128]{2,1,0:T(8,128)(2,1)} %bitcast.190), channel_id=1, source_target_pairs={{0,1},{2,0},{3,2},{1,3},{4,5},{6,4},{7,6},{5,7},{8,9},{10,8},{11,1... | collective-permute-start | bytes 1511432 | tf_op jit(solution)/shard_map/ppermute | solution.py:420
  87.3 34.0 %collective-permute-start.13 = (bf16[3,656,128]{2,1,0:T(8,128)(2,1)}, bf16[3,656,128]{2,1,0:T(8,128)(2,1)}, u32[]{:S(2)}, u32[]{:S(2)}) collective-permute-start(bf16[3,656,128]{2,1,0:T(8,128)(2,1)} %copy-done.21), channel_id=1, source_target_pairs={{0,16},{4,20},{8,24},{12,28},{16,0},{20,4},{24,8},{28,12},{1,17},{... | collective-permute-start | bytes 1511432 | tf_op jit(solution)/shard_map/ppermute | solution.py:401
  88.8 32.5 %collective-permute-start.12 = (bf16[3,656,128]{2,1,0:T(8,128)(2,1)}, bf16[3,656,128]{2,1,0:T(8,128)(2,1)}, u32[]{:S(2)}, u32[]{:S(2)}) collective-permute-start(bf16[3,656,128]{2,1,0:T(8,128)(2,1)} %copy-done.21), channel_id=1, source_target_pairs={{0,8},{4,12},{8,0},{12,4},{16,24},{20,28},{24,16},{28,20},{1,9},{5... | collective-permute-start | bytes 1511432 | tf_op jit(solution)/shard_map/ppermute | solution.py:401
  90.3 31.0 %collective-permute-start.11 = (bf16[3,656,128]{2,1,0:T(8,128)(2,1)}, bf16[3,656,128]{2,1,0:T(8,128)(2,1)}, u32[]{:S(2)}, u32[]{:S(2)}) collective-permute-start(bf16[3,656,128]{2,1,0:T(8,128)(2,1)} %copy-done.17), channel_id=1, source_target_pairs={{0,16},{4,20},{8,24},{12,28},{16,0},{20,4},{24,8},{28,12},{1,17},{... | collective-permute-start | bytes 1511432 | tf_op jit(solution)/shard_map/ppermute | solution.py:401
  123.3 25.7 %collective-permute-start.27 = (bf16[3,656,128]{2,1,0:T(8,128)(2,1)}, bf16[3,656,128]{2,1,0:T(8,128)(2,1)S(1)}, u32[]{:S(2)}, u32[]{:S(2)}) collective-permute-start(bf16[3,656,128]{2,1,0:T(8,128)(2,1)} %collective-permute-done.13), channel_id=1, source_target_pairs={{0,8},{4,12},{8,0},{12,4},{16,24},{20,28},{24,16},{28,20},{1,9},{5... | collective-permute-start | bytes 1511432 | tf_op jit(solution)/shard_map/ppermute | solution.py:401
  151.2 27.8 %collective-permute-start.34 = (bf16[3,656,128]{2,1,0:T(8,128)(2,1)S(1)}, bf16[3,656,128]{2,1,0:T(8,128)(2,1)S(1)}, u32[]{:S(2)}, u32[]{:S(2)}) collective-permute-start(bf16[3,656,128]{2,1,0:T(8,128)(2,1)S(1)} %collective-permute-done.28), channel_id=1, source_target_pairs={{0,4},{4,0},{8,12},{12,8},{16,20},{20,16},{24,28},{28,24},{1,5},{5... | collective-permute-start | bytes 1511432 | tf_op jit(solution)/shard_map/ppermute | solution.py:401
  151.6 27.4 %collective-permute-start.32 = (bf16[3,656,128]{2,1,0:T(8,128)(2,1)S(1)}, bf16[3,656,128]{2,1,0:T(8,128)(2,1)}, u32[]{:S(2)}, u32[]{:S(2)}) collective-permute-start(bf16[3,656,128]{2,1,0:T(8,128)(2,1)S(1)} %collective-permute-done.28), channel_id=1, source_target_pairs={{0,16},{4,20},{8,24},{12,28},{16,0},{20,4},{24,8},{28,12},{1,17},{... | collective-permute-start | bytes 1511432 | tf_op jit(solution)/shard_map/ppermute | solution.py:401
  152.4 26.6 %collective-permute-start.35 = (bf16[3,656,128]{2,1,0:T(8,128)(2,1)S(1)}, bf16[3,656,128]{2,1,0:T(8,128)(2,1)S(1)}, u32[]{:S(2)}, u32[]{:S(2)}) collective-permute-start(bf16[3,656,128]{2,1,0:T(8,128)(2,1)S(1)} %collective-permute-done.29), channel_id=1, source_target_pairs={{0,4},{4,0},{8,12},{12,8},{16,20},{20,16},{24,28},{28,24},{1,5},{5... | collective-permute-start | bytes 1511432 | tf_op jit(solution)/shard_map/ppermute | solution.py:401
  152.4 26.6 %collective-permute-start.37 = (bf16[3,656,128]{2,1,0:T(8,128)(2,1)S(1)}, bf16[3,656,128]{2,1,0:T(8,128)(2,1)}, u32[]{:S(2)}, u32[]{:S(2)}) collective-permute-start(bf16[3,656,128]{2,1,0:T(8,128)(2,1)S(1)} %collective-permute-done.30), channel_id=1, source_target_pairs={{0,16},{4,20},{8,24},{12,28},{16,0},{20,4},{24,8},{28,12},{1,17},{... | collective-permute-start | bytes 1511432 | tf_op jit(solution)/shard_map/ppermute | solution.py:401
  153.7 25.4 %collective-permute-start.36 = (bf16[3,656,128]{2,1,0:T(8,128)(2,1)S(1)}, bf16[3,656,128]{2,1,0:T(8,128)(2,1)S(1)}, u32[]{:S(2)}, u32[]{:S(2)}) collective-permute-start(bf16[3,656,128]{2,1,0:T(8,128)(2,1)S(1)} %collective-permute-done.30), channel_id=1, source_target_pairs={{0,8},{4,12},{8,0},{12,4},{16,24},{20,28},{24,16},{28,20},{1,9},{5... | collective-permute-start | bytes 1511432 | tf_op jit(solution)/shard_map/ppermute | solution.py:401
  200.0 29.2 %collective-permute-start.45 = (bf16[1,3,656,128]{3,2,1,0:T(8,128)(2,1)}, bf16[1,3,656,128]{3,2,1,0:T(8,128)(2,1)S(1)}, u32[]{:S(2)}, u32[]{:S(2)}) collective-permute-start(bf16[1,3,656,128]{3,2,1,0:T(8,128)(2,1)} %get-tuple-element.312), channel_id=1, source_target_pairs={{0,16},{4,20},{8,24},{12,28},{16,0},{20,4},{24,8},{28,12},{1,17},{... | collective-permute-start | bytes 1511432 | tf_op jit(solution)/shard_map/ppermute | solution.py:401
  201.1 28.0 %collective-permute-start.46 = (bf16[1,3,656,128]{3,2,1,0:T(8,128)(2,1)}, bf16[1,3,656,128]{3,2,1,0:T(8,128)(2,1)}, u32[]{:S(2)}, u32[]{:S(2)}) collective-permute-start(bf16[1,3,656,128]{3,2,1,0:T(8,128)(2,1)} %get-tuple-element.313), channel_id=1, source_target_pairs={{0,8},{4,12},{8,0},{12,4},{16,24},{20,28},{24,16},{28,20},{1,9},{5... | collective-permute-start | bytes 1511432 | tf_op jit(solution)/shard_map/ppermute | solution.py:401
  229.1 28.6 %collective-permute-start.49 = (bf16[4,2,3,656,128]{4,3,2,1,0:T(8,128)(2,1)}, bf16[4,2,3,656,128]{4,3,2,1,0:T(8,128)(2,1)}, u32[]{:S(2)}, u32[]{:S(2)}) collective-permute-start(bf16[4,2,3,656,128]{4,3,2,1,0:T(8,128)(2,1)} %get-tuple-element.339), channel_id=1, source_target_pairs={{0,4},{4,0},{8,12},{12,8},{16,20},{20,16},{24,28},{28,24},{1,5},{5... | collective-permute-start | bytes 12091400 | tf_op jit(solution)/shard_map/ppermute | solution.py:401
  232.4 24.9 %collective-permute-start.47 = (bf16[2,3,656,128]{3,2,1,0:T(8,128)(2,1)}, bf16[2,3,656,128]{3,2,1,0:T(8,128)(2,1)S(1)}, u32[]{:S(2)}, u32[]{:S(2)}) collective-permute-start(bf16[2,3,656,128]{3,2,1,0:T(8,128)(2,1)} %pad_maximum_fusion.4), channel_id=1, source_target_pairs={{0,8},{4,12},{8,0},{12,4},{16,24},{20,28},{24,16},{28,20},{1,9},{5... | collective-permute-start | bytes 3022856 | tf_op jit(solution)/shard_map/ppermute | solution.py:401
  233.3 24.4 %collective-permute-start.48 = (bf16[2,3,656,128]{3,2,1,0:T(8,128)(2,1)S(1)}, bf16[2,3,656,128]{3,2,1,0:T(8,128)(2,1)S(1)}, u32[]{:S(2)}, u32[]{:S(2)}) collective-permute-start(bf16[2,3,656,128]{3,2,1,0:T(8,128)(2,1)S(1)} %pad_maximum_fusion.5), channel_id=1, source_target_pairs={{0,16},{4,20},{8,24},{12,28},{16,0},{20,4},{24,8},{28,12},{1,17},{... | collective-permute-start | bytes 3022856 | tf_op jit(solution)/shard_map/ppermute | solution.py:401
  290.7 27.6 %collective-permute-start.53 = (bf16[2,3,656,128]{3,2,1,0:T(8,128)(2,1)}, bf16[2,3,656,128]{3,2,1,0:T(8,128)(2,1)S(1)}, u32[]{:S(2)}, u32[]{:S(2)}) collective-permute-start(bf16[2,3,656,128]{3,2,1,0:T(8,128)(2,1)} %pad_maximum_fusion.6), channel_id=1, source_target_pairs={{0,8},{4,12},{8,0},{12,4},{16,24},{20,28},{24,16},{28,20},{1,9},{5... | collective-permute-start | bytes 3022856 | tf_op jit(solution)/shard_map/ppermute | solution.py:401
  291.6 26.8 %collective-permute-start.54 = (bf16[2,3,656,128]{3,2,1,0:T(8,128)(2,1)}, bf16[2,3,656,128]{3,2,1,0:T(8,128)(2,1)}, u32[]{:S(2)}, u32[]{:S(2)}) collective-permute-start(bf16[2,3,656,128]{3,2,1,0:T(8,128)(2,1)} %pad_maximum_fusion.7), channel_id=1, source_target_pairs={{0,16},{4,20},{8,24},{12,28},{16,0},{20,4},{24,8},{28,12},{1,17},{... | collective-permute-start | bytes 3022856 | tf_op jit(solution)/shard_map/ppermute | solution.py:401
  320.5 36.4 %collective-permute-start.63 = (bf16[512,1024]{1,0:T(8,128)(2,1)}, bf16[512,1024]{1,0:T(8,128)(2,1)S(1)}, u32[]{:S(2)}, u32[]{:S(2)}) collective-permute-start(bf16[512,1024]{1,0:T(8,128)(2,1)} %get-tuple-element.391), channel_id=1, source_target_pairs={{0,1},{1,0},{2,3},{3,2},{4,5},{5,4},{6,7},{7,6},{8,9},{9,8},{10,11... | collective-permute-start | bytes 3145736 | tf_op jit(solution)/shard_map/ppermute | solution.py:709
  (105 other events, 1421.6 us)

commit v3 on v2

--- a/solution.py
+++ b/solution.py
@@ -392,6 +392,43 @@
         cost_estimate=pl.CostEstimate(flops=1,transcendentals=0,bytes_accessed=1),
         name="soap_"+("mlp" if turned else "attn"))(scalars,g,first,second,left,right,*carry)
 
+def norm_kernel(own, far, gain, a1, a1T, xh, *, T):
+    for lo,ref in ((0,own),(T,far)):
+        v=ref[...].astype(F32)
+        ce=v-jnp.mean(v,axis=1,keepdims=True)
+        x=ce*lax.rsqrt(jnp.mean(ce*ce,axis=1,keepdims=True)+NORM_EPS)
+        n=ref.shape[0]
+        xh[lo:lo+n,:]=x.astype(BF)
+        y=x*gain[...]
+        a1[lo:lo+n,:]=y.astype(BF)
+        a1T[:,lo:lo+n]=y.T.astype(BF)
+
+def norm_first(own,far,gain):
+    T,D=own.shape; KV=T+far.shape[0]
+    sd=jax.ShapeDtypeStruct
+    outs=[sd((KV,D),BF),sd((D,KV),BF),sd((KV,D),BF)]
+    return pl.pallas_call(functools.partial(norm_kernel,T=T),grid=(1,),in_specs=[full(x.shape) for x in (own,far,gain)],
+        out_specs=[full(o.shape) for o in outs],out_shape=outs,
+        cost_estimate=pl.CostEstimate(flops=1,transcendentals=0,bytes_accessed=1),name="norm_first")(own,far,gain)
+
+def input_kernel(hid, da, dres, gain, *rest):
+    out=rest[-1]
+    v=hid[...].astype(F32)
+    ce=v-jnp.mean(v,axis=1,keepdims=True)
+    rstd=lax.rsqrt(jnp.mean(ce*ce,axis=1,keepdims=True)+NORM_EPS)
+    x=ce*rstd
+    d=da[...]
+    for r in rest[:-1]:
+        d=d+r[...].astype(F32)
+    e=d*gain[...]
+    out[...]=(dres[...]+rstd*(e-jnp.mean(e,axis=1,keepdims=True)-x*jnp.mean(e*x,axis=1,keepdims=True))).astype(BF)
+
+def input_back(hid,da,dres,gain,*back):
+    args=(hid,da,dres,gain)+back
+    return pl.pallas_call(input_kernel,grid=(1,),in_specs=[full(x.shape) for x in args],out_specs=full(hid.shape),
+        out_shape=jax.ShapeDtypeStruct(hid.shape,BF),
+        cost_estimate=pl.CostEstimate(flops=1,transcendentals=0,bytes_accessed=1),name="input_back")(*args)
+
 
 def ring_order(count):
     return list(range(0, count, 2)) + list(range(1, count, 2))[::-1]
@@ -587,58 +624,71 @@
     query_seg = seg[None, :rows]
     keep_own = keep_seq[:rows].astype(F32)[:, None]
 
-    def normalize_first(far_rows):
-        hidden_seq = jnp.concatenate([hidden_in] + far_rows).astype(F32)
-        centred = hidden_seq - jnp.mean(hidden_seq, axis=-1, keepdims=True)
-        rstd = lax.rsqrt(jnp.mean(centred * centred, axis=-1, keepdims=True) + NORM_EPS)
-        xhat = centred * rstd
-        first_norm = (xhat * gain_rows[0]).astype(BF)
-        return first_norm, first_norm.T, xhat.astype(BF), xhat[:rows], rstd[:rows]
-
-    back_args = (cos_table, sin_table, key_seg, query_seg)
+    first_gain, second_gain = gain_rows[0:1], gain_rows[1:2]
     if fast:
-        line = [attn_weight] + [None] * 3
-        for t in (1, 3, 2):
-            line[t] = along_line(attn_weight, t, shards)
-        mlp_line = [mlp_turned] + [None] * 3
+        together = lax.optimization_barrier
         mlp_x, mlp_y, mlp_z = [None] * 4, [None] * 4, [None] * 4
+        line_1 = along_line(attn_weight, 1, shards)
         mlp_x[0], mlp_y[0] = swap_dp(mlp_turned, 2, owners), swap_dp(mlp_turned, 4, owners)
-        line, mlp_x[0], mlp_y[0] = lax.optimization_barrier((line, mlp_x[0], mlp_y[0]))
-        far_rows = from_peer(after(hidden_in, line[2]), 1)
-        stacked = jnp.stack(line)
-        by_x, by_y = swap_dp(stacked, 2, owners), swap_dp(stacked, 4, owners)
-        by_x, by_y, far_rows = lax.optimization_barrier((by_x, by_y, far_rows))
-        across = [swap_dp(by_x[:half], 4, owners), swap_dp(by_y[half:], 2, owners)]
-        turn = after(mlp_turned, far_rows)
-        for t in (1, 3, 2):
-            mlp_line[t] = along_line(turn, t, shards)
-        normal = normalize_first([far_rows])
-        across, normal, mlp_line[1] = lax.optimization_barrier((across, normal, mlp_line[1]))
-        first_norm, first_turned, xhat_low, own_hat, own_rstd = normal
-        arrays = [stacked, by_x, by_y, *across]
-        metas = tuple((r, f, n, shards) for r, f, n in ((0, 0, shards), (2, 0, shards), (4, 0, shards), (6, 0, half), (6, half, half)))
-        attn_pieces = (*with_partner(arrays, metas, owners), shards, slab, attn_weight.shape[2])
+        tables = (cos_table, sin_table, key_seg, query_seg, keep_own, attn_perm, mlp_perm, slots, first_gain, second_gain)
+        line_1, mlp_x[0], mlp_y[0] = together((line_1, mlp_x[0], mlp_y[0]))
+        pair_a = jnp.stack([attn_weight, line_1])
+        x_a, y_a = swap_dp(pair_a, 2, owners), swap_dp(pair_a, 4, owners)
+        line_2, line_3 = along_line(line_1, 1, shards), along_line(after(attn_weight, line_1), 3, shards)
+        mlp_z[0] = swap_dp(mlp_y[0], 2, owners)
+        x_a, y_a, line_2, line_3, tables = together((x_a, y_a, line_2, line_3, tables))
+        cos_table, sin_table, key_seg, query_seg, keep_own, attn_perm, mlp_perm, slots, first_gain, second_gain = tables
+        z_a = swap_dp(x_a, 4, owners)
+        far_rows = from_peer(after(hidden_in, line_2), 1)
+        core_own_a, core_x_a, core_y_a = to_core([after(pair_a, line_2), x_a, y_a], owners)
+        mlp_line = [mlp_turned, along_line(after(mlp_turned, core_x_a), 1, shards), None, None]
+        pair_b = jnp.stack([line_2, line_3])
+        z_a, mlp_z[0], core_own_a, core_x_a, core_y_a, pair_b = together((z_a, mlp_z[0], core_own_a, core_x_a, core_y_a, pair_b))
+        x_b, y_b = swap_dp(pair_b, 2, owners), swap_dp(pair_b, 4, owners)
+        core_z_a, core_own_b = to_core([z_a, pair_b], owners)
+        normal = norm_first(hidden_in, far_rows, first_gain)
+        x_b, y_b, core_z_a, core_own_b, normal, mlp_line[1] = together((x_b, y_b, core_z_a, core_own_b, tuple(normal), mlp_line[1]))
+        z_b = swap_dp(y_b, 2, owners)
+        core_x_b, core_y_b = to_core([x_b, y_b], owners)
+        core_0 = to_core([after(a, y_b) for a in (mlp_turned, mlp_x[0], mlp_y[0], mlp_z[0])], owners)
+        normal, mlp_line[1], core_x_b, core_y_b, core_0 = together((normal, mlp_line[1], core_x_b, core_y_b, core_0))
+        first_norm, first_turned, xhat_low = normal
+
+        def attn_set(arrays, first):
+            return arrays, tuple((r, first, 2, shards) for r in (0, 2, 4, 6, 1, 3, 5, 7))
+
+        sizes = (shards, slab, attn_weight.shape[2])
+        arrays_a, metas_a = attn_set([pair_a, x_a, y_a, z_a, core_own_a, core_x_a, core_y_a, core_z_a], 0)
+        attn_part_a = (arrays_a, metas_a, *sizes)
         mlp_x[1], mlp_y[1] = swap_dp(mlp_line[1], 2, owners), swap_dp(mlp_line[1], 4, owners)
-        mlp_z[0] = swap_dp(after(mlp_x[0], mlp_line[1]), 4, owners)
+        mlp_line[2], mlp_line[3] = along_line(mlp_line[1], 1, shards), along_line(after(mlp_turned, mlp_line[1]), 3, shards)
     else:
         far_rows = [from_peer(hidden_in, d) for d in range(1, span)]
         attn_pieces = ([attn_all], (None,), shards, slab, attn_weight.shape[2])
-        first_norm, first_turned, xhat_low, own_hat, own_rstd = normalize_first(far_rows)
-    fwd_args = (attn_perm, first_norm, hidden_in, gain_rows[1:2], cos_table, sin_table, key_seg, query_seg, keep_own)
+        first_norm, first_turned, xhat_low = norm_first(hidden_in, jnp.concatenate(far_rows), first_gain)
+    back_args = (cos_table, sin_table, key_seg, query_seg)
+    fwd_args = (attn_perm, first_norm, hidden_in, second_gain, cos_table, sin_table, key_seg, query_seg, keep_own)
     if fast:
-        carry = fwd_attn(*fwd_args, attn_pieces, S0=0, N=half)
-        set_0 = [mlp_line[0], mlp_x[0], mlp_y[0], mlp_z[0]]
-        set_1 = [mlp_line[1], mlp_x[1], mlp_y[1]]
-        set_0, set_1, mlp_line[3], carry = lax.optimization_barrier((set_0, set_1, mlp_line[3], tuple(carry)))
-        mlp_z[1] = swap_dp(set_1[2], 2, owners)
+        carry = fwd_attn(*fwd_args, attn_part_a, S0=0, N=half)
+        z_b, mlp_x[1], mlp_y[1], mlp_line[2], mlp_line[3], carry = together(
+            (z_b, mlp_x[1], mlp_y[1], mlp_line[2], mlp_line[3], tuple(carry))
+        )
+        core_z_b = swap_dp(z_b, 1, owners)
+        core_z_b, mlp_x[1], mlp_y[1], mlp_line[2], mlp_line[3] = together((core_z_b, mlp_x[1], mlp_y[1], mlp_line[2], mlp_line[3]))
+        arrays_b, metas_b = attn_set([pair_b, x_b, y_b, z_b, core_own_b, core_x_b, core_y_b, core_z_b], 2)
+        attn_part_b = (arrays_b, metas_b, *sizes)
+        attn_pieces = (arrays_a + arrays_b, metas_a + metas_b, *sizes)
+        mlp_z[1] = swap_dp(mlp_y[1], 2, owners)
+        mlp_x[2], mlp_y[2] = swap_dp(mlp_line[2], 2, owners), swap_dp(mlp_line[2], 4, owners)
         mlp_x[3], mlp_y[3] = swap_dp(mlp_line[3], 2, owners), swap_dp(mlp_line[3], 4, owners)
-        core_0, core_1 = to_core(set_0, owners), to_core(set_1, owners)
-        out = fwd_attn(*fwd_args, attn_pieces, S0=half, N=half, carry=carry)
-        set_3 = [mlp_line[3], mlp_x[3], mlp_y[3]]
-        core_0, core_1, far_z, set_3, mlp_line[2], out = lax.optimization_barrier((core_0, core_1, mlp_z[1], set_3, mlp_line[2], tuple(out)))
+        out = fwd_attn(*fwd_args, attn_part_b, S0=half, N=half, carry=carry)
+        mlp_z[1], mlp_x[2], mlp_y[2], mlp_y[3], mlp_x[0], mlp_x[1], out = together(
+            (mlp_z[1], mlp_x[2], mlp_y[2], mlp_y[3], mlp_x[0], mlp_x[1], tuple(out))
+        )
         queries, keys, values, attended, log_sums, resid, second_norm, stat_a = out
-        set_1, core_1 = set_1 + [far_z], core_1 + to_core([far_z], owners)
-        core_1, second_norm, set_3, mlp_line[2] = lax.optimization_barrier((core_1, second_norm, set_3, mlp_line[2]))
+
+        def mlp_set(slot):
+            return [mlp_line[slot], mlp_x[slot], mlp_y[slot], mlp_z[slot]]
 
         def mlp_pieces(*slots_of):
             arrays, metas = [], []
@@ -647,17 +697,19 @@
                 metas += [(r, slot, 1, shards) for r in (0, 2, 4, 6, 1, 3, 5, 7)]
             return arrays, tuple(metas), shards, slab, hid_cols
 
-        mlp_z[3] = swap_dp(set_3[1], 4, owners)
-        set_2 = [mlp_line[2], swap_dp(mlp_line[2], 2, owners), swap_dp(mlp_line[2], 4, owners)]
-        core_3 = to_core(set_3, owners)
-        mlp_args = (mlp_perm, slots, second_norm, out_grad, resid, gain_rows[1:2], keep_own)
+        set_0, set_1 = mlp_set(0), mlp_set(1)
+        set_1 = [after(a, mlp_z[1]) for a in set_1]
+        core_1 = to_core(set_1, owners)
+        core_1, second_norm, mlp_x[2], mlp_y[3] = together((core_1, second_norm, mlp_x[2], mlp_y[3]))
+        mlp_z[2], mlp_z[3] = swap_dp(mlp_x[2], 4, owners), swap_dp(mlp_y[3], 2, owners)
+        core_2 = to_core([after(mlp_line[2], second_norm), mlp_x[2]], owners)
+        mlp_args = (mlp_perm, slots, second_norm, out_grad, resid, second_gain, keep_own)
         out = mlp(*mlp_args, mlp_pieces((0, set_0 + core_0), (1, set_1 + core_1)), S0=0, N=half)
-        far_z, core_3, set_2, out = lax.optimization_barrier((mlp_z[3], core_3, set_2, tuple(out)))
-        set_3, core_3 = set_3 + [far_z], core_3 + to_core([far_z], owners)
-        far_z = swap_dp(set_2[2], 2, owners)
-        core_2 = to_core(set_2, owners)
-        set_2, core_2 = set_2 + [far_z], core_2 + to_core([far_z], owners)
+        mlp_x[3], mlp_z[2], mlp_z[3], core_2, out = together((mlp_x[3], mlp_z[2], mlp_z[3], core_2, tuple(out)))
         *carry, even_a, odd_a = out
+        set_2, set_3 = mlp_set(2), mlp_set(3)
+        set_2, set_3 = [after(a, odd_a) for a in set_2], [after(a, odd_a) for a in set_3]
+        core_2, core_3 = core_2 + to_core(set_2[2:], owners), to_core(set_3, owners)
         core_a = swap_dp(odd_a, 1, owners)
         low, high = cross_sends(even_a, core_a, 1)
         low, high, core_2, core_3, carry = lax.optimization_barrier((low, high, core_2, core_3, carry))
@@ -688,7 +740,7 @@
     else:
         queries, keys, values, attended, log_sums, resid, second_norm, stat_a = fwd_attn(*fwd_args, attn_pieces)
         output, dresid, dres_low, dres_turned, gain_two, stat_m, mlp_even, mlp_odd = mlp(
-            mlp_perm, slots, second_norm, out_grad, resid, gain_rows[1:2], keep_own,
+            mlp_perm, slots, second_norm, out_grad, resid, second_gain, keep_own,
             ([mlp_all], (None,), shards, mlp_all.shape[-1], hid_cols),
         )
         if joined > 1:
@@ -713,14 +765,7 @@
         return lax.ppermute(value, "tensor", [(i, i ^ bit) for i in range(shards)])
 
     def finish_input(da_back):
-        first_grad = add_all(da_own, *da_back)
-        scaled = first_grad * gain_rows[0]
-        input_part = own_rstd * (
-            scaled
-            - jnp.mean(scaled, axis=-1, keepdims=True)
-            - own_hat * jnp.mean(scaled * own_hat, axis=-1, keepdims=True)
-        )
-        return (dresid + input_part).astype(BF)
+        return input_back(hidden_in, da_own, dresid, first_gain, *da_back)
 
     step_count = step.astype(F32)
     step_size = (
@@ -740,31 +785,33 @@
     small = jnp.concatenate([gain_one, gain_two, jnp.pad(sums, (0, width - 5))[None]], axis=0)
     if fast:
         attn_core = swap_dp(attn_odd, 1, owners)
-        da_back = send_back(da_far)
+        ring_2 = (own_part(even_b, core_b, from_x, from_y, 0) + ring_1.astype(F32)).astype(BF)
+        ring_2 = to_ring_succ(ring_2, shards)
         small = small + swap_dp(small, 1, owners)
         small, attn_core = lax.optimization_barrier((small, attn_core))
-        ring_2 = (own_part(even_b, core_b, from_x, from_y, 0) + ring_1.astype(F32)).astype(BF)
-        ring_2 = to_ring_succ(ring_2, shards)
         low, high = cross_sends(attn_even, attn_core, half)
         cross_y, cross_x = swap_dp(low, 4, owners), swap_dp(high, 2, owners)
+        da_back = send_back(da_far)
         small = (small + swap_dp(small, 2, owners)) + (swap_dp(small, 4, owners) + swap_dp(small, 6, owners))
-        small, cross_x, cross_y = lax.optimization_barrier((small, cross_x, cross_y))
+        small, cross_x, cross_y, da_back = lax.optimization_barrier((small, cross_x, cross_y, da_back))
         to_x, to_y = side_sends(attn_even, attn_core, cross_y, cross_x, half)
-        to_x, to_y, ring_2, da_back, small = lax.optimization_barrier((to_x, to_y, ring_2, da_back, small))
+        to_x, to_y, small, ring_2 = lax.optimization_barrier((to_x, to_y, small, ring_2))
         attn_x, attn_y = swap_dp(to_x, 2, owners), swap_dp(to_y, 4, owners)
         ring_3 = (own_part(even_b, core_b, from_x, from_y, 1) + ring_2.astype(F32)).astype(BF)
         ring_3 = to_ring_succ(ring_3, shards)
-        small = (small + swap_line(small, 1)) + (swap_line(small, 2) + swap_line(small, 3))
-        input_grad = finish_input(da_back)
-        small, attn_x, attn_y, ring_3, input_grad = lax.optimization_barrier((small, attn_x, attn_y, ring_3, input_grad))
+        mlp_sum = own_part(even_a, core_a, back_x, back_y, 0) + ring_3.astype(F32)
+        mlp_new = soap_mlp(mlp_sum)
+        attn_x, attn_y, mlp_sum, mlp_new = lax.optimization_barrier((attn_x, attn_y, mlp_sum, tuple(mlp_new)))
         moving = own_part(attn_even, attn_core, attn_x, attn_y, 1).astype(BF)
-        mlp_sum = own_part(even_a, core_a, back_x, back_y, 0) + ring_3.astype(F32)
-        mlp_new = ()
         for slot in range(1, shards):
-            moving, mlp_sum = lax.optimization_barrier((moving, mlp_sum))
+            moving, small, da_back = lax.optimization_barrier((moving, small, da_back))
             moving = to_ring_succ(moving, shards)
-            mlp_new = soap_mlp(mlp_sum, slot - 1, 1, mlp_new)
-            moving, mlp_new = lax.optimization_barrier((moving, tuple(mlp_new)))
+            if slot < 3:
+                small = small + swap_line(small, slot)
+            if slot == 1:
+                input_grad = finish_input(da_back)
+                moving, input_grad = lax.optimization_barrier((moving, input_grad))
+            moving, small = lax.optimization_barrier((moving, small))
             moving = moving.astype(F32) + own_part(attn_even, attn_core, attn_x, attn_y, (slot + 1) % shards)
             if slot + 1 < shards:
                 moving = moving.astype(BF)

time: 442 us -> 418 us (0.946)
  waiting for transfers between devices: 114 us -> 97.5 us
  local copies, waits for them, and re-layouts: 19.9 us -> 12.4 us
  other arithmetic: 56.3 us -> 50.2 us
    ppermute x56 -> x61, waiting for transfers between devices: 62.3 us -> 40.8 us  [swap_dp(): return lax.ppermute(value, 'dp', [(i, i ^ bit) for i in range(owners)])]
    ppermute x6, waiting for transfers between devices: 34.7 us -> 17.5 us  [along_line(): lax.ppermute(value, 'tensor', [(ring[p], ring[(p + steps) % shards]) for...]
    pallas_call x0 -> x2, Pallas kernels: none -> 11.1 us  [the longest x1 5.88 us: norm_first(): pl.pallas_call(functools.partial(norm_kernel, T=T), grid=(1,), in_specs=[...]
    ppermute x1, waiting for transfers between devices: 0.01 us -> 9.52 us  [send_back(): got.append(lax.ppermute(da_far[(d - 1) * rows:d * rows], 'tensor', pairs))]
    pallas_call x4 -> x2, Pallas kernels: 28.3 us -> 21.6 us  [soap(): pl.pallas_call(functools.partial(soap_kernel, turned=turned), grid_spec=g...]
    ppermute x3 -> x2, waiting for transfers between devices: 0.01 us -> 6.16 us  [swap_line(): return lax.ppermute(value, 'tensor', [(i, i ^ bit) for i in range(shards)])]
    ppermute x1, waiting for transfers between devices: 0.57 us -> 5.01 us  [from_peer(): return lax.ppermute(value, 'tensor', pairs)]
    ppermute x56 -> x61, starting transfers between devices: 42.5 us -> 42.1 us  [swap_dp(): return lax.ppermute(value, 'dp', [(i, i ^ bit) for i in range(owners)])]
  transfers between devices with their start and end apart: 73 -> 77, of which waited for: 22 -> 26; matrix products, arithmetic and copies ran while one was open for 11% -> 9% of each run, Pallas kernels for 39% -> 42%
where the time goes in v3:
time: 418 us; the launch traced here: 411 us
  Pallas kernels  180 us (43%)
  waiting for transfers between devices  97.5 us (23%)
  starting transfers between devices  65.9 us (16%)
  other arithmetic  50.2 us (12%)
  local copies, waits for them, and re-layouts  12.4 us (3%)
  between operations  5.12 us (1%)
    pallas_call x2, Pallas kernels, mlp(): pl.pallas_call(functools.partial(mlp_kernel, T=T, D=D, HC=HC, R=R, metas=...  50.3 us
    ppermute x61, starting transfers between devices, swap_dp(): return lax.ppermute(value, 'dp', [(i, i ^ bit) for i in range(owners)])  42.1 us
    ppermute x61, waiting for transfers between devices, swap_dp(): return lax.ppermute(value, 'dp', [(i, i ^ bit) for i in range(owners)])  40.8 us
    pallas_call x2, Pallas kernels, bwd_attn(): pl.pallas_call(functools.partial(bwd_attn_kernel, T=T, KV=KV, C=C, metas=...  38.1 us
    pallas_call x2, Pallas kernels, fwd_attn(): pl.pallas_call(functools.partial(fwd_attn_kernel, T=T, KV=KV, C=C, metas=...  36.7 us
    pallas_call x1, Pallas kernels, grad_attn(): pl.pallas_call(functools.partial(grad_attn_kernel, T=T, KV=KV, C=C, R=R,...  22.6 us
    pallas_call x2, Pallas kernels, soap(): pl.pallas_call(functools.partial(soap_kernel, turned=turned), grid_spec=g...  21.6 us
    ppermute x6, waiting for transfers between devices, to_ring_succ(): lax.ppermute(value, 'tensor', [(ring[p], ring[(p + 1) % shards]) for p in...  18.5 us
  transfers between devices with their start and end apart: 77, of which 26 were waited for; matrix products, arithmetic and copies ran while one was open for 9% of the time, Pallas kernels for 42%

profile of v3, /device:TPU:0, one launch (start us, length us, event | category | flops | bytes accessed | tf_op | source)
XLA Modules:
  0.0 411.5 jit_solution(6720658624609438182)
XLA Ops:
  27.7 9.3 %collective-permute-done.6 = bf16[4,128,256]{2,1,0:T(8,128)(2,1)} collective-permute-done((bf16[4,128,256]{2,1,0:T(8,128)(2,1)S(1)}, bf16[4,128,256]{2,1,0:T(8,128)(2,1)}, u32[]{:S(2)}, u32[]{:S(2)}) %collective-permute-start.6) | collective-permute-done | bytes 262176 | tf_op jit(solution)/shard_map/ppermute | solution.py:457
  38.9 3.7 collective-permute-done.8
  45.0 9.3 %collective-permute-done.7.rest_3_ = bf16[2,4,128,256]{3,2,1,0:T(8,128)(2,1)} collective-permute-done((bf16[2,4,128,256]{3,2,1,0:T(8,128)(2,1)S(1)}, bf16[2,4,128,256]{3,2,1,0:T(8,128)(2,1)}, u32[]{:S(2)}, u32[]{:S(2)}) %collective-permute-start.7) | collective-permute-done | bytes 524320 | tf_op jit(solution)/shard_map/ppermute | solution.py:438
  57.2 5.0 %collective-permute-done.16.far = bf16[512,1024]{1,0:T(8,128)(2,1)S(1)} collective-permute-done((bf16[512,1024]{1,0:T(8,128)(2,1)S(1)}, bf16[512,1024]{1,0:T(8,128)(2,1)S(1)}, u32[]{:S(2)}, u32[]{:S(2)}) %collective-permute-start.16) | collective-permute-done | bytes 1048608 | tf_op jit(solution)/shard_map/ppermute | solution.py:578
  64.9 5.9 %norm_first.1 = (bf16[1024,1024]{1,0:T(8,128)(2,1)}, bf16[1024,1024]{1,0:T(8,128)(2,1)}, bf16[1024,1024]{1,0:T(8,128)(2,1)}) custom-call(bf16[512,1024]{1,0:T(8,128)(2,1)} %hid.5, bf16[512,1024]{1,0:T(8,128)(2,1)} %copy-done.13, f32[1,1024]{1,0:T(1,128)} %get-tuple-element.267.gain), custom_call_target="tpu_custom_call" | custom-call | flops 1 | bytes 1 | tf_op jit(solution)/shard_map/norm_first/pallas_call | solution.py:410
  70.8 4.9 %collective-permute-done.17 = bf16[3,656,128]{2,1,0:T(8,128)(2,1)S(1)} collective-permute-done((bf16[3,656,128]{2,1,0:T(8,128)(2,1)}, bf16[3,656,128]{2,1,0:T(8,128)(2,1)S(1)}, u32[]{:S(2)}, u32[]{:S(2)}) %collective-permute-start.17) | collective-permute-done | bytes 503840 | tf_op jit(solution)/shard_map/ppermute | solution.py:457
  88.5 16.7 %attn_fwd.2 = (bf16[4,512,256]{2,1,0:T(8,128)(2,1)}, bf16[4,1024,256]{2,1,0:T(8,128)(2,1)}, bf16[4,1024,256]{2,1,0:T(8,128)(2,1)}, bf16[4,512,256]{2,1,0:T(8,128...) custom-call(s32[16]{0:T(128)} %pad_add_fusion.1.perm, bf16[1024,1024]{1,0:T(8,128)(2,1)} %get-tuple-element.287.a1, ...), custom_call_target="tpu_custom_call" | custom-call | flops 1 | bytes 1 | tf_op jit(solution)/shard_map/attn_fwd/pallas_call | solution.py:134
  114.8 20.0 %attn_fwd.3 = (bf16[4,512,256]{2,1,0:T(8,128)(2,1)}, bf16[4,1024,256]{2,1,0:T(8,128)(2,1)}, bf16[4,1024,256]{2,1,0:T(8,128)(2,1)}, bf16[4,512,256]{2,1,0:T(8,128...) custom-call(s32[16]{0:T(128)} %pad_add_fusion.1.perm, ...), custom_call_target="tpu_custom_call", output_to_operand_aliasing={{0}: (18, {}), {1}: (19, {}), {2}: (20, {}), {3}: (21, {}),... | custom-call | flops 1 | bytes 1 | tf_op jit(solution)/shard_map/attn_fwd/pallas_call | solution.py:134
  142.5 24.0 %mlp_both.2 = (f32[512,1024]{1,0:T(8,128)}, f32[512,1024]{1,0:T(8,128)}, bf16[4,2,3,656,128]{4,3,2,1,0:T(8,128)(2,1)}, bf16[4,2,3,656,128]{4,3,2,1,0:T(8,128)(2,1)}) custom-call(s32[16]{0:T(128)} %pad_add_fusion.1.perm, s32[4]{0:T(128)} %iota.18.slots, bf16[512,1024]{1,0:T(8,128)(2,1)} %get-tuple-element.342.a2, bf16[512,1024]{1,0:T(8,128)(2,1)} %g.3, ...), custom_call_target="tpu_custom_call" | custom-call | flops 1 | bytes 1 | tf_op jit(solution)/shard_map/mlp_both/pallas_call | solution.py:232
  167.9 4.6 %collective-permute-done.44 = bf16[3,656,128]{2,1,0:T(8,128)(2,1)S(1)} collective-permute-done((bf16[3,656,128]{2,1,0:T(8,128)(2,1)S(1)}, bf16[3,656,128]{2,1,0:T(8,128)(2,1)S(1)}, u32[]{:S(2)}, u32[]{:S(2)}) %collective-permute-start.44) | collective-permute-done | bytes 503840 | tf_op jit(solution)/shard_map/ppermute | solution.py:438
  184.2 26.3 %mlp_both.3 = (bf16[512,1024]{1,0:T(8,128)(2,1)}, f32[512,1024]{1,0:T(8,128)}, bf16[512,1024]{1,0:T(8,128)(2,1)}, bf16[1024,512]{1,0:T(8,128)(2,1)}, f32[1,1024]...) custom-call(s32[16]{0:T(128)} %pad_add_fusion.1.perm, ...), custom_call_target="tpu_custom_call" | custom-call | flops 1 | bytes 1 | tf_op jit(solution)/shard_map/mlp_both/pallas_call | solution.py:232
  217.2 18.9 %attn_bwd.2 = (bf16[4,512,256]{2,1,0:T(8,128)(2,1)}, bf16[4,1024,256]{2,1,0:T(8,128)(2,1)}, bf16[4,1024,256]{2,1,0:T(8,128)(2,1)}) custom-call(s32[16]{0:T(128)} %pad_add_fusion.1.perm, bf16[512,1024]{1,0:T(8,128)(2,1)} %get-tuple-element.420.dres, f32[1024,128]{1,0:T(8,128)} %get-tuple-element.289.cos, f32[1024,128]{1,0:T(8,128)} %get-tuple-element.290.sin, ...), custom_call_target="tpu_custom_call" | custom-call | flops 1 | bytes 1 | tf_op jit(solution)/shard_map/attn_bwd/pallas_call | solution.py:290
  240.9 3.9 fusion.29
  249.4 19.2 %attn_bwd.3 = (bf16[4,512,256]{2,1,0:T(8,128)(2,1)}, bf16[4,1024,256]{2,1,0:T(8,128)(2,1)}, bf16[4,1024,256]{2,1,0:T(8,128)(2,1)}) custom-call(s32[16]{0:T(128)} %pad_add_fusion.1.perm, bf16[512,1024]{1,0:T(8,128)(2,1)} %get-tuple-element.420.dres, ...), custom_call_target="tpu_custom_call", output_to_operand_aliasing={{0}: (26, {}), {1}: (27, {}), {2}: (28, {})} | custom-call | flops 1 | bytes 1 | tf_op jit(solution)/shard_map/attn_bwd/pallas_call | solution.py:290
  275.3 22.6 %attn_grad.1 = (f32[512,1024]{1,0:T(8,128)}, bf16[512,1024]{1,0:T(8,128)(2,1)}, f32[1,1024]{1,0:T(1,128)}, bf16[4,4,4,128,256]{4,3,2,1,0:T(8,128)(2,1)}, bf16[4,4,4,128,256]{4,3,2,1,0:T(8,128)(2,1)}) custom-call(s32[16]{0:T(128)} %pad_add_fusion.1.perm, s32[4]{0:T(128)} %iota.18.slots, bf16[1024,1024]{1,0:T(8,128)(2,1)} %get-tuple-element.432.a1T, ...), custom_call_target="tpu_custom_call" | custom-call | flops 1 | bytes 1 | tf_op jit(solution)/shard_map/attn_grad/pallas_call | solution.py:346
  301.4 3.8 collective-permute-done.60
  317.6 9.5 %collective-permute-done.67.rest_0_ = bf16[512,1024]{1,0:T(8,128)(2,1)S(1)} collective-permute-done((bf16[512,1024]{1,0:T(8,128)(2,1)}, bf16[512,1024]{1,0:T(8,128)(2,1)S(1)}, u32[]{:S(2)}, u32[]{:S(2)}) %collective-permute-start.67) | collective-permute-done | bytes 1048608 | tf_op jit(solution)/shard_map/ppermute | solution.py:761
  330.7 6.5 %collective-permute-done.68 = bf16[3,656,128]{2,1,0:T(8,128)(2,1)S(1)} collective-permute-done((bf16[3,656,128]{2,1,0:T(8,128)(2,1)S(1)}, bf16[3,656,128]{2,1,0:T(8,128)(2,1)S(1)}, u32[]{:S(2)}, u32[]{:S(2)}) %collective-permute-start.68) | collective-permute-done | bytes 503840 | tf_op jit(solution)/shard_map/ppermute | solution.py:450
  345.9 7.7 %collective-permute-done.71 = bf16[3,656,128]{2,1,0:T(8,128)(2,1)} collective-permute-done((bf16[3,656,128]{2,1,0:T(8,128)(2,1)}, bf16[3,656,128]{2,1,0:T(8,128)(2,1)}, u32[]{:S(2)}, u32[]{:S(2)}) %collective-permute-start.71) | collective-permute-done | bytes 503840 | tf_op jit(solution)/shard_map/ppermute | solution.py:450
  356.5 14.6 %soap_mlp.1 = (f32[3,656,128]{2,1,0:T(8,128)}, f32[3,656,128]{2,1,0:T(8,128)}, f32[3,656,128]{2,1,0:T(8,128)}, f32[3,8,128]{2,1,0:T(8,128)}) custom-call(f32[3]{0:T(128)} %pad_maximum_fusion.11.sc, f32[3,656,128]{2,1,0:T(8,128)} %fusion.4.g_in, f32[3,656,128]{2,1,0:T(8,128)} %bitcast.173, f32[3,656,128]{2,1,0:T(8,128)} %bitcast.174, f32[3,128,128]{2,1,0:T(8,128)} %left.2, ...), custom_call_target="tpu_custom_call" | custom-call | flops 1 | bytes 1 | tf_op jit(solution)/shard_map/soap_mlp/pallas_call | solution.py:390
  375.2 5.2 %input_back.1 = bf16[512,1024]{1,0:T(8,128)(2,1)} custom-call(bf16[512,1024]{1,0:T(8,128)(2,1)} %hid.5, f32[512,1024]{1,0:T(8,128)} %get-tuple-element.471.da, f32[512,1024]{1,0:T(8,128)} %get-tuple-element.472.dres, f32[1,1024]{1,0:T(1,128)} %get-tuple-element.267.gain, bf16[512,1024]{1,0:T(8,128)(2,1)} %copy-done.12), custom_call_target="tpu_custom_call" | custom-call | flops 1 | bytes 1 | tf_op jit(solution)/shard_map/input_back/pallas_call | solution.py:428
  384.7 6.2 %collective-permute-done.75 = f32[3,1024]{1,0:T(4,128)S(1)} collective-permute-done((f32[3,1024]{1,0:T(4,128)S(1)}, f32[3,1024]{1,0:T(4,128)S(1)}, u32[]{:S(2)}, u32[]{:S(2)}) %collective-permute-start.75) | collective-permute-done | bytes 12320 | tf_op jit(solution)/shard_map/ppermute | solution.py:765
  394.2 4.3 %collective-permute-done.76 = bf16[4,128,256]{2,1,0:T(8,128)(2,1)S(1)} collective-permute-done((bf16[4,128,256]{2,1,0:T(8,128)(2,1)S(1)}, bf16[4,128,256]{2,1,0:T(8,128)(2,1)S(1)}, u32[]{:S(2)}, u32[]{:S(2)}) %collective-permute-start.76) | collective-permute-done | bytes 262176 | tf_op jit(solution)/shard_map/ppermute | solution.py:450
  402.2 7.0 %soap_attn.1 = (f32[4,128,256]{2,1,0:T(8,128)}, f32[4,128,256]{2,1,0:T(8,128)}, f32[4,128,256]{2,1,0:T(8,128)}, f32[4,8,128]{2,1,0:T(8,128)}) custom-call(f32[3]{0:T(128)} %pad_maximum_fusion.11.sc, f32[4,128,256]{2,1,0:T(8,128)} %fusion.16.g_in, f32[4,128,256]{2,1,0:T(8,128)} %first.1, f32[4,128,256]{2,1,0:T(8,128)} %second.1, f32[4,128,128]{2,1,0:T(8,128)} %left.3, ...), custom_call_target="tpu_custom_call" | custom-call | flops 1 | bytes 1 | tf_op jit(solution)/shard_map/soap_attn/pallas_call | solution.py:390
  (306 shorter events, 147.3 us)
Async XLA Ops:
  37.6 24.6 %collective-permute-start.16 = (bf16[512,1024]{1,0:T(8,128)(2,1)S(1)}, bf16[512,1024]{1,0:T(8,128)(2,1)S(1)}, u32[]{:S(2)}, u32[]{:S(2)}) collective-permute-start(bf16[512,1024]{1,0:T(8,128)(2,1)S(1)} %copy-done), channel_id=1, source_target_pairs={{1,0},{0,1},{3,2},{2,3},{5,4},{4,5},{7,6},{6,7},{9,8},{8,9},{11,10... | collective-permute-start | bytes 3145736 | tf_op jit(solution)/shard_map/ppermute | solution.py:578
  80.8 24.4 %collective-permute-start.18 = (bf16[2,4,128,256]{3,2,1,0:T(8,128)(2,1)}, bf16[2,4,128,256]{3,2,1,0:T(8,128)(2,1)}, u32[]{:S(2)}, u32[]{:S(2)}) collective-permute-start(bf16[2,4,128,256]{3,2,1,0:T(8,128)(2,1)} %collective-permute-done.13.rest_2_.rest_10_), channel_id=1, source_target_pairs={{0,8},{4,12},{8,0},{12,4},{16,24},{20,28},{24,16},{28,20},{1,9},{5... | collective-permute-start | bytes 1572872 | tf_op jit(solution)/shard_map/ppermute | solution.py:438
  82.3 22.9 %collective-permute-start.28 = (bf16[3,656,128]{2,1,0:T(8,128)(2,1)}, bf16[3,656,128]{2,1,0:T(8,128)(2,1)}, u32[]{:S(2)}, u32[]{:S(2)}) collective-permute-start(bf16[3,656,128]{2,1,0:T(8,128)(2,1)} %bitcast.179), channel_id=1, source_target_pairs={{0,1},{2,0},{3,2},{1,3},{4,5},{6,4},{7,6},{5,7},{8,9},{10,8},{11,1... | collective-permute-start | bytes 1511432 | tf_op jit(solution)/shard_map/ppermute | solution.py:457
  84.4 24.1 %collective-permute-start.27 = (bf16[3,656,128]{2,1,0:T(8,128)(2,1)}, bf16[3,656,128]{2,1,0:T(8,128)(2,1)}, u32[]{:S(2)}, u32[]{:S(2)}) collective-permute-start(bf16[3,656,128]{2,1,0:T(8,128)(2,1)} %copy-done.23), channel_id=1, source_target_pairs={{0,2},{2,3},{3,1},{1,0},{4,6},{6,7},{7,5},{5,4},{8,10},{10,11},{11... | collective-permute-start | bytes 1511432 | tf_op jit(solution)/shard_map/ppermute | solution.py:457
  86.0 22.5 %collective-permute-start.26 = (bf16[3,656,128]{2,1,0:T(8,128)(2,1)}, bf16[3,656,128]{2,1,0:T(8,128)(2,1)}, u32[]{:S(2)}, u32[]{:S(2)}) collective-permute-start(bf16[3,656,128]{2,1,0:T(8,128)(2,1)} %copy-done.23), channel_id=1, source_target_pairs={{0,16},{4,20},{8,24},{12,28},{16,0},{20,4},{24,8},{28,12},{1,17},{... | collective-permute-start | bytes 1511432 | tf_op jit(solution)/shard_map/ppermute | solution.py:438
  110.7 24.1 %collective-permute-start.31 = (bf16[3,656,128]{2,1,0:T(8,128)(2,1)}, bf16[3,656,128]{2,1,0:T(8,128)(2,1)S(1)}, u32[]{:S(2)}, u32[]{:S(2)}) collective-permute-start(bf16[3,656,128]{2,1,0:T(8,128)(2,1)} %collective-permute-done.26), channel_id=1, source_target_pairs={{0,8},{4,12},{8,0},{12,4},{16,24},{20,28},{24,16},{28,20},{1,9},{5... | collective-permute-start | bytes 1511432 | tf_op jit(solution)/shard_map/ppermute | solution.py:438
  111.2 23.6 %collective-permute-start.34 = (bf16[3,656,128]{2,1,0:T(8,128)(2,1)}, bf16[3,656,128]{2,1,0:T(8,128)(2,1)S(1)}, u32[]{:S(2)}, u32[]{:S(2)}) collective-permute-start(bf16[3,656,128]{2,1,0:T(8,128)(2,1)} %collective-permute-done.28), channel_id=1, source_target_pairs={{0,16},{4,20},{8,24},{12,28},{16,0},{20,4},{24,8},{28,12},{1,17},{... | collective-permute-start | bytes 1511432 | tf_op jit(solution)/shard_map/ppermute | solution.py:438
  112.2 23.3 %collective-permute-start.33 = (bf16[3,656,128]{2,1,0:T(8,128)(2,1)}, bf16[3,656,128]{2,1,0:T(8,128)(2,1)S(1)}, u32[]{:S(2)}, u32[]{:S(2)}) collective-permute-start(bf16[3,656,128]{2,1,0:T(8,128)(2,1)} %collective-permute-done.27), channel_id=1, source_target_pairs={{0,16},{4,20},{8,24},{12,28},{16,0},{20,4},{24,8},{28,12},{1,17},{... | collective-permute-start | bytes 1511432 | tf_op jit(solution)/shard_map/ppermute | solution.py:438
  136.6 30.0 %collective-permute-start.30 = (bf16[3,656,128]{2,1,0:T(8,128)(2,1)}, bf16[3,656,128]{2,1,0:T(8,128)(2,1)S(1)}, u32[]{:S(2)}, u32[]{:S(2)}) collective-permute-start(bf16[3,656,128]{2,1,0:T(8,128)(2,1)} %collective-permute-done.28), channel_id=1, source_target_pairs={{0,8},{4,12},{8,0},{12,4},{16,24},{20,28},{24,16},{28,20},{1,9},{5... | collective-permute-start | bytes 1511432 | tf_op jit(solution)/shard_map/ppermute | solution.py:438
  139.8 26.8 %collective-permute-start.41 = (bf16[3,656,128]{2,1,0:T(8,128)(2,1)}, bf16[3,656,128]{2,1,0:T(8,128)(2,1)S(1)}, u32[]{:S(2)}, u32[]{:S(2)}) collective-permute-start(bf16[3,656,128]{2,1,0:T(8,128)(2,1)} %collective-permute-done.27), channel_id=1, source_target_pairs={{0,4},{4,0},{8,12},{12,8},{16,20},{20,16},{24,28},{28,24},{1,5},{5... | collective-permute-start | bytes 1511432 | tf_op jit(solution)/shard_map/ppermute | solution.py:438
  140.0 26.7 %collective-permute-start.40 = (bf16[3,656,128]{2,1,0:T(8,128)(2,1)S(1)}, bf16[3,656,128]{2,1,0:T(8,128)(2,1)}, u32[]{:S(2)}, u32[]{:S(2)}) collective-permute-start(bf16[3,656,128]{2,1,0:T(8,128)(2,1)S(1)} %collective-permute-done.34), channel_id=1, source_target_pairs={{0,8},{4,12},{8,0},{12,4},{16,24},{20,28},{24,16},{28,20},{1,9},{5... | collective-permute-start | bytes 1511432 | tf_op jit(solution)/shard_map/ppermute | solution.py:438
  141.5 25.2 %collective-permute-start.42 = (bf16[3,656,128]{2,1,0:T(8,128)(2,1)S(1)}, bf16[3,656,128]{2,1,0:T(8,128)(2,1)S(1)}, u32[]{:S(2)}, u32[]{:S(2)}) collective-permute-start(bf16[3,656,128]{2,1,0:T(8,128)(2,1)S(1)} %collective-permute-done.32), channel_id=1, source_target_pairs={{0,4},{4,0},{8,12},{12,8},{16,20},{20,16},{24,28},{28,24},{1,5},{5... | collective-permute-start | bytes 1511432 | tf_op jit(solution)/shard_map/ppermute | solution.py:438
  141.6 25.1 %collective-permute-start.39 = (bf16[3,656,128]{2,1,0:T(8,128)(2,1)S(1)}, bf16[3,656,128]{2,1,0:T(8,128)(2,1)}, u32[]{:S(2)}, u32[]{:S(2)}) collective-permute-start(bf16[3,656,128]{2,1,0:T(8,128)(2,1)S(1)} %collective-permute-done.32), channel_id=1, source_target_pairs={{0,16},{4,20},{8,24},{12,28},{16,0},{20,4},{24,8},{28,12},{1,17},{... | collective-permute-start | bytes 1511432 | tf_op jit(solution)/shard_map/ppermute | solution.py:438
  182.6 27.9 %collective-permute-start.50 = (bf16[1,3,656,128]{3,2,1,0:T(8,128)(2,1)}, bf16[1,3,656,128]{3,2,1,0:T(8,128)(2,1)S(1)}, u32[]{:S(2)}, u32[]{:S(2)}) collective-permute-start(bf16[1,3,656,128]{3,2,1,0:T(8,128)(2,1)} %get-tuple-element.376), channel_id=1, source_target_pairs={{0,16},{4,20},{8,24},{12,28},{16,0},{20,4},{24,8},{28,12},{1,17},{... | collective-permute-start | bytes 1511432 | tf_op jit(solution)/shard_map/ppermute | solution.py:438
  183.6 26.8 %collective-permute-start.51 = (bf16[1,3,656,128]{3,2,1,0:T(8,128)(2,1)}, bf16[1,3,656,128]{3,2,1,0:T(8,128)(2,1)}, u32[]{:S(2)}, u32[]{:S(2)}) collective-permute-start(bf16[1,3,656,128]{3,2,1,0:T(8,128)(2,1)} %get-tuple-element.377), channel_id=1, source_target_pairs={{0,8},{4,12},{8,0},{12,4},{16,24},{20,28},{24,16},{28,20},{1,9},{5... | collective-permute-start | bytes 1511432 | tf_op jit(solution)/shard_map/ppermute | solution.py:438
  210.5 30.4 %collective-permute-start.54 = (bf16[4,2,3,656,128]{4,3,2,1,0:T(8,128)(2,1)}, bf16[4,2,3,656,128]{4,3,2,1,0:T(8,128)(2,1)}, u32[]{:S(2)}, u32[]{:S(2)}) collective-permute-start(bf16[4,2,3,656,128]{4,3,2,1,0:T(8,128)(2,1)} %get-tuple-element.405), channel_id=1, source_target_pairs={{0,4},{4,0},{8,12},{12,8},{16,20},{20,16},{24,28},{28,24},{1,5},{5... | collective-permute-start | bytes 12091400 | tf_op jit(solution)/shard_map/ppermute | solution.py:438
  214.7 24.9 %collective-permute-start.52 = (bf16[2,3,656,128]{3,2,1,0:T(8,128)(2,1)}, bf16[2,3,656,128]{3,2,1,0:T(8,128)(2,1)S(1)}, u32[]{:S(2)}, u32[]{:S(2)}) collective-permute-start(bf16[2,3,656,128]{3,2,1,0:T(8,128)(2,1)} %pad_maximum_fusion.2), channel_id=1, source_target_pairs={{0,8},{4,12},{8,0},{12,4},{16,24},{20,28},{24,16},{28,20},{1,9},{5... | collective-permute-start | bytes 3022856 | tf_op jit(solution)/shard_map/ppermute | solution.py:438
  216.2 24.6 %collective-permute-start.53 = (bf16[2,3,656,128]{3,2,1,0:T(8,128)(2,1)}, bf16[2,3,656,128]{3,2,1,0:T(8,128)(2,1)S(1)}, u32[]{:S(2)}, u32[]{:S(2)}) collective-permute-start(bf16[2,3,656,128]{3,2,1,0:T(8,128)(2,1)} %pad_maximum_fusion.3), channel_id=1, source_target_pairs={{0,16},{4,20},{8,24},{12,28},{16,0},{20,4},{24,8},{28,12},{1,17},{... | collective-permute-start | bytes 3022856 | tf_op jit(solution)/shard_map/ppermute | solution.py:438
  246.3 22.4 %collective-permute-start.55 = (bf16[1,3,656,128]{3,2,1,0:T(8,128)(2,1)}, bf16[1,3,656,128]{3,2,1,0:T(8,128)(2,1)S(1)}, u32[]{:S(2)}, u32[]{:S(2)}) collective-permute-start(bf16[1,3,656,128]{3,2,1,0:T(8,128)(2,1)} %get-tuple-element.417), channel_id=1, source_target_pairs={{0,16},{4,20},{8,24},{12,28},{16,0},{20,4},{24,8},{28,12},{1,17},{... | collective-permute-start | bytes 1511432 | tf_op jit(solution)/shard_map/ppermute | solution.py:438
  272.9 25.1 %collective-permute-start.58 = (bf16[2,3,656,128]{3,2,1,0:T(8,128)(2,1)}, bf16[2,3,656,128]{3,2,1,0:T(8,128)(2,1)S(1)}, u32[]{:S(2)}, u32[]{:S(2)}) collective-permute-start(bf16[2,3,656,128]{3,2,1,0:T(8,128)(2,1)} %pad_maximum_fusion.4), channel_id=1, source_target_pairs={{0,8},{4,12},{8,0},{12,4},{16,24},{20,28},{24,16},{28,20},{1,9},{5... | collective-permute-start | bytes 3022856 | tf_op jit(solution)/shard_map/ppermute | solution.py:438
  274.3 23.7 %collective-permute-start.59 = (bf16[2,3,656,128]{3,2,1,0:T(8,128)(2,1)}, bf16[2,3,656,128]{3,2,1,0:T(8,128)(2,1)S(1)}, u32[]{:S(2)}, u32[]{:S(2)}) collective-permute-start(bf16[2,3,656,128]{3,2,1,0:T(8,128)(2,1)} %pad_maximum_fusion.5), channel_id=1, source_target_pairs={{0,16},{4,20},{8,24},{12,28},{16,0},{20,4},{24,8},{28,12},{1,17},{... | collective-permute-start | bytes 3022856 | tf_op jit(solution)/shard_map/ppermute | solution.py:438
  300.9 26.2 %collective-permute-start.67 = (bf16[512,1024]{1,0:T(8,128)(2,1)}, bf16[512,1024]{1,0:T(8,128)(2,1)S(1)}, u32[]{:S(2)}, u32[]{:S(2)}) collective-permute-start(bf16[512,1024]{1,0:T(8,128)(2,1)} %get-tuple-element.452), channel_id=1, source_target_pairs={{0,1},{1,0},{2,3},{3,2},{4,5},{5,4},{6,7},{7,6},{8,9},{9,8},{10,11... | collective-permute-start | bytes 3145736 | tf_op jit(solution)/shard_map/ppermute | solution.py:761
  337.2 33.9 %collective-permute-start.69 = (bf16[4,4,128,256]{3,2,1,0:T(8,128)(2,1)}, bf16[4,4,128,256]{3,2,1,0:T(8,128)(2,1)S(1)}, u32[]{:S(2)}, u32[]{:S(2)}) collective-permute-start(bf16[4,4,128,256]{3,2,1,0:T(8,128)(2,1)} %pad_maximum_fusion), channel_id=1, source_target_pairs={{0,8},{4,12},{8,0},{12,4},{16,24},{20,28},{24,16},{28,20},{1,9},{5... | collective-permute-start | bytes 3145736 | tf_op jit(solution)/shard_map/ppermute | solution.py:438
  337.8 33.3 %collective-permute-start.70 = (bf16[4,4,128,256]{3,2,1,0:T(8,128)(2,1)S(1)}, bf16[4,4,128,256]{3,2,1,0:T(8,128)(2,1)S(1)}, u32[]{:S(2)}, u32[]{:S(2)}) collective-permute-start(bf16[4,4,128,256]{3,2,1,0:T(8,128)(2,1)S(1)} %pad_maximum_fusion.1), channel_id=1, source_target_pairs={{0,16},{4,20},{8,24},{12,28},{16,0},{20,4},{24,8},{28,12},{1,17},{... | collective-permute-start | bytes 3145736 | tf_op jit(solution)/shard_map/ppermute | solution.py:438
  (107 other events, 1463.2 us)

commit v4 on v3

--- a/solution.py
+++ b/solution.py
@@ -634,34 +634,32 @@
         line_1, mlp_x[0], mlp_y[0] = together((line_1, mlp_x[0], mlp_y[0]))
         pair_a = jnp.stack([attn_weight, line_1])
         x_a, y_a = swap_dp(pair_a, 2, owners), swap_dp(pair_a, 4, owners)
-        line_2, line_3 = along_line(line_1, 1, shards), along_line(after(attn_weight, line_1), 3, shards)
-        mlp_z[0] = swap_dp(mlp_y[0], 2, owners)
-        x_a, y_a, line_2, line_3, tables = together((x_a, y_a, line_2, line_3, tables))
+        far_rows = from_peer(after(hidden_in, line_1), 1)
+        core_0 = to_core([after(a, line_1) for a in (mlp_turned, mlp_x[0])], owners)
+        x_a, y_a, core_0, tables = together((x_a, y_a, core_0, tables))
         cos_table, sin_table, key_seg, query_seg, keep_own, attn_perm, mlp_perm, slots, first_gain, second_gain = tables
-        z_a = swap_dp(x_a, 4, owners)
-        far_rows = from_peer(after(hidden_in, line_2), 1)
-        core_own_a, core_x_a, core_y_a = to_core([after(pair_a, line_2), x_a, y_a], owners)
-        mlp_line = [mlp_turned, along_line(after(mlp_turned, core_x_a), 1, shards), None, None]
+        z_a, mlp_z[0] = swap_dp(x_a, 4, owners), swap_dp(after(mlp_y[0], y_a), 2, owners)
+        line_2, line_3 = along_line(after(line_1, x_a), 1, shards), along_line(after(attn_weight, x_a), 3, shards)
+        normal = norm_first(hidden_in, far_rows, first_gain)
+        z_a, mlp_z[0], normal, line_2, line_3 = together((z_a, mlp_z[0], tuple(normal), line_2, line_3))
         pair_b = jnp.stack([line_2, line_3])
-        z_a, mlp_z[0], core_own_a, core_x_a, core_y_a, pair_b = together((z_a, mlp_z[0], core_own_a, core_x_a, core_y_a, pair_b))
         x_b, y_b = swap_dp(pair_b, 2, owners), swap_dp(pair_b, 4, owners)
-        core_z_a, core_own_b = to_core([z_a, pair_b], owners)
-        normal = norm_first(hidden_in, far_rows, first_gain)
-        x_b, y_b, core_z_a, core_own_b, normal, mlp_line[1] = together((x_b, y_b, core_z_a, core_own_b, tuple(normal), mlp_line[1]))
+        mlp_line = [mlp_turned, along_line(after(mlp_turned, line_3), 1, shards), None, None]
+        core_a4 = to_core([after(a, z_a) for a in (pair_a, x_a, y_a, z_a)], owners)
+        core_b = [swap_dp(after(pair_b, core_a4[1]), 1, owners)]
+        normal, core_a4, mlp_line[1], core_b, x_b, y_b = together((tuple(normal), core_a4, mlp_line[1], core_b, x_b, y_b))
         z_b = swap_dp(y_b, 2, owners)
-        core_x_b, core_y_b = to_core([x_b, y_b], owners)
-        core_0 = to_core([after(a, y_b) for a in (mlp_turned, mlp_x[0], mlp_y[0], mlp_z[0])], owners)
-        normal, mlp_line[1], core_x_b, core_y_b, core_0 = together((normal, mlp_line[1], core_x_b, core_y_b, core_0))
+        mlp_x[1], mlp_y[1] = swap_dp(mlp_line[1], 2, owners), swap_dp(mlp_line[1], 4, owners)
+        mlp_line[3] = along_line(after(mlp_turned, mlp_line[1]), 3, shards)
+        mlp_line[2] = along_line(mlp_line[1], 1, shards)
         first_norm, first_turned, xhat_low = normal
 
         def attn_set(arrays, first):
             return arrays, tuple((r, first, 2, shards) for r in (0, 2, 4, 6, 1, 3, 5, 7))
 
         sizes = (shards, slab, attn_weight.shape[2])
-        arrays_a, metas_a = attn_set([pair_a, x_a, y_a, z_a, core_own_a, core_x_a, core_y_a, core_z_a], 0)
+        arrays_a, metas_a = attn_set([pair_a, x_a, y_a, z_a, *core_a4], 0)
         attn_part_a = (arrays_a, metas_a, *sizes)
-        mlp_x[1], mlp_y[1] = swap_dp(mlp_line[1], 2, owners), swap_dp(mlp_line[1], 4, owners)
-        mlp_line[2], mlp_line[3] = along_line(mlp_line[1], 1, shards), along_line(after(mlp_turned, mlp_line[1]), 3, shards)
     else:
         far_rows = [from_peer(hidden_in, d) for d in range(1, span)]
         attn_pieces = ([attn_all], (None,), shards, slab, attn_weight.shape[2])
@@ -670,21 +668,20 @@
     fwd_args = (attn_perm, first_norm, hidden_in, second_gain, cos_table, sin_table, key_seg, query_seg, keep_own)
     if fast:
         carry = fwd_attn(*fwd_args, attn_part_a, S0=0, N=half)
-        z_b, mlp_x[1], mlp_y[1], mlp_line[2], mlp_line[3], carry = together(
-            (z_b, mlp_x[1], mlp_y[1], mlp_line[2], mlp_line[3], tuple(carry))
+        z_b, mlp_x[1], mlp_y[1], mlp_line[3], mlp_line[2], carry = together(
+            (z_b, mlp_x[1], mlp_y[1], mlp_line[3], mlp_line[2], tuple(carry))
         )
+        core_b = core_b + to_core([after(x_b, z_b), after(y_b, z_b)], owners)
         core_z_b = swap_dp(z_b, 1, owners)
-        core_z_b, mlp_x[1], mlp_y[1], mlp_line[2], mlp_line[3] = together((core_z_b, mlp_x[1], mlp_y[1], mlp_line[2], mlp_line[3]))
-        arrays_b, metas_b = attn_set([pair_b, x_b, y_b, z_b, core_own_b, core_x_b, core_y_b, core_z_b], 2)
+        core_b, core_z_b, mlp_x[1], mlp_y[1], mlp_line[3], mlp_line[2] = together((core_b, core_z_b, mlp_x[1], mlp_y[1], mlp_line[3], mlp_line[2]))
+        mlp_z[1] = swap_dp(mlp_y[1], 2, owners)
+        mlp_y[2] = swap_dp(mlp_line[2], 4, owners)
+        arrays_b, metas_b = attn_set([pair_b, x_b, y_b, z_b, *core_b, core_z_b], 2)
         attn_part_b = (arrays_b, metas_b, *sizes)
         attn_pieces = (arrays_a + arrays_b, metas_a + metas_b, *sizes)
-        mlp_z[1] = swap_dp(mlp_y[1], 2, owners)
-        mlp_x[2], mlp_y[2] = swap_dp(mlp_line[2], 2, owners), swap_dp(mlp_line[2], 4, owners)
         mlp_x[3], mlp_y[3] = swap_dp(mlp_line[3], 2, owners), swap_dp(mlp_line[3], 4, owners)
         out = fwd_attn(*fwd_args, attn_part_b, S0=half, N=half, carry=carry)
-        mlp_z[1], mlp_x[2], mlp_y[2], mlp_y[3], mlp_x[0], mlp_x[1], out = together(
-            (mlp_z[1], mlp_x[2], mlp_y[2], mlp_y[3], mlp_x[0], mlp_x[1], tuple(out))
-        )
+        mlp_x[3], mlp_y[3], mlp_z[1], mlp_y[2], out = together((mlp_x[3], mlp_y[3], mlp_z[1], mlp_y[2], tuple(out)))
         queries, keys, values, attended, log_sums, resid, second_norm, stat_a = out
 
         def mlp_set(slot):
@@ -698,18 +695,19 @@
             return arrays, tuple(metas), shards, slab, hid_cols
 
         set_0, set_1 = mlp_set(0), mlp_set(1)
-        set_1 = [after(a, mlp_z[1]) for a in set_1]
-        core_1 = to_core(set_1, owners)
-        core_1, second_norm, mlp_x[2], mlp_y[3] = together((core_1, second_norm, mlp_x[2], mlp_y[3]))
-        mlp_z[2], mlp_z[3] = swap_dp(mlp_x[2], 4, owners), swap_dp(mlp_y[3], 2, owners)
-        core_2 = to_core([after(mlp_line[2], second_norm), mlp_x[2]], owners)
+        core_1 = to_core([after(a, mlp_z[1]) for a in set_1], owners)
+        core_0 = core_0 + to_core([after(a, core_1[1]) for a in (mlp_y[0], mlp_z[0])], owners)
+        core_1, core_0, second_norm, mlp_x[3], mlp_y[2] = together((core_1, core_0, second_norm, mlp_x[3], mlp_y[2]))
+        mlp_z[3], mlp_z[2] = swap_dp(mlp_x[3], 4, owners), swap_dp(mlp_y[2], 2, owners)
+        mlp_x[2] = swap_dp(after(mlp_line[2], second_norm), 2, owners)
+        core_3 = to_core([mlp_line[3], mlp_x[3]], owners)
         mlp_args = (mlp_perm, slots, second_norm, out_grad, resid, second_gain, keep_own)
         out = mlp(*mlp_args, mlp_pieces((0, set_0 + core_0), (1, set_1 + core_1)), S0=0, N=half)
-        mlp_x[3], mlp_z[2], mlp_z[3], core_2, out = together((mlp_x[3], mlp_z[2], mlp_z[3], core_2, tuple(out)))
+        mlp_x[2], mlp_z[2], mlp_z[3], core_3, out = together((mlp_x[2], mlp_z[2], mlp_z[3], core_3, tuple(out)))
         *carry, even_a, odd_a = out
         set_2, set_3 = mlp_set(2), mlp_set(3)
-        set_2, set_3 = [after(a, odd_a) for a in set_2], [after(a, odd_a) for a in set_3]
-        core_2, core_3 = core_2 + to_core(set_2[2:], owners), to_core(set_3, owners)
+        core_2 = to_core([after(a, odd_a) for a in set_2], owners)
+        core_3 = core_3 + to_core([after(a, odd_a) for a in set_3[2:]], owners)
         core_a = swap_dp(odd_a, 1, owners)
         low, high = cross_sends(even_a, core_a, 1)
         low, high, core_2, core_3, carry = lax.optimization_barrier((low, high, core_2, core_3, carry))
@@ -717,21 +715,21 @@
         out = mlp(*mlp_args, mlp_pieces((2, set_2 + core_2), (3, set_3 + core_3)), S0=half, N=half, carry=carry)
         from_y, from_x, *out = lax.optimization_barrier((from_y, from_x, *out))
         output, dresid, dres_low, dres_turned, gain_two, stat_m, even_b, odd_b = out
-        core_b = swap_dp(odd_b, 1, owners)
+        core_b2 = swap_dp(odd_b, 1, owners)
         to_x, to_y = side_sends(even_a, core_a, from_y, from_x, 1)
         to_x, to_y, dres_low = lax.optimization_barrier((to_x, to_y, dres_low))
         back_x, back_y = swap_dp(to_x, 2, owners), swap_dp(to_y, 4, owners)
         fwd_kept = (queries, keys, values, log_sums, attn_pieces)
         grads = bwd_attn(attn_perm, dres_low, *back_args, *fwd_kept, S0=0, N=half)
-        back_x, back_y, core_b, *grads = lax.optimization_barrier((back_x, back_y, core_b, *grads))
-        low, high = cross_sends(even_b, core_b, 1)
+        back_x, back_y, core_b2, *grads = lax.optimization_barrier((back_x, back_y, core_b2, *grads))
+        low, high = cross_sends(even_b, core_b2, 1)
         ring_1 = own_part(even_a, core_a, back_x, back_y, 1).astype(BF)
         low, high, ring_1, dres_low = lax.optimization_barrier((low, high, ring_1, dres_low))
         from_y, from_x = swap_dp(low, 4, owners), swap_dp(high, 2, owners)
         ring_1 = to_ring_succ(ring_1, shards)
         grads = bwd_attn(attn_perm, dres_low, *back_args, *fwd_kept, S0=half, N=half, carry=tuple(grads))
         from_y, from_x, ring_1, *grads = lax.optimization_barrier((from_y, from_x, ring_1, *grads))
-        to_x, to_y = side_sends(even_b, core_b, from_y, from_x, 1)
+        to_x, to_y = side_sends(even_b, core_b2, from_y, from_x, 1)
         to_x, to_y, dres_turned = lax.optimization_barrier((to_x, to_y, dres_turned))
         from_x, from_y = swap_dp(to_x, 2, owners), swap_dp(to_y, 4, owners)
         out = grad_attn(attn_perm, slots, first_turned, dres_turned, xhat_low, attended, *grads, attn_pieces)
@@ -785,20 +783,22 @@
     small = jnp.concatenate([gain_one, gain_two, jnp.pad(sums, (0, width - 5))[None]], axis=0)
     if fast:
         attn_core = swap_dp(attn_odd, 1, owners)
-        ring_2 = (own_part(even_b, core_b, from_x, from_y, 0) + ring_1.astype(F32)).astype(BF)
+        ring_2 = (own_part(even_b, core_b2, from_x, from_y, 0) + ring_1.astype(F32)).astype(BF)
         ring_2 = to_ring_succ(ring_2, shards)
         small = small + swap_dp(small, 1, owners)
         small, attn_core = lax.optimization_barrier((small, attn_core))
         low, high = cross_sends(attn_even, attn_core, half)
+        low, high, small = lax.optimization_barrier((low, high, small))
         cross_y, cross_x = swap_dp(low, 4, owners), swap_dp(high, 2, owners)
-        da_back = send_back(da_far)
-        small = (small + swap_dp(small, 2, owners)) + (swap_dp(small, 4, owners) + swap_dp(small, 6, owners))
-        small, cross_x, cross_y, da_back = lax.optimization_barrier((small, cross_x, cross_y, da_back))
+        small = small + swap_dp(small, 2, owners)
+        ring_3 = (own_part(even_b, core_b2, from_x, from_y, 1) + ring_2.astype(F32)).astype(BF)
+        ring_3 = to_ring_succ(ring_3, shards)
+        small, cross_x, cross_y = lax.optimization_barrier((small, cross_x, cross_y))
         to_x, to_y = side_sends(attn_even, attn_core, cross_y, cross_x, half)
-        to_x, to_y, small, ring_2 = lax.optimization_barrier((to_x, to_y, small, ring_2))
+        to_x, to_y, small, ring_3 = lax.optimization_barrier((to_x, to_y, small, ring_3))
         attn_x, attn_y = swap_dp(to_x, 2, owners), swap_dp(to_y, 4, owners)
-        ring_3 = (own_part(even_b, core_b, from_x, from_y, 1) + ring_2.astype(F32)).astype(BF)
-        ring_3 = to_ring_succ(ring_3, shards)
+        small = small + swap_dp(small, 4, owners)
+        da_back = send_back(after(da_far, ring_3))
         mlp_sum = own_part(even_a, core_a, back_x, back_y, 0) + ring_3.astype(F32)
         mlp_new = soap_mlp(mlp_sum)
         attn_x, attn_y, mlp_sum, mlp_new = lax.optimization_barrier((attn_x, attn_y, mlp_sum, tuple(mlp_new)))

time: 418 us -> 402 us (0.962)
  waiting for transfers between devices: 97.5 us -> 85 us
    ppermute x1, waiting for transfers between devices: 5.01 us -> 15.4 us  [from_peer(): return lax.ppermute(value, 'tensor', pairs)]
    ppermute x1, waiting for transfers between devices: 9.52 us -> 0.01 us  [send_back(): got.append(lax.ppermute(da_far[(d - 1) * rows:d * rows], 'tensor', pairs))]
    ppermute x6, waiting for transfers between devices: 18.5 us -> 12.3 us  [to_ring_succ(): lax.ppermute(value, 'tensor', [(ring[p], ring[(p + 1) % shards]) for p in...]
    ppermute x61 -> x60, waiting for transfers between devices: 40.8 us -> 37.6 us  [swap_dp(): return lax.ppermute(value, 'dp', [(i, i ^ bit) for i in range(owners)])]
    ppermute x61 -> x60, starting transfers between devices: 42.1 us -> 40.6 us  [swap_dp(): return lax.ppermute(value, 'dp', [(i, i ^ bit) for i in range(owners)])]
  transfers between devices with their start and end apart: 77 -> 76, of which waited for: 26 -> 29; matrix products, arithmetic and copies ran while one was open for 9% -> 9% of each run, Pallas kernels for 42% -> 44%
where the time goes in v4:
time: 402 us; the launch traced here: 395 us
  Pallas kernels  181 us (45%)
  waiting for transfers between devices  85 us (21%)
  starting transfers between devices  67.3 us (17%)
  other arithmetic  48.8 us (12%)
  local copies, waits for them, and re-layouts  8.32 us (2%)
  between operations  5.02 us (1%)
    pallas_call x2, Pallas kernels, mlp(): pl.pallas_call(functools.partial(mlp_kernel, T=T, D=D, HC=HC, R=R, metas=...  50.7 us
    ppermute x60, starting transfers between devices, swap_dp(): return lax.ppermute(value, 'dp', [(i, i ^ bit) for i in range(owners)])  40.6 us
    pallas_call x2, Pallas kernels, bwd_attn(): pl.pallas_call(functools.partial(bwd_attn_kernel, T=T, KV=KV, C=C, metas=...  37.9 us
    ppermute x60, waiting for transfers between devices, swap_dp(): return lax.ppermute(value, 'dp', [(i, i ^ bit) for i in range(owners)])  37.6 us
    pallas_call x2, Pallas kernels, fwd_attn(): pl.pallas_call(functools.partial(fwd_attn_kernel, T=T, KV=KV, C=C, metas=...  36.5 us
    pallas_call x1, Pallas kernels, grad_attn(): pl.pallas_call(functools.partial(grad_attn_kernel, T=T, KV=KV, C=C, R=R,...  22.9 us
    pallas_call x2, Pallas kernels, soap(): pl.pallas_call(functools.partial(soap_kernel, turned=turned), grid_spec=g...  21.6 us
    ppermute x1, waiting for transfers between devices, from_peer(): return lax.ppermute(value, 'tensor', pairs)  15.4 us
  transfers between devices with their start and end apart: 76, of which 29 were waited for; matrix products, arithmetic and copies ran while one was open for 9% of the time, Pallas kernels for 44%

profile of v4, /device:TPU:0, one launch (start us, length us, event | category | flops | bytes accessed | tf_op | source)
XLA Modules:
  0.0 395.1 jit_solution(251923247206837440)
XLA Ops:
  0.7 3.0 collective-permute-start.2
  24.7 5.8 %collective-permute-done.4.rest_2_ = bf16[2,4,128,256]{3,2,1,0:T(8,128)(2,1)S(1)} collective-permute-done((bf16[2,4,128,256]{3,2,1,0:T(8,128)(2,1)S(1)}, bf16[2,4,128,256]{3,2,1,0:T(8,128)(2,1)S(1)}, u32[]{:S(2)}, u32[]{:S(2)}) %collective-permute-start.4) | collective-permute-done | bytes 524320 | tf_op jit(solution)/shard_map/ppermute | solution.py:438
  36.9 15.4 %collective-permute-done.9.far = bf16[512,1024]{1,0:T(8,128)(2,1)} collective-permute-done((bf16[512,1024]{1,0:T(8,128)(2,1)S(1)}, bf16[512,1024]{1,0:T(8,128)(2,1)}, u32[]{:S(2)}, u32[]{:S(2)}) %collective-permute-start.9) | collective-permute-done | bytes 1048608 | tf_op jit(solution)/shard_map/ppermute | solution.py:578
  52.3 5.8 %norm_first.1 = (bf16[1024,1024]{1,0:T(8,128)(2,1)}, bf16[1024,1024]{1,0:T(8,128)(2,1)}, bf16[1024,1024]{1,0:T(8,128)(2,1)}) custom-call(bf16[512,1024]{1,0:T(8,128)(2,1)} %hid.5, bf16[512,1024]{1,0:T(8,128)(2,1)} %collective-permute-done.9.far, f32[1,1024]{1,0:T(1,128)} %get-tuple-element.273.gain), custom_call_target="tpu_custom_call" | custom-call | flops 1 | bytes 1 | tf_op jit(solution)/shard_map/norm_first/pallas_call | solution.py:410
  63.7 11.2 %collective-permute-done.16 = bf16[3,656,128]{2,1,0:T(8,128)(2,1)} collective-permute-done((bf16[3,656,128]{2,1,0:T(8,128)(2,1)}, bf16[3,656,128]{2,1,0:T(8,128)(2,1)}, u32[]{:S(2)}, u32[]{:S(2)}) %collective-permute-start.16) | collective-permute-done | bytes 503840 | tf_op jit(solution)/shard_map/ppermute | solution.py:457
  84.2 16.7 %attn_fwd.2 = (bf16[4,512,256]{2,1,0:T(8,128)(2,1)}, bf16[4,1024,256]{2,1,0:T(8,128)(2,1)}, bf16[4,1024,256]{2,1,0:T(8,128)(2,1)}, bf16[4,512,256]{2,1,0:T(8,128...) custom-call(s32[16]{0:T(128)} %pad_add_fusion.1.perm, bf16[1024,1024]{1,0:T(8,128)(2,1)} %get-tuple-element.297.a1, ...), custom_call_target="tpu_custom_call" | custom-call | flops 1 | bytes 1 | tf_op jit(solution)/shard_map/attn_fwd/pallas_call | solution.py:134
  111.1 19.8 %attn_fwd.3 = (bf16[4,512,256]{2,1,0:T(8,128)(2,1)}, bf16[4,1024,256]{2,1,0:T(8,128)(2,1)}, bf16[4,1024,256]{2,1,0:T(8,128)(2,1)}, bf16[4,512,256]{2,1,0:T(8,128...) custom-call(s32[16]{0:T(128)} %pad_add_fusion.1.perm, ...), custom_call_target="tpu_custom_call", output_to_operand_aliasing={{0}: (18, {}), {1}: (19, {}), {2}: (20, {}), {3}: (21, {}),... | custom-call | flops 1 | bytes 1 | tf_op jit(solution)/shard_map/attn_fwd/pallas_call | solution.py:134
  141.1 24.5 %mlp_both.2 = (f32[512,1024]{1,0:T(8,128)}, f32[512,1024]{1,0:T(8,128)}, bf16[4,2,3,656,128]{4,3,2,1,0:T(8,128)(2,1)}, bf16[4,2,3,656,128]{4,3,2,1,0:T(8,128)(2,1)}) custom-call(s32[16]{0:T(128)} %pad_add_fusion.1.perm, s32[4]{0:T(128)} %iota.18.slots, bf16[512,1024]{1,0:T(8,128)(2,1)} %get-tuple-element.356.a2, bf16[512,1024]{1,0:T(8,128)(2,1)} %g.3, ...), custom_call_target="tpu_custom_call" | custom-call | flops 1 | bytes 1 | tf_op jit(solution)/shard_map/mlp_both/pallas_call | solution.py:232
  166.9 8.0 %collective-permute-done.44 = bf16[3,656,128]{2,1,0:T(8,128)(2,1)S(1)} collective-permute-done((bf16[3,656,128]{2,1,0:T(8,128)(2,1)}, bf16[3,656,128]{2,1,0:T(8,128)(2,1)S(1)}, u32[]{:S(2)}, u32[]{:S(2)}) %collective-permute-start.44) | collective-permute-done | bytes 503840 | tf_op jit(solution)/shard_map/ppermute | solution.py:438
  177.1 3.1 fusion.25
  183.2 26.3 %mlp_both.3 = (bf16[512,1024]{1,0:T(8,128)(2,1)}, f32[512,1024]{1,0:T(8,128)}, bf16[512,1024]{1,0:T(8,128)(2,1)}, bf16[1024,512]{1,0:T(8,128)(2,1)}, f32[1,1024]...) custom-call(s32[16]{0:T(128)} %pad_add_fusion.1.perm, ...), custom_call_target="tpu_custom_call" | custom-call | flops 1 | bytes 1 | tf_op jit(solution)/shard_map/mlp_both/pallas_call | solution.py:232
  215.5 18.9 %attn_bwd.2 = (bf16[4,512,256]{2,1,0:T(8,128)(2,1)}, bf16[4,1024,256]{2,1,0:T(8,128)(2,1)}, bf16[4,1024,256]{2,1,0:T(8,128)(2,1)}) custom-call(s32[16]{0:T(128)} %pad_add_fusion.1.perm, bf16[512,1024]{1,0:T(8,128)(2,1)} %get-tuple-element.433.dres, f32[1024,128]{1,0:T(8,128)} %get-tuple-element.299.cos, f32[1024,128]{1,0:T(8,128)} %get-tuple-element.300.sin, ...), custom_call_target="tpu_custom_call" | custom-call | flops 1 | bytes 1 | tf_op jit(solution)/shard_map/attn_bwd/pallas_call | solution.py:290
  234.5 4.0 %collective-permute-done.52 = bf16[2,3,656,128]{3,2,1,0:T(8,128)(2,1)S(1)} collective-permute-done((bf16[2,3,656,128]{3,2,1,0:T(8,128)(2,1)}, bf16[2,3,656,128]{3,2,1,0:T(8,128)(2,1)S(1)}, u32[]{:S(2)}, u32[]{:S(2)}) %collective-permute-start.52) | collective-permute-done | bytes 1007648 | tf_op jit(solution)/shard_map/ppermute | solution.py:438
  239.6 4.0 %fusion.29 = (bf16[1,3,656,128]{3,2,1,0:T(8,128)(2,1)S(1)}, bf16[1,3,656,128]{3,2,1,0:T(8,128)(2,1)S(1)}, bf16[1,3,656,128]{3,2,1,0:T(8,128)(2,1)}, bf16[1,3,656,128]{3,2,1,0:T(8,128)(2,1)}) fusion(bf16[4,2,3,656,128]{4,3,2,1,0:T(8,128)(2,1)} %collective-permute-done.54, bf16[4,2,3,656,128]{4,3,2,1,0:T(8,128)(2,1)} %get-tuple-element.412), kind=kLoop, calls=%fused_computation.75 | loop fusion | flops 4030464 | bytes 6045696 | tf_op jit(solution)/shard_map/add | solution.py:508
  248.8 19.0 %attn_bwd.3 = (bf16[4,512,256]{2,1,0:T(8,128)(2,1)}, bf16[4,1024,256]{2,1,0:T(8,128)(2,1)}, bf16[4,1024,256]{2,1,0:T(8,128)(2,1)}) custom-call(s32[16]{0:T(128)} %pad_add_fusion.1.perm, bf16[512,1024]{1,0:T(8,128)(2,1)} %get-tuple-element.433.dres, ...), custom_call_target="tpu_custom_call", output_to_operand_aliasing={{0}: (26, {}), {1}: (27, {}), {2}: (28, {})} | custom-call | flops 1 | bytes 1 | tf_op jit(solution)/shard_map/attn_bwd/pallas_call | solution.py:290
  274.1 22.9 %attn_grad.1 = (f32[512,1024]{1,0:T(8,128)}, bf16[512,1024]{1,0:T(8,128)(2,1)}, f32[1,1024]{1,0:T(1,128)}, bf16[4,4,4,128,256]{4,3,2,1,0:T(8,128)(2,1)}, bf16[4,4,4,128,256]{4,3,2,1,0:T(8,128)(2,1)}) custom-call(s32[16]{0:T(128)} %pad_add_fusion.1.perm, s32[4]{0:T(128)} %iota.18.slots, bf16[1024,1024]{1,0:T(8,128)(2,1)} %get-tuple-element.445.a1T, ...), custom_call_target="tpu_custom_call" | custom-call | flops 1 | bytes 1 | tf_op jit(solution)/shard_map/attn_grad/pallas_call | solution.py:346
  310.5 4.4 %collective-permute-done.65 = bf16[3,656,128]{2,1,0:T(8,128)(2,1)S(1)} collective-permute-done((bf16[3,656,128]{2,1,0:T(8,128)(2,1)S(1)}, bf16[3,656,128]{2,1,0:T(8,128)(2,1)S(1)}, u32[]{:S(2)}, u32[]{:S(2)}) %collective-permute-start.65) | collective-permute-done | bytes 503840 | tf_op jit(solution)/shard_map/ppermute | solution.py:450
  319.2 3.1 collective-permute-done.62
  339.5 14.6 %soap_mlp.1 = (f32[3,656,128]{2,1,0:T(8,128)}, f32[3,656,128]{2,1,0:T(8,128)}, f32[3,656,128]{2,1,0:T(8,128)}, f32[3,8,128]{2,1,0:T(8,128)}) custom-call(f32[3]{0:T(128)} %pad_maximum_fusion.11.sc, f32[3,656,128]{2,1,0:T(8,128)} %fusion.2.g_in, f32[3,656,128]{2,1,0:T(8,128)} %bitcast.173, f32[3,656,128]{2,1,0:T(8,128)} %bitcast.174, f32[3,128,128]{2,1,0:T(8,128)} %left.2, ...), custom_call_target="tpu_custom_call" | custom-call | flops 1 | bytes 1 | tf_op jit(solution)/shard_map/soap_mlp/pallas_call | solution.py:390
  355.3 3.4 collective-permute-start.71
  358.7 5.2 %input_back.1 = bf16[512,1024]{1,0:T(8,128)(2,1)} custom-call(bf16[512,1024]{1,0:T(8,128)(2,1)} %hid.5, f32[512,1024]{1,0:T(8,128)} %get-tuple-element.487.da, f32[512,1024]{1,0:T(8,128)} %get-tuple-element.488.dres, f32[1,1024]{1,0:T(1,128)} %get-tuple-element.273.gain, bf16[512,1024]{1,0:T(8,128)(2,1)} %copy-done.16), custom_call_target="tpu_custom_call" | custom-call | flops 1 | bytes 1 | tf_op jit(solution)/shard_map/input_back/pallas_call | solution.py:428
  368.4 6.1 %collective-permute-done.74 = f32[3,1024]{1,0:T(4,128)S(1)} collective-permute-done((f32[3,1024]{1,0:T(4,128)S(1)}, f32[3,1024]{1,0:T(4,128)S(1)}, u32[]{:S(2)}, u32[]{:S(2)}) %collective-permute-start.74) | collective-permute-done | bytes 12320 | tf_op jit(solution)/shard_map/ppermute | solution.py:763
  377.1 5.1 %collective-permute-done.75 = bf16[4,128,256]{2,1,0:T(8,128)(2,1)S(1)} collective-permute-done((bf16[4,128,256]{2,1,0:T(8,128)(2,1)S(1)}, bf16[4,128,256]{2,1,0:T(8,128)(2,1)S(1)}, u32[]{:S(2)}, u32[]{:S(2)}) %collective-permute-start.75) | collective-permute-done | bytes 262176 | tf_op jit(solution)/shard_map/ppermute | solution.py:450
  385.9 7.0 %soap_attn.1 = (f32[4,128,256]{2,1,0:T(8,128)}, f32[4,128,256]{2,1,0:T(8,128)}, f32[4,128,256]{2,1,0:T(8,128)}, f32[4,8,128]{2,1,0:T(8,128)}) custom-call(f32[3]{0:T(128)} %pad_maximum_fusion.11.sc, f32[4,128,256]{2,1,0:T(8,128)} %fusion.16.g_in, f32[4,128,256]{2,1,0:T(8,128)} %first.1, f32[4,128,256]{2,1,0:T(8,128)} %second.1, f32[4,128,128]{2,1,0:T(8,128)} %left.3, ...), custom_call_target="tpu_custom_call" | custom-call | flops 1 | bytes 1 | tf_op jit(solution)/shard_map/soap_attn/pallas_call | solution.py:390
  (295 shorter events, 132.9 us)
Async XLA Ops:
  20.6 31.8 %collective-permute-start.9 = (bf16[512,1024]{1,0:T(8,128)(2,1)S(1)}, bf16[512,1024]{1,0:T(8,128)(2,1)}, u32[]{:S(2)}, u32[]{:S(2)}) collective-permute-start(bf16[512,1024]{1,0:T(8,128)(2,1)S(1)} %copy-done), channel_id=1, source_target_pairs={{1,0},{0,1},{3,2},{2,3},{5,4},{4,5},{7,6},{6,7},{9,8},{8,9},{11,10... | collective-permute-start | bytes 3145736 | tf_op jit(solution)/shard_map/ppermute | solution.py:578
  31.6 26.6 %collective-permute-start.7 = (bf16[2,4,128,256]{3,2,1,0:T(8,128)(2,1)S(1)}, bf16[2,4,128,256]{3,2,1,0:T(8,128)(2,1)S(1)}, u32[]{:S(2)}, u32[]{:S(2)}) collective-permute-start(bf16[2,4,128,256]{3,2,1,0:T(8,128)(2,1)S(1)} %collective-permute-done.3.rest_1_), channel_id=1, source_target_pairs={{0,16},{4,20},{8,24},{12,28},{16,0},{20,4},{24,8},{28,12},{1,17},{... | collective-permute-start | bytes 1572872 | tf_op jit(solution)/shard_map/ppermute | solution.py:438
  32.8 25.3 %collective-permute-start.8 = (bf16[3,656,128]{2,1,0:T(8,128)(2,1)}, bf16[3,656,128]{2,1,0:T(8,128)(2,1)}, u32[]{:S(2)}, u32[]{:S(2)}) collective-permute-start(bf16[3,656,128]{2,1,0:T(8,128)(2,1)} %copy-done.19), channel_id=1, source_target_pairs={{0,8},{4,12},{8,0},{12,4},{16,24},{20,28},{24,16},{28,20},{1,9},{5... | collective-permute-start | bytes 1511432 | tf_op jit(solution)/shard_map/ppermute | solution.py:438
  34.3 23.8 %collective-permute-start.10 = (bf16[4,128,256]{2,1,0:T(8,128)(2,1)}, bf16[4,128,256]{2,1,0:T(8,128)(2,1)}, u32[]{:S(2)}, u32[]{:S(2)}) collective-permute-start(bf16[4,128,256]{2,1,0:T(8,128)(2,1)} %collective-permute-done), channel_id=1, source_target_pairs={{0,2},{2,3},{3,1},{1,0},{4,6},{6,7},{7,5},{5,4},{8,10},{10,11},{11... | collective-permute-start | bytes 786440 | tf_op jit(solution)/shard_map/ppermute | solution.py:457
  77.5 25.8 %collective-permute-start.20 = (bf16[2,4,128,256]{3,2,1,0:T(8,128)(2,1)}, bf16[2,4,128,256]{3,2,1,0:T(8,128)(2,1)}, u32[]{:S(2)}, u32[]{:S(2)}) collective-permute-start(bf16[2,4,128,256]{3,2,1,0:T(8,128)(2,1)} %collective-permute-done.19.rest_2_.rest_10_), channel_id=1, source_target_pairs={{0,8},{4,12},{8,0},{12,4},{16,24},{20,28},{24,16},{28,20},{1,9},{5... | collective-permute-start | bytes 1572872 | tf_op jit(solution)/shard_map/ppermute | solution.py:438
  78.1 22.8 %collective-permute-start.23 = (bf16[3,656,128]{2,1,0:T(8,128)(2,1)}, bf16[3,656,128]{2,1,0:T(8,128)(2,1)}, u32[]{:S(2)}, u32[]{:S(2)}) collective-permute-start(bf16[3,656,128]{2,1,0:T(8,128)(2,1)} %bitcast.1), channel_id=1, source_target_pairs={{0,1},{2,0},{3,2},{1,3},{4,5},{6,4},{7,6},{5,7},{8,9},{10,8},{11,1... | collective-permute-start | bytes 1511432 | tf_op jit(solution)/shard_map/ppermute | solution.py:457
  80.5 22.8 %collective-permute-start.24 = (bf16[3,656,128]{2,1,0:T(8,128)(2,1)}, bf16[3,656,128]{2,1,0:T(8,128)(2,1)}, u32[]{:S(2)}, u32[]{:S(2)}) collective-permute-start(bf16[3,656,128]{2,1,0:T(8,128)(2,1)} %collective-permute-done.16), channel_id=1, source_target_pairs={{0,2},{2,3},{3,1},{1,0},{4,6},{6,7},{7,5},{5,4},{8,10},{10,11},{11... | collective-permute-start | bytes 1511432 | tf_op jit(solution)/shard_map/ppermute | solution.py:457
  107.0 23.9 %collective-permute-start.30 = (bf16[3,656,128]{2,1,0:T(8,128)(2,1)}, bf16[3,656,128]{2,1,0:T(8,128)(2,1)}, u32[]{:S(2)}, u32[]{:S(2)}) collective-permute-start(bf16[3,656,128]{2,1,0:T(8,128)(2,1)} %collective-permute-done.22), channel_id=1, source_target_pairs={{0,8},{4,12},{8,0},{12,4},{16,24},{20,28},{24,16},{28,20},{1,9},{5... | collective-permute-start | bytes 1511432 | tf_op jit(solution)/shard_map/ppermute | solution.py:438
  109.0 23.7 %collective-permute-start.29 = (bf16[3,656,128]{2,1,0:T(8,128)(2,1)}, bf16[3,656,128]{2,1,0:T(8,128)(2,1)S(1)}, u32[]{:S(2)}, u32[]{:S(2)}) collective-permute-start(bf16[3,656,128]{2,1,0:T(8,128)(2,1)} %collective-permute-done.23), channel_id=1, source_target_pairs={{0,16},{4,20},{8,24},{12,28},{16,0},{20,4},{24,8},{28,12},{1,17},{... | collective-permute-start | bytes 1511432 | tf_op jit(solution)/shard_map/ppermute | solution.py:438
  135.6 30.0 %collective-permute-start.41 = (bf16[3,656,128]{2,1,0:T(8,128)(2,1)}, bf16[3,656,128]{2,1,0:T(8,128)(2,1)S(1)}, u32[]{:S(2)}, u32[]{:S(2)}) collective-permute-start(bf16[3,656,128]{2,1,0:T(8,128)(2,1)} %collective-permute-done.23), channel_id=1, source_target_pairs={{0,4},{4,0},{8,12},{12,8},{16,20},{20,16},{24,28},{28,24},{1,5},{5... | collective-permute-start | bytes 1511432 | tf_op jit(solution)/shard_map/ppermute | solution.py:438
  138.5 27.1 %collective-permute-start.38 = (bf16[3,656,128]{2,1,0:T(8,128)(2,1)}, bf16[3,656,128]{2,1,0:T(8,128)(2,1)S(1)}, u32[]{:S(2)}, u32[]{:S(2)}) collective-permute-start(bf16[3,656,128]{2,1,0:T(8,128)(2,1)} %collective-permute-done.24), channel_id=1, source_target_pairs={{0,8},{4,12},{8,0},{12,4},{16,24},{20,28},{24,16},{28,20},{1,9},{5... | collective-permute-start | bytes 1511432 | tf_op jit(solution)/shard_map/ppermute | solution.py:438
  139.0 26.6 %collective-permute-start.39 = (bf16[3,656,128]{2,1,0:T(8,128)(2,1)S(1)}, bf16[3,656,128]{2,1,0:T(8,128)(2,1)}, u32[]{:S(2)}, u32[]{:S(2)}) collective-permute-start(bf16[3,656,128]{2,1,0:T(8,128)(2,1)S(1)} %collective-permute-done.31), channel_id=1, source_target_pairs={{0,8},{4,12},{8,0},{12,4},{16,24},{20,28},{24,16},{28,20},{1,9},{5... | collective-permute-start | bytes 1511432 | tf_op jit(solution)/shard_map/ppermute | solution.py:438
  140.6 25.1 %collective-permute-start.42 = (bf16[3,656,128]{2,1,0:T(8,128)(2,1)}, bf16[3,656,128]{2,1,0:T(8,128)(2,1)S(1)}, u32[]{:S(2)}, u32[]{:S(2)}) collective-permute-start(bf16[3,656,128]{2,1,0:T(8,128)(2,1)} %collective-permute-done.28), channel_id=1, source_target_pairs={{0,4},{4,0},{8,12},{12,8},{16,20},{20,16},{24,28},{28,24},{1,5},{5... | collective-permute-start | bytes 1511432 | tf_op jit(solution)/shard_map/ppermute | solution.py:438
  140.6 25.1 %collective-permute-start.40 = (bf16[3,656,128]{2,1,0:T(8,128)(2,1)}, bf16[3,656,128]{2,1,0:T(8,128)(2,1)}, u32[]{:S(2)}, u32[]{:S(2)}) collective-permute-start(bf16[3,656,128]{2,1,0:T(8,128)(2,1)} %collective-permute-done.28), channel_id=1, source_target_pairs={{0,16},{4,20},{8,24},{12,28},{16,0},{20,4},{24,8},{28,12},{1,17},{... | collective-permute-start | bytes 1511432 | tf_op jit(solution)/shard_map/ppermute | solution.py:438
  181.1 28.4 %collective-permute-start.50 = (bf16[1,3,656,128]{3,2,1,0:T(8,128)(2,1)}, bf16[1,3,656,128]{3,2,1,0:T(8,128)(2,1)S(1)}, u32[]{:S(2)}, u32[]{:S(2)}) collective-permute-start(bf16[1,3,656,128]{3,2,1,0:T(8,128)(2,1)} %get-tuple-element.391), channel_id=1, source_target_pairs={{0,16},{4,20},{8,24},{12,28},{16,0},{20,4},{24,8},{28,12},{1,17},{... | collective-permute-start | bytes 1511432 | tf_op jit(solution)/shard_map/ppermute | solution.py:438
  182.6 26.8 %collective-permute-start.51 = (bf16[1,3,656,128]{3,2,1,0:T(8,128)(2,1)}, bf16[1,3,656,128]{3,2,1,0:T(8,128)(2,1)S(1)}, u32[]{:S(2)}, u32[]{:S(2)}) collective-permute-start(bf16[1,3,656,128]{3,2,1,0:T(8,128)(2,1)} %get-tuple-element.392), channel_id=1, source_target_pairs={{0,8},{4,12},{8,0},{12,4},{16,24},{20,28},{24,16},{28,20},{1,9},{5... | collective-permute-start | bytes 1511432 | tf_op jit(solution)/shard_map/ppermute | solution.py:438
  209.5 30.2 %collective-permute-start.54 = (bf16[4,2,3,656,128]{4,3,2,1,0:T(8,128)(2,1)}, bf16[4,2,3,656,128]{4,3,2,1,0:T(8,128)(2,1)}, u32[]{:S(2)}, u32[]{:S(2)}) collective-permute-start(bf16[4,2,3,656,128]{4,3,2,1,0:T(8,128)(2,1)} %get-tuple-element.418), channel_id=1, source_target_pairs={{0,4},{4,0},{8,12},{12,8},{16,20},{20,16},{24,28},{28,24},{1,5},{5... | collective-permute-start | bytes 12091400 | tf_op jit(solution)/shard_map/ppermute | solution.py:438
  213.5 24.9 %collective-permute-start.52 = (bf16[2,3,656,128]{3,2,1,0:T(8,128)(2,1)}, bf16[2,3,656,128]{3,2,1,0:T(8,128)(2,1)S(1)}, u32[]{:S(2)}, u32[]{:S(2)}) collective-permute-start(bf16[2,3,656,128]{3,2,1,0:T(8,128)(2,1)} %pad_maximum_fusion.2), channel_id=1, source_target_pairs={{0,8},{4,12},{8,0},{12,4},{16,24},{20,28},{24,16},{28,20},{1,9},{5... | collective-permute-start | bytes 3022856 | tf_op jit(solution)/shard_map/ppermute | solution.py:438
  215.0 24.6 %collective-permute-start.53 = (bf16[2,3,656,128]{3,2,1,0:T(8,128)(2,1)}, bf16[2,3,656,128]{3,2,1,0:T(8,128)(2,1)S(1)}, u32[]{:S(2)}, u32[]{:S(2)}) collective-permute-start(bf16[2,3,656,128]{3,2,1,0:T(8,128)(2,1)} %pad_maximum_fusion.3), channel_id=1, source_target_pairs={{0,16},{4,20},{8,24},{12,28},{16,0},{20,4},{24,8},{28,12},{1,17},{... | collective-permute-start | bytes 3022856 | tf_op jit(solution)/shard_map/ppermute | solution.py:438
  271.1 25.9 %collective-permute-start.58 = (bf16[2,3,656,128]{3,2,1,0:T(8,128)(2,1)}, bf16[2,3,656,128]{3,2,1,0:T(8,128)(2,1)S(1)}, u32[]{:S(2)}, u32[]{:S(2)}) collective-permute-start(bf16[2,3,656,128]{3,2,1,0:T(8,128)(2,1)} %pad_maximum_fusion.4), channel_id=1, source_target_pairs={{0,8},{4,12},{8,0},{12,4},{16,24},{20,28},{24,16},{28,20},{1,9},{5... | collective-permute-start | bytes 3022856 | tf_op jit(solution)/shard_map/ppermute | solution.py:438
  272.6 24.4 %collective-permute-start.59 = (bf16[2,3,656,128]{3,2,1,0:T(8,128)(2,1)S(1)}, bf16[2,3,656,128]{3,2,1,0:T(8,128)(2,1)S(1)}, u32[]{:S(2)}, u32[]{:S(2)}) collective-permute-start(bf16[2,3,656,128]{3,2,1,0:T(8,128)(2,1)S(1)} %pad_maximum_fusion.5), channel_id=1, source_target_pairs={{0,16},{4,20},{8,24},{12,28},{16,0},{20,4},{24,8},{28,12},{1,17},{... | collective-permute-start | bytes 3022856 | tf_op jit(solution)/shard_map/ppermute | solution.py:438
  329.3 24.8 %collective-permute-start.67 = (bf16[4,4,128,256]{3,2,1,0:T(8,128)(2,1)}, bf16[4,4,128,256]{3,2,1,0:T(8,128)(2,1)S(1)}, u32[]{:S(2)}, u32[]{:S(2)}) collective-permute-start(bf16[4,4,128,256]{3,2,1,0:T(8,128)(2,1)} %pad_maximum_fusion), channel_id=1, source_target_pairs={{0,8},{4,12},{8,0},{12,4},{16,24},{20,28},{24,16},{28,20},{1,9},{5... | collective-permute-start | bytes 3145736 | tf_op jit(solution)/shard_map/ppermute | solution.py:438
  330.0 24.1 %collective-permute-start.68 = (bf16[4,4,128,256]{3,2,1,0:T(8,128)(2,1)}, bf16[4,4,128,256]{3,2,1,0:T(8,128)(2,1)S(1)}, u32[]{:S(2)}, u32[]{:S(2)}) collective-permute-start(bf16[4,4,128,256]{3,2,1,0:T(8,128)(2,1)} %pad_maximum_fusion.1), channel_id=1, source_target_pairs={{0,16},{4,20},{8,24},{12,28},{16,0},{20,4},{24,8},{28,12},{1,17},{... | collective-permute-start | bytes 3145736 | tf_op jit(solution)/shard_map/ppermute | solution.py:438
  330.6 24.7 %collective-permute-start.70 = (bf16[512,1024]{1,0:T(8,128)(2,1)}, bf16[512,1024]{1,0:T(8,128)(2,1)S(1)}, u32[]{:S(2)}, u32[]{:S(2)}) collective-permute-start(bf16[512,1024]{1,0:T(8,128)(2,1)} %get-tuple-element.485), channel_id=1, source_target_pairs={{0,1},{1,0},{2,3},{3,2},{4,5},{5,4},{6,7},{7,6},{8,9},{9,8},{10,11... | collective-permute-start | bytes 3145736 | tf_op jit(solution)/shard_map/ppermute | solution.py:759
  (101 other events, 1338.6 us)

commit v5 on v4

--- a/solution.py
+++ b/solution.py
@@ -708,32 +708,33 @@
         set_2, set_3 = mlp_set(2), mlp_set(3)
         core_2 = to_core([after(a, odd_a) for a in set_2], owners)
         core_3 = core_3 + to_core([after(a, odd_a) for a in set_3[2:]], owners)
-        core_a = swap_dp(odd_a, 1, owners)
+        core_2, core_3, carry = together((core_2, core_3, carry))
+        core_a = swap_dp(after(odd_a, core_2[3]), 1, owners)
+        out = mlp(*mlp_args, mlp_pieces((2, set_2 + core_2), (3, set_3 + core_3)), S0=half, N=half, carry=carry)
+        core_a, out = together((core_a, tuple(out)))
+        output, dresid, dres_low, dres_turned, gain_two, stat_m, even_b, odd_b = out
         low, high = cross_sends(even_a, core_a, 1)
-        low, high, core_2, core_3, carry = lax.optimization_barrier((low, high, core_2, core_3, carry))
+        low, high, dres_low = together((low, high, dres_low))
         from_y, from_x = swap_dp(low, 4, owners), swap_dp(high, 2, owners)
-        out = mlp(*mlp_args, mlp_pieces((2, set_2 + core_2), (3, set_3 + core_3)), S0=half, N=half, carry=carry)
-        from_y, from_x, *out = lax.optimization_barrier((from_y, from_x, *out))
-        output, dresid, dres_low, dres_turned, gain_two, stat_m, even_b, odd_b = out
         core_b2 = swap_dp(odd_b, 1, owners)
-        to_x, to_y = side_sends(even_a, core_a, from_y, from_x, 1)
-        to_x, to_y, dres_low = lax.optimization_barrier((to_x, to_y, dres_low))
-        back_x, back_y = swap_dp(to_x, 2, owners), swap_dp(to_y, 4, owners)
         fwd_kept = (queries, keys, values, log_sums, attn_pieces)
         grads = bwd_attn(attn_perm, dres_low, *back_args, *fwd_kept, S0=0, N=half)
-        back_x, back_y, core_b2, *grads = lax.optimization_barrier((back_x, back_y, core_b2, *grads))
+        from_y, from_x, core_b2, *grads = together((from_y, from_x, core_b2, *grads))
         low, high = cross_sends(even_b, core_b2, 1)
+        to_x, to_y = side_sends(even_a, core_a, from_y, from_x, 1)
+        low, high, to_x, to_y, dres_low = together((low, high, to_x, to_y, dres_low))
+        from_y, from_x = swap_dp(low, 4, owners), swap_dp(high, 2, owners)
+        back_x, back_y = swap_dp(to_x, 2, owners), swap_dp(to_y, 4, owners)
+        grads = bwd_attn(attn_perm, dres_low, *back_args, *fwd_kept, S0=half, N=half, carry=tuple(grads))
+        from_y, from_x, *grads = together((from_y, from_x, *grads))
+        to_x, to_y = side_sends(even_b, core_b2, from_y, from_x, 1)
+        to_x, to_y, back_x, back_y = together((to_x, to_y, back_x, back_y))
+        from_x, from_y = swap_dp(to_x, 2, owners), swap_dp(to_y, 4, owners)
         ring_1 = own_part(even_a, core_a, back_x, back_y, 1).astype(BF)
-        low, high, ring_1, dres_low = lax.optimization_barrier((low, high, ring_1, dres_low))
-        from_y, from_x = swap_dp(low, 4, owners), swap_dp(high, 2, owners)
+        ring_1, dres_turned = together((ring_1, dres_turned))
         ring_1 = to_ring_succ(ring_1, shards)
-        grads = bwd_attn(attn_perm, dres_low, *back_args, *fwd_kept, S0=half, N=half, carry=tuple(grads))
-        from_y, from_x, ring_1, *grads = lax.optimization_barrier((from_y, from_x, ring_1, *grads))
-        to_x, to_y = side_sends(even_b, core_b2, from_y, from_x, 1)
-        to_x, to_y, dres_turned = lax.optimization_barrier((to_x, to_y, dres_turned))
-        from_x, from_y = swap_dp(to_x, 2, owners), swap_dp(to_y, 4, owners)
         out = grad_attn(attn_perm, slots, first_turned, dres_turned, xhat_low, attended, *grads, attn_pieces)
-        from_x, from_y, *out = lax.optimization_barrier((from_x, from_y, *out))
+        from_x, from_y, ring_1, *out = lax.optimization_barrier((from_x, from_y, ring_1, *out))
         da_own, da_far, gain_one, attn_even, attn_odd = out
     else:
         queries, keys, values, attended, log_sums, resid, second_norm, stat_a = fwd_attn(*fwd_args, attn_pieces)
@@ -795,7 +796,7 @@
         ring_3 = to_ring_succ(ring_3, shards)
         small, cross_x, cross_y = lax.optimization_barrier((small, cross_x, cross_y))
         to_x, to_y = side_sends(attn_even, attn_core, cross_y, cross_x, half)
-        to_x, to_y, small, ring_3 = lax.optimization_barrier((to_x, to_y, small, ring_3))
+        to_x, to_y, small = lax.optimization_barrier((to_x, to_y, small))
         attn_x, attn_y = swap_dp(to_x, 2, owners), swap_dp(to_y, 4, owners)
         small = small + swap_dp(small, 4, owners)
         da_back = send_back(after(da_far, ring_3))

time: 402 us -> 397 us (0.988)
  transfers between devices with their start and end apart: 76 -> 76, of which waited for: 29 -> 32; matrix products, arithmetic and copies ran while one was open for 9% -> 10% of each run, Pallas kernels for 44% -> 44%
where the time goes in v5:
time: 397 us; the launch traced here: 391 us
  Pallas kernels  181 us (46%)
  waiting for transfers between devices  81.3 us (20%)
  starting transfers between devices  68.4 us (17%)
  other arithmetic  48.9 us (12%)
  local copies, waits for them, and re-layouts  6.38 us (2%)
  between operations  5.02 us (1%)
    pallas_call x2, Pallas kernels, mlp(): pl.pallas_call(functools.partial(mlp_kernel, T=T, D=D, HC=HC, R=R, metas=...  50.5 us
    ppermute x60, starting transfers between devices, swap_dp(): return lax.ppermute(value, 'dp', [(i, i ^ bit) for i in range(owners)])  41.3 us
    pallas_call x2, Pallas kernels, bwd_attn(): pl.pallas_call(functools.partial(bwd_attn_kernel, T=T, KV=KV, C=C, metas=...  38.2 us
    pallas_call x2, Pallas kernels, fwd_attn(): pl.pallas_call(functools.partial(fwd_attn_kernel, T=T, KV=KV, C=C, metas=...  36.7 us
    ppermute x60, waiting for transfers between devices, swap_dp(): return lax.ppermute(value, 'dp', [(i, i ^ bit) for i in range(owners)])  35.2 us
    pallas_call x1, Pallas kernels, grad_attn(): pl.pallas_call(functools.partial(grad_attn_kernel, T=T, KV=KV, C=C, R=R,...  22.6 us
    pallas_call x2, Pallas kernels, soap(): pl.pallas_call(functools.partial(soap_kernel, turned=turned), grid_spec=g...  21.6 us
    ppermute x1, waiting for transfers between devices, from_peer(): return lax.ppermute(value, 'tensor', pairs)  15.4 us
  transfers between devices with their start and end apart: 76, of which 32 were waited for; matrix products, arithmetic and copies ran while one was open for 10% of the time, Pallas kernels for 44%

profile of v5, /device:TPU:0, one launch (start us, length us, event | category | flops | bytes accessed | tf_op | source)
XLA Modules:
  0.0 390.6 jit_solution(553812579889063962)
XLA Ops:
  0.7 3.0 collective-permute-start.2
  24.7 5.8 %collective-permute-done.4.rest_2_ = bf16[2,4,128,256]{3,2,1,0:T(8,128)(2,1)S(1)} collective-permute-done((bf16[2,4,128,256]{3,2,1,0:T(8,128)(2,1)S(1)}, bf16[2,4,128,256]{3,2,1,0:T(8,128)(2,1)S(1)}, u32[]{:S(2)}, u32[]{:S(2)}) %collective-permute-start.4) | collective-permute-done | bytes 524320 | tf_op jit(solution)/shard_map/ppermute | solution.py:438
  36.9 15.4 %collective-permute-done.9.far = bf16[512,1024]{1,0:T(8,128)(2,1)} collective-permute-done((bf16[512,1024]{1,0:T(8,128)(2,1)S(1)}, bf16[512,1024]{1,0:T(8,128)(2,1)}, u32[]{:S(2)}, u32[]{:S(2)}) %collective-permute-start.9) | collective-permute-done | bytes 1048608 | tf_op jit(solution)/shard_map/ppermute | solution.py:578
  52.3 5.8 %norm_first.1 = (bf16[1024,1024]{1,0:T(8,128)(2,1)}, bf16[1024,1024]{1,0:T(8,128)(2,1)}, bf16[1024,1024]{1,0:T(8,128)(2,1)}) custom-call(bf16[512,1024]{1,0:T(8,128)(2,1)} %hid.5, bf16[512,1024]{1,0:T(8,128)(2,1)} %collective-permute-done.9.far, f32[1,1024]{1,0:T(1,128)} %get-tuple-element.274.gain), custom_call_target="tpu_custom_call" | custom-call | flops 1 | bytes 1 | tf_op jit(solution)/shard_map/norm_first/pallas_call | solution.py:410
  63.7 11.2 %collective-permute-done.16 = bf16[3,656,128]{2,1,0:T(8,128)(2,1)} collective-permute-done((bf16[3,656,128]{2,1,0:T(8,128)(2,1)}, bf16[3,656,128]{2,1,0:T(8,128)(2,1)}, u32[]{:S(2)}, u32[]{:S(2)}) %collective-permute-start.16) | collective-permute-done | bytes 503840 | tf_op jit(solution)/shard_map/ppermute | solution.py:457
  84.2 16.6 %attn_fwd.2 = (bf16[4,512,256]{2,1,0:T(8,128)(2,1)}, bf16[4,1024,256]{2,1,0:T(8,128)(2,1)}, bf16[4,1024,256]{2,1,0:T(8,128)(2,1)}, bf16[4,512,256]{2,1,0:T(8,128...) custom-call(s32[16]{0:T(128)} %pad_add_fusion.1.perm, bf16[1024,1024]{1,0:T(8,128)(2,1)} %get-tuple-element.298.a1, ...), custom_call_target="tpu_custom_call" | custom-call | flops 1 | bytes 1 | tf_op jit(solution)/shard_map/attn_fwd/pallas_call | solution.py:134
  111.1 20.1 %attn_fwd.3 = (bf16[4,512,256]{2,1,0:T(8,128)(2,1)}, bf16[4,1024,256]{2,1,0:T(8,128)(2,1)}, bf16[4,1024,256]{2,1,0:T(8,128)(2,1)}, bf16[4,512,256]{2,1,0:T(8,128...) custom-call(s32[16]{0:T(128)} %pad_add_fusion.1.perm, ...), custom_call_target="tpu_custom_call", output_to_operand_aliasing={{0}: (18, {}), {1}: (19, {}), {2}: (20, {}), {3}: (21, {}),... | custom-call | flops 1 | bytes 1 | tf_op jit(solution)/shard_map/attn_fwd/pallas_call | solution.py:134
  141.1 24.2 %mlp_both.2 = (f32[512,1024]{1,0:T(8,128)}, f32[512,1024]{1,0:T(8,128)}, bf16[4,2,3,656,128]{4,3,2,1,0:T(8,128)(2,1)}, bf16[4,2,3,656,128]{4,3,2,1,0:T(8,128)(2,1)}) custom-call(s32[16]{0:T(128)} %pad_add_fusion.1.perm, s32[4]{0:T(128)} %iota.18.slots, bf16[512,1024]{1,0:T(8,128)(2,1)} %get-tuple-element.357.a2, bf16[512,1024]{1,0:T(8,128)(2,1)} %g.3, ...), custom_call_target="tpu_custom_call" | custom-call | flops 1 | bytes 1 | tf_op jit(solution)/shard_map/mlp_both/pallas_call | solution.py:232
  171.8 26.3 %mlp_both.3 = (bf16[512,1024]{1,0:T(8,128)(2,1)}, f32[512,1024]{1,0:T(8,128)}, bf16[512,1024]{1,0:T(8,128)(2,1)}, bf16[1024,512]{1,0:T(8,128)(2,1)}, f32[1,1024]...) custom-call(s32[16]{0:T(128)} %pad_add_fusion.1.perm, ...), custom_call_target="tpu_custom_call" | custom-call | flops 1 | bytes 1 | tf_op jit(solution)/shard_map/mlp_both/pallas_call | solution.py:232
  203.1 19.0 %attn_bwd.2 = (bf16[4,512,256]{2,1,0:T(8,128)(2,1)}, bf16[4,1024,256]{2,1,0:T(8,128)(2,1)}, bf16[4,1024,256]{2,1,0:T(8,128)(2,1)}) custom-call(s32[16]{0:T(128)} %pad_add_fusion.1.perm, bf16[512,1024]{1,0:T(8,128)(2,1)} %get-tuple-element.431.dres, f32[1024,128]{1,0:T(8,128)} %get-tuple-element.300.cos, f32[1024,128]{1,0:T(8,128)} %get-tuple-element.301.sin, ...), custom_call_target="tpu_custom_call" | custom-call | flops 1 | bytes 1 | tf_op jit(solution)/shard_map/attn_bwd/pallas_call | solution.py:290
  226.3 3.0 fusion.29
  233.3 19.2 %attn_bwd.3 = (bf16[4,512,256]{2,1,0:T(8,128)(2,1)}, bf16[4,1024,256]{2,1,0:T(8,128)(2,1)}, bf16[4,1024,256]{2,1,0:T(8,128)(2,1)}) custom-call(s32[16]{0:T(128)} %pad_add_fusion.1.perm, bf16[512,1024]{1,0:T(8,128)(2,1)} %get-tuple-element.431.dres, ...), custom_call_target="tpu_custom_call", output_to_operand_aliasing={{0}: (26, {}), {1}: (27, {}), {2}: (28, {})} | custom-call | flops 1 | bytes 1 | tf_op jit(solution)/shard_map/attn_bwd/pallas_call | solution.py:290
  256.7 7.6 %collective-permute-done.55 = bf16[2,3,656,128]{3,2,1,0:T(8,128)(2,1)S(1)} collective-permute-done((bf16[2,3,656,128]{3,2,1,0:T(8,128)(2,1)}, bf16[2,3,656,128]{3,2,1,0:T(8,128)(2,1)S(1)}, u32[]{:S(2)}, u32[]{:S(2)}) %collective-permute-start.55) | collective-permute-done | bytes 1007648 | tf_op jit(solution)/shard_map/ppermute | solution.py:438
  271.6 22.6 %attn_grad.1 = (f32[512,1024]{1,0:T(8,128)}, bf16[512,1024]{1,0:T(8,128)(2,1)}, f32[1,1024]{1,0:T(1,128)}, bf16[4,4,4,128,256]{4,3,2,1,0:T(8,128)(2,1)}, bf16[4,4,4,128,256]{4,3,2,1,0:T(8,128)(2,1)}) custom-call(s32[16]{0:T(128)} %pad_add_fusion.1.perm, s32[4]{0:T(128)} %iota.18.slots, bf16[1024,1024]{1,0:T(8,128)(2,1)} %get-tuple-element.448.a1T, ...), custom_call_target="tpu_custom_call" | custom-call | flops 1 | bytes 1 | tf_op jit(solution)/shard_map/attn_grad/pallas_call | solution.py:346
  302.3 2.9 fusion.15
  307.8 4.7 %collective-permute-done.67 = bf16[3,656,128]{2,1,0:T(8,128)(2,1)S(1)} collective-permute-done((bf16[3,656,128]{2,1,0:T(8,128)(2,1)S(1)}, bf16[3,656,128]{2,1,0:T(8,128)(2,1)S(1)}, u32[]{:S(2)}, u32[]{:S(2)}) %collective-permute-start.67) | collective-permute-done | bytes 503840 | tf_op jit(solution)/shard_map/ppermute | solution.py:450
  316.9 2.7 collective-permute-done.62
  332.1 2.9 fusion.6.g_in
  335.0 14.6 %soap_mlp.1 = (f32[3,656,128]{2,1,0:T(8,128)}, f32[3,656,128]{2,1,0:T(8,128)}, f32[3,656,128]{2,1,0:T(8,128)}, f32[3,8,128]{2,1,0:T(8,128)}) custom-call(f32[3]{0:T(128)} %pad_maximum_fusion.11.sc, f32[3,656,128]{2,1,0:T(8,128)} %fusion.6.g_in, f32[3,656,128]{2,1,0:T(8,128)} %bitcast.173, f32[3,656,128]{2,1,0:T(8,128)} %bitcast.174, f32[3,128,128]{2,1,0:T(8,128)} %left.2, ...), custom_call_target="tpu_custom_call" | custom-call | flops 1 | bytes 1 | tf_op jit(solution)/shard_map/soap_mlp/pallas_call | solution.py:390
  350.8 3.4 collective-permute-start.71
  354.2 5.2 %input_back.1 = bf16[512,1024]{1,0:T(8,128)(2,1)} custom-call(bf16[512,1024]{1,0:T(8,128)(2,1)} %hid.5, f32[512,1024]{1,0:T(8,128)} %get-tuple-element.489.da, f32[512,1024]{1,0:T(8,128)} %get-tuple-element.490.dres, f32[1,1024]{1,0:T(1,128)} %get-tuple-element.274.gain, bf16[512,1024]{1,0:T(8,128)(2,1)} %copy-done.16), custom_call_target="tpu_custom_call" | custom-call | flops 1 | bytes 1 | tf_op jit(solution)/shard_map/input_back/pallas_call | solution.py:428
  364.1 5.9 %collective-permute-done.74 = f32[3,1024]{1,0:T(4,128)S(1)} collective-permute-done((f32[3,1024]{1,0:T(4,128)S(1)}, f32[3,1024]{1,0:T(4,128)S(1)}, u32[]{:S(2)}, u32[]{:S(2)}) %collective-permute-start.74) | collective-permute-done | bytes 12320 | tf_op jit(solution)/shard_map/ppermute | solution.py:764
  372.5 5.1 %collective-permute-done.75 = bf16[4,128,256]{2,1,0:T(8,128)(2,1)S(1)} collective-permute-done((bf16[4,128,256]{2,1,0:T(8,128)(2,1)S(1)}, bf16[4,128,256]{2,1,0:T(8,128)(2,1)S(1)}, u32[]{:S(2)}, u32[]{:S(2)}) %collective-permute-start.75) | collective-permute-done | bytes 262176 | tf_op jit(solution)/shard_map/ppermute | solution.py:450
  381.4 7.0 %soap_attn.1 = (f32[4,128,256]{2,1,0:T(8,128)}, f32[4,128,256]{2,1,0:T(8,128)}, f32[4,128,256]{2,1,0:T(8,128)}, f32[4,8,128]{2,1,0:T(8,128)}) custom-call(f32[3]{0:T(128)} %pad_maximum_fusion.11.sc, f32[4,128,256]{2,1,0:T(8,128)} %fusion.16.g_in, f32[4,128,256]{2,1,0:T(8,128)} %first.1, f32[4,128,256]{2,1,0:T(8,128)} %second.1, f32[4,128,128]{2,1,0:T(8,128)} %left.3, ...), custom_call_target="tpu_custom_call" | custom-call | flops 1 | bytes 1 | tf_op jit(solution)/shard_map/soap_attn/pallas_call | solution.py:390
  (291 shorter events, 131.3 us)
Async XLA Ops:
  20.6 31.8 %collective-permute-start.9 = (bf16[512,1024]{1,0:T(8,128)(2,1)S(1)}, bf16[512,1024]{1,0:T(8,128)(2,1)}, u32[]{:S(2)}, u32[]{:S(2)}) collective-permute-start(bf16[512,1024]{1,0:T(8,128)(2,1)S(1)} %copy-done), channel_id=1, source_target_pairs={{1,0},{0,1},{3,2},{2,3},{5,4},{4,5},{7,6},{6,7},{9,8},{8,9},{11,10... | collective-permute-start | bytes 3145736 | tf_op jit(solution)/shard_map/ppermute | solution.py:578
  31.6 26.6 %collective-permute-start.7 = (bf16[2,4,128,256]{3,2,1,0:T(8,128)(2,1)S(1)}, bf16[2,4,128,256]{3,2,1,0:T(8,128)(2,1)S(1)}, u32[]{:S(2)}, u32[]{:S(2)}) collective-permute-start(bf16[2,4,128,256]{3,2,1,0:T(8,128)(2,1)S(1)} %collective-permute-done.3.rest_1_), channel_id=1, source_target_pairs={{0,16},{4,20},{8,24},{12,28},{16,0},{20,4},{24,8},{28,12},{1,17},{... | collective-permute-start | bytes 1572872 | tf_op jit(solution)/shard_map/ppermute | solution.py:438
  32.8 25.3 %collective-permute-start.8 = (bf16[3,656,128]{2,1,0:T(8,128)(2,1)}, bf16[3,656,128]{2,1,0:T(8,128)(2,1)}, u32[]{:S(2)}, u32[]{:S(2)}) collective-permute-start(bf16[3,656,128]{2,1,0:T(8,128)(2,1)} %copy-done.19), channel_id=1, source_target_pairs={{0,8},{4,12},{8,0},{12,4},{16,24},{20,28},{24,16},{28,20},{1,9},{5... | collective-permute-start | bytes 1511432 | tf_op jit(solution)/shard_map/ppermute | solution.py:438
  34.3 23.8 %collective-permute-start.10 = (bf16[4,128,256]{2,1,0:T(8,128)(2,1)}, bf16[4,128,256]{2,1,0:T(8,128)(2,1)}, u32[]{:S(2)}, u32[]{:S(2)}) collective-permute-start(bf16[4,128,256]{2,1,0:T(8,128)(2,1)} %collective-permute-done), channel_id=1, source_target_pairs={{0,2},{2,3},{3,1},{1,0},{4,6},{6,7},{7,5},{5,4},{8,10},{10,11},{11... | collective-permute-start | bytes 786440 | tf_op jit(solution)/shard_map/ppermute | solution.py:457
  77.5 25.8 %collective-permute-start.20 = (bf16[2,4,128,256]{3,2,1,0:T(8,128)(2,1)}, bf16[2,4,128,256]{3,2,1,0:T(8,128)(2,1)}, u32[]{:S(2)}, u32[]{:S(2)}) collective-permute-start(bf16[2,4,128,256]{3,2,1,0:T(8,128)(2,1)} %collective-permute-done.19.rest_2_.rest_10_), channel_id=1, source_target_pairs={{0,8},{4,12},{8,0},{12,4},{16,24},{20,28},{24,16},{28,20},{1,9},{5... | collective-permute-start | bytes 1572872 | tf_op jit(solution)/shard_map/ppermute | solution.py:438
  107.0 24.1 %collective-permute-start.30 = (bf16[3,656,128]{2,1,0:T(8,128)(2,1)}, bf16[3,656,128]{2,1,0:T(8,128)(2,1)}, u32[]{:S(2)}, u32[]{:S(2)}) collective-permute-start(bf16[3,656,128]{2,1,0:T(8,128)(2,1)} %collective-permute-done.22), channel_id=1, source_target_pairs={{0,8},{4,12},{8,0},{12,4},{16,24},{20,28},{24,16},{28,20},{1,9},{5... | collective-permute-start | bytes 1511432 | tf_op jit(solution)/shard_map/ppermute | solution.py:438
  109.0 23.7 %collective-permute-start.29 = (bf16[3,656,128]{2,1,0:T(8,128)(2,1)}, bf16[3,656,128]{2,1,0:T(8,128)(2,1)S(1)}, u32[]{:S(2)}, u32[]{:S(2)}) collective-permute-start(bf16[3,656,128]{2,1,0:T(8,128)(2,1)} %collective-permute-done.23), channel_id=1, source_target_pairs={{0,16},{4,20},{8,24},{12,28},{16,0},{20,4},{24,8},{28,12},{1,17},{... | collective-permute-start | bytes 1511432 | tf_op jit(solution)/shard_map/ppermute | solution.py:438
  135.6 29.7 %collective-permute-start.41 = (bf16[3,656,128]{2,1,0:T(8,128)(2,1)}, bf16[3,656,128]{2,1,0:T(8,128)(2,1)S(1)}, u32[]{:S(2)}, u32[]{:S(2)}) collective-permute-start(bf16[3,656,128]{2,1,0:T(8,128)(2,1)} %collective-permute-done.23), channel_id=1, source_target_pairs={{0,4},{4,0},{8,12},{12,8},{16,20},{20,16},{24,28},{28,24},{1,5},{5... | collective-permute-start | bytes 1511432 | tf_op jit(solution)/shard_map/ppermute | solution.py:438
  138.5 26.9 %collective-permute-start.38 = (bf16[3,656,128]{2,1,0:T(8,128)(2,1)}, bf16[3,656,128]{2,1,0:T(8,128)(2,1)S(1)}, u32[]{:S(2)}, u32[]{:S(2)}) collective-permute-start(bf16[3,656,128]{2,1,0:T(8,128)(2,1)} %collective-permute-done.24), channel_id=1, source_target_pairs={{0,8},{4,12},{8,0},{12,4},{16,24},{20,28},{24,16},{28,20},{1,9},{5... | collective-permute-start | bytes 1511432 | tf_op jit(solution)/shard_map/ppermute | solution.py:438
  139.0 26.3 %collective-permute-start.39 = (bf16[3,656,128]{2,1,0:T(8,128)(2,1)S(1)}, bf16[3,656,128]{2,1,0:T(8,128)(2,1)S(1)}, u32[]{:S(2)}, u32[]{:S(2)}) collective-permute-start(bf16[3,656,128]{2,1,0:T(8,128)(2,1)S(1)} %collective-permute-done.31), channel_id=1, source_target_pairs={{0,8},{4,12},{8,0},{12,4},{16,24},{20,28},{24,16},{28,20},{1,9},{5... | collective-permute-start | bytes 1511432 | tf_op jit(solution)/shard_map/ppermute | solution.py:438
  140.6 24.8 %collective-permute-start.42 = (bf16[3,656,128]{2,1,0:T(8,128)(2,1)}, bf16[3,656,128]{2,1,0:T(8,128)(2,1)S(1)}, u32[]{:S(2)}, u32[]{:S(2)}) collective-permute-start(bf16[3,656,128]{2,1,0:T(8,128)(2,1)} %collective-permute-done.28), channel_id=1, source_target_pairs={{0,4},{4,0},{8,12},{12,8},{16,20},{20,16},{24,28},{28,24},{1,5},{5... | collective-permute-start | bytes 1511432 | tf_op jit(solution)/shard_map/ppermute | solution.py:438
  140.6 24.8 %collective-permute-start.40 = (bf16[3,656,128]{2,1,0:T(8,128)(2,1)}, bf16[3,656,128]{2,1,0:T(8,128)(2,1)}, u32[]{:S(2)}, u32[]{:S(2)}) collective-permute-start(bf16[3,656,128]{2,1,0:T(8,128)(2,1)} %collective-permute-done.28), channel_id=1, source_target_pairs={{0,16},{4,20},{8,24},{12,28},{16,0},{20,4},{24,8},{28,12},{1,17},{... | collective-permute-start | bytes 1511432 | tf_op jit(solution)/shard_map/ppermute | solution.py:438
  171.0 27.1 %collective-permute-start.49 = (bf16[4,2,3,656,128]{4,3,2,1,0:T(8,128)(2,1)}, bf16[4,2,3,656,128]{4,3,2,1,0:T(8,128)(2,1)}, u32[]{:S(2)}, u32[]{:S(2)}) collective-permute-start(bf16[4,2,3,656,128]{4,3,2,1,0:T(8,128)(2,1)} %get-tuple-element.392), channel_id=1, source_target_pairs={{0,4},{4,0},{8,12},{12,8},{16,20},{20,16},{24,28},{28,24},{1,5},{5... | collective-permute-start | bytes 12091400 | tf_op jit(solution)/shard_map/ppermute | solution.py:438
  198.1 24.0 %collective-permute-start.52 = (bf16[4,2,3,656,128]{4,3,2,1,0:T(8,128)(2,1)}, bf16[4,2,3,656,128]{4,3,2,1,0:T(8,128)(2,1)}, u32[]{:S(2)}, u32[]{:S(2)}) collective-permute-start(bf16[4,2,3,656,128]{4,3,2,1,0:T(8,128)(2,1)} %get-tuple-element.417), channel_id=1, source_target_pairs={{0,4},{4,0},{8,12},{12,8},{16,20},{20,16},{24,28},{28,24},{1,5},{5... | collective-permute-start | bytes 12091400 | tf_op jit(solution)/shard_map/ppermute | solution.py:438
  229.2 23.3 %collective-permute-start.53 = (bf16[1,3,656,128]{3,2,1,0:T(8,128)(2,1)}, bf16[1,3,656,128]{3,2,1,0:T(8,128)(2,1)S(1)}, u32[]{:S(2)}, u32[]{:S(2)}) collective-permute-start(bf16[1,3,656,128]{3,2,1,0:T(8,128)(2,1)} %get-tuple-element.429), channel_id=1, source_target_pairs={{0,16},{4,20},{8,24},{12,28},{16,0},{20,4},{24,8},{28,12},{1,17},{... | collective-permute-start | bytes 1511432 | tf_op jit(solution)/shard_map/ppermute | solution.py:438
  229.6 22.9 %collective-permute-start.54 = (bf16[1,3,656,128]{3,2,1,0:T(8,128)(2,1)}, bf16[1,3,656,128]{3,2,1,0:T(8,128)(2,1)}, u32[]{:S(2)}, u32[]{:S(2)}) collective-permute-start(bf16[1,3,656,128]{3,2,1,0:T(8,128)(2,1)} %get-tuple-element.430), channel_id=1, source_target_pairs={{0,8},{4,12},{8,0},{12,4},{16,24},{20,28},{24,16},{28,20},{1,9},{5... | collective-permute-start | bytes 1511432 | tf_op jit(solution)/shard_map/ppermute | solution.py:438
  231.2 33.1 %collective-permute-start.55 = (bf16[2,3,656,128]{3,2,1,0:T(8,128)(2,1)}, bf16[2,3,656,128]{3,2,1,0:T(8,128)(2,1)S(1)}, u32[]{:S(2)}, u32[]{:S(2)}) collective-permute-start(bf16[2,3,656,128]{3,2,1,0:T(8,128)(2,1)} %pad_maximum_fusion.2), channel_id=1, source_target_pairs={{0,8},{4,12},{8,0},{12,4},{16,24},{20,28},{24,16},{28,20},{1,9},{5... | collective-permute-start | bytes 3022856 | tf_op jit(solution)/shard_map/ppermute | solution.py:438
  231.6 32.7 %collective-permute-start.56 = (bf16[2,3,656,128]{3,2,1,0:T(8,128)(2,1)}, bf16[2,3,656,128]{3,2,1,0:T(8,128)(2,1)S(1)}, u32[]{:S(2)}, u32[]{:S(2)}) collective-permute-start(bf16[2,3,656,128]{3,2,1,0:T(8,128)(2,1)} %pad_maximum_fusion.3), channel_id=1, source_target_pairs={{0,16},{4,20},{8,24},{12,28},{16,0},{20,4},{24,8},{28,12},{1,17},{... | collective-permute-start | bytes 3022856 | tf_op jit(solution)/shard_map/ppermute | solution.py:438
  264.3 30.0 %collective-permute-start.57 = (bf16[2,3,656,128]{3,2,1,0:T(8,128)(2,1)}, bf16[2,3,656,128]{3,2,1,0:T(8,128)(2,1)S(1)}, u32[]{:S(2)}, u32[]{:S(2)}) collective-permute-start(bf16[2,3,656,128]{3,2,1,0:T(8,128)(2,1)} %pad_maximum_fusion.4), channel_id=1, source_target_pairs={{0,8},{4,12},{8,0},{12,4},{16,24},{20,28},{24,16},{28,20},{1,9},{5... | collective-permute-start | bytes 3022856 | tf_op jit(solution)/shard_map/ppermute | solution.py:438
  266.0 28.3 %collective-permute-start.58 = (bf16[2,3,656,128]{3,2,1,0:T(8,128)(2,1)}, bf16[2,3,656,128]{3,2,1,0:T(8,128)(2,1)}, u32[]{:S(2)}, u32[]{:S(2)}) collective-permute-start(bf16[2,3,656,128]{3,2,1,0:T(8,128)(2,1)} %pad_maximum_fusion.5), channel_id=1, source_target_pairs={{0,16},{4,20},{8,24},{12,28},{16,0},{20,4},{24,8},{28,12},{1,17},{... | collective-permute-start | bytes 3022856 | tf_op jit(solution)/shard_map/ppermute | solution.py:438
  269.1 25.2 %collective-permute-start.59 = (bf16[3,656,128]{2,1,0:T(8,128)(2,1)S(1)}, bf16[3,656,128]{2,1,0:T(8,128)(2,1)}, u32[]{:S(2)}, u32[]{:S(2)}) collective-permute-start(bf16[3,656,128]{2,1,0:T(8,128)(2,1)S(1)} %fusion.7), channel_id=1, source_target_pairs={{0,2},{2,3},{3,1},{1,0},{4,6},{6,7},{7,5},{5,4},{8,10},{10,11},{11... | collective-permute-start | bytes 1511432 | tf_op jit(solution)/shard_map/ppermute | solution.py:450
  323.8 25.8 %collective-permute-start.65 = (bf16[4,4,128,256]{3,2,1,0:T(8,128)(2,1)}, bf16[4,4,128,256]{3,2,1,0:T(8,128)(2,1)S(1)}, u32[]{:S(2)}, u32[]{:S(2)}) collective-permute-start(bf16[4,4,128,256]{3,2,1,0:T(8,128)(2,1)} %pad_maximum_fusion), channel_id=1, source_target_pairs={{0,8},{4,12},{8,0},{12,4},{16,24},{20,28},{24,16},{28,20},{1,9},{5... | collective-permute-start | bytes 3145736 | tf_op jit(solution)/shard_map/ppermute | solution.py:438
  325.1 24.5 %collective-permute-start.66 = (bf16[4,4,128,256]{3,2,1,0:T(8,128)(2,1)}, bf16[4,4,128,256]{3,2,1,0:T(8,128)(2,1)S(1)}, u32[]{:S(2)}, u32[]{:S(2)}) collective-permute-start(bf16[4,4,128,256]{3,2,1,0:T(8,128)(2,1)} %pad_maximum_fusion.1), channel_id=1, source_target_pairs={{0,16},{4,20},{8,24},{12,28},{16,0},{20,4},{24,8},{28,12},{1,17},{... | collective-permute-start | bytes 3145736 | tf_op jit(solution)/shard_map/ppermute | solution.py:438
  327.0 23.8 %collective-permute-start.70 = (bf16[512,1024]{1,0:T(8,128)(2,1)}, bf16[512,1024]{1,0:T(8,128)(2,1)S(1)}, u32[]{:S(2)}, u32[]{:S(2)}) collective-permute-start(bf16[512,1024]{1,0:T(8,128)(2,1)} %get-tuple-element.487), channel_id=1, source_target_pairs={{0,1},{1,0},{2,3},{3,2},{4,5},{5,4},{6,7},{7,6},{8,9},{9,8},{10,11... | collective-permute-start | bytes 3145736 | tf_op jit(solution)/shard_map/ppermute | solution.py:760
  (99 other events, 1299.2 us)

commit v6 on v5

--- a/solution.py
+++ b/solution.py
@@ -355,39 +355,40 @@
     ah,al=a; bh,bl=b
     return dot(ah,bh,ca,cb)+(dot(ah,bl,ca,cb)+dot(al,bh,ca,cb))
 
-def soap_kernel(sc, g_in, first, second, left, right, *rest, turned):
+def soap_kernel(sc, g_in, first, second, left, right, *rest, turned, each):
     f_out, s_out, u_out, n_out = rest[-4:]
     step,b1,b2=sc[0],sc[1],sc[2]
-    ql=split3(left[0]); qr=split3(right[0])
-    if turned:
-        x=dot3(split3(g_in[0]),ql,1,0)
-        r=dot3(split3(x),qr,0,0).T
-    else:
-        x=dot3(ql,split3(g_in[0]),0,0)
-        r=dot3(split3(x),qr,1,0)
-    fn=b1*first[0]+(1.0-b1)*r
-    sn=b2*second[0]+(1.0-b2)*r*r
-    f_out[0]=fn; s_out[0]=sn
-    n=fn/(jnp.sqrt(sn)+ADAM_EPS)
-    if turned:
-        t=dot3(split3(dot3(qr,split3(n),1,0)),ql,1,1)
-    else:
-        t=dot3(split3(dot3(ql,split3(n),1,0)),qr,1,1)
-    size=n.shape[0]*n.shape[1]
-    fac=jnp.sqrt(jnp.sum(n*n,keepdims=True)*(1.0/size))*lax.rsqrt(jnp.sum(t*t,keepdims=True)*(1.0/size)+SCALE_EPS)
-    u_out[0]=(-step*fac)*t
-    n_out[0]=jnp.broadcast_to(fac,(8,128))
-
-def soap(scalars,g,first,second,left,right,turned,K0=0,N=None,carry=()):
+    for i in range(each):
+        ql=split3(left[i]); qr=split3(right[i])
+        if turned:
+            x=dot3(split3(g_in[i]),ql,1,0)
+            r=dot3(split3(x),qr,0,0).T
+        else:
+            x=dot3(ql,split3(g_in[i]),0,0)
+            r=dot3(split3(x),qr,1,0)
+        fn=b1*first[i]+(1.0-b1)*r
+        sn=b2*second[i]+(1.0-b2)*r*r
+        f_out[i]=fn; s_out[i]=sn
+        n=fn/(jnp.sqrt(sn)+ADAM_EPS)
+        if turned:
+            t=dot3(split3(dot3(qr,split3(n),1,0)),ql,1,1)
+        else:
+            t=dot3(split3(dot3(ql,split3(n),1,0)),qr,1,1)
+        size=n.shape[0]*n.shape[1]
+        fac=jnp.sqrt(jnp.sum(n*n,keepdims=True)*(1.0/size))*lax.rsqrt(jnp.sum(t*t,keepdims=True)*(1.0/size)+SCALE_EPS)
+        u_out[i]=(-step*fac)*t
+        n_out[i]=jnp.broadcast_to(fac,(8,128))
+
+def soap(scalars,g,first,second,left,right,turned,each=1,K0=0,N=None,carry=()):
     K=first.shape[0]
     N=K if N is None else N
-    b=lambda x:pl.BlockSpec((1,)+x.shape[1:],lambda k,s:(k+K0,0,0))
+    b=lambda x:pl.BlockSpec((each,)+x.shape[1:],lambda k,s:(k+K0,0,0))
     sd=jax.ShapeDtypeStruct
     o=sd(first.shape,F32)
     outs=[o,o,o,sd((K,8,128),F32)]
-    gs=pltpu.PrefetchScalarGridSpec(num_scalar_prefetch=1,grid=(N,),
+    gs=pltpu.PrefetchScalarGridSpec(num_scalar_prefetch=1,grid=(N//each,),
         in_specs=[b(x) for x in (g,first,second,left,right)]+[pl.BlockSpec(memory_space=ANY)]*len(carry),out_specs=[b(x) for x in outs])
-    return pl.pallas_call(functools.partial(soap_kernel,turned=turned),grid_spec=gs,out_shape=outs,
+    return pl.pallas_call(functools.partial(soap_kernel,turned=turned,each=each),grid_spec=gs,out_shape=outs,
         input_output_aliases={6+i:i for i in range(len(carry))},
         cost_estimate=pl.CostEstimate(flops=1,transcendentals=0,bytes_accessed=1),
         name="soap_"+("mlp" if turned else "attn"))(scalars,g,first,second,left,right,*carry)
@@ -647,7 +648,10 @@
         mlp_line = [mlp_turned, along_line(after(mlp_turned, line_3), 1, shards), None, None]
         core_a4 = to_core([after(a, z_a) for a in (pair_a, x_a, y_a, z_a)], owners)
         core_b = [swap_dp(after(pair_b, core_a4[1]), 1, owners)]
-        normal, core_a4, mlp_line[1], core_b, x_b, y_b = together((tuple(normal), core_a4, mlp_line[1], core_b, x_b, y_b))
+        core_0 = core_0 + to_core([after(a, core_b[0]) for a in (mlp_y[0], mlp_z[0])], owners)
+        normal, core_a4, mlp_line[1], core_b, x_b, y_b, core_0 = together(
+            (tuple(normal), core_a4, mlp_line[1], core_b, x_b, y_b, core_0)
+        )
         z_b = swap_dp(y_b, 2, owners)
         mlp_x[1], mlp_y[1] = swap_dp(mlp_line[1], 2, owners), swap_dp(mlp_line[1], 4, owners)
         mlp_line[3] = along_line(after(mlp_turned, mlp_line[1]), 3, shards)
@@ -696,8 +700,7 @@
 
         set_0, set_1 = mlp_set(0), mlp_set(1)
         core_1 = to_core([after(a, mlp_z[1]) for a in set_1], owners)
-        core_0 = core_0 + to_core([after(a, core_1[1]) for a in (mlp_y[0], mlp_z[0])], owners)
-        core_1, core_0, second_norm, mlp_x[3], mlp_y[2] = together((core_1, core_0, second_norm, mlp_x[3], mlp_y[2]))
+        core_1, second_norm, mlp_x[3], mlp_y[2] = together((core_1, second_norm, mlp_x[3], mlp_y[2]))
         mlp_z[3], mlp_z[2] = swap_dp(mlp_x[3], 4, owners), swap_dp(mlp_y[2], 2, owners)
         mlp_x[2] = swap_dp(after(mlp_line[2], second_norm), 2, owners)
         core_3 = to_core([mlp_line[3], mlp_x[3]], owners)
@@ -827,7 +830,7 @@
 
     attn_grad = attn_sum
     attn_first_new, attn_second_new, attn_update, attn_scale = soap(
-        scalars, attn_sum, attn_first, attn_second, attn_left, attn_right, False
+        scalars, attn_sum, attn_first, attn_second, attn_left, attn_right, False, 2
     )
     mlp_grad, mlp_first_new, mlp_second_new, mlp_update = (flip(v) for v in (mlp_sum, *mlp_new[:3]))
     mlp_scale = mlp_new[3]

time: 397 us -> 396 us (level)
  transfers between devices with their start and end apart: 76 -> 76, of which waited for: 32 -> 32; matrix products, arithmetic and copies ran while one was open for 10% -> 10% of each run, Pallas kernels for 44% -> 45%
where the time goes in v6:
time: 396 us; the launch traced here: 389 us
  Pallas kernels  180 us (45%)
  waiting for transfers between devices  79.5 us (20%)
  starting transfers between devices  69.9 us (18%)
  other arithmetic  48.9 us (12%)
  local copies, waits for them, and re-layouts  6.37 us (2%)
  between operations  5.06 us (1%)
    pallas_call x2, Pallas kernels, mlp(): pl.pallas_call(functools.partial(mlp_kernel, T=T, D=D, HC=HC, R=R, metas=...  50.4 us
    ppermute x60, starting transfers between devices, swap_dp(): return lax.ppermute(value, 'dp', [(i, i ^ bit) for i in range(owners)])  42.9 us
    pallas_call x2, Pallas kernels, bwd_attn(): pl.pallas_call(functools.partial(bwd_attn_kernel, T=T, KV=KV, C=C, metas=...  38.2 us
    ppermute x60, waiting for transfers between devices, swap_dp(): return lax.ppermute(value, 'dp', [(i, i ^ bit) for i in range(owners)])  37.7 us
    pallas_call x2, Pallas kernels, fwd_attn(): pl.pallas_call(functools.partial(fwd_attn_kernel, T=T, KV=KV, C=C, metas=...  36.7 us
    pallas_call x1, Pallas kernels, grad_attn(): pl.pallas_call(functools.partial(grad_attn_kernel, T=T, KV=KV, C=C, R=R,...  22.6 us
    pallas_call x2, Pallas kernels, soap(): pl.pallas_call(functools.partial(soap_kernel, turned=turned, each=each),...  20.6 us
    ppermute x1, waiting for transfers between devices, from_peer(): return lax.ppermute(value, 'tensor', pairs)  15.4 us
  transfers between devices with their start and end apart: 76, of which 32 were waited for; matrix products, arithmetic and copies ran while one was open for 10% of the time, Pallas kernels for 45%

profile of v6, /device:TPU:0, one launch (start us, length us, event | category | flops | bytes accessed | tf_op | source)
XLA Modules:
  0.0 389.4 jit_solution(3541415215284382504)
XLA Ops:
  0.7 3.0 collective-permute-start.2
  24.7 5.8 %collective-permute-done.4.rest_2_ = bf16[2,4,128,256]{3,2,1,0:T(8,128)(2,1)S(1)} collective-permute-done((bf16[2,4,128,256]{3,2,1,0:T(8,128)(2,1)S(1)}, bf16[2,4,128,256]{3,2,1,0:T(8,128)(2,1)S(1)}, u32[]{:S(2)}, u32[]{:S(2)}) %collective-permute-start.4) | collective-permute-done | bytes 524320 | tf_op jit(solution)/shard_map/ppermute | solution.py:439
  36.9 15.4 %collective-permute-done.9.far = bf16[512,1024]{1,0:T(8,128)(2,1)} collective-permute-done((bf16[512,1024]{1,0:T(8,128)(2,1)S(1)}, bf16[512,1024]{1,0:T(8,128)(2,1)}, u32[]{:S(2)}, u32[]{:S(2)}) %collective-permute-start.9) | collective-permute-done | bytes 1048608 | tf_op jit(solution)/shard_map/ppermute | solution.py:579
  52.3 5.9 %norm_first.1 = (bf16[1024,1024]{1,0:T(8,128)(2,1)}, bf16[1024,1024]{1,0:T(8,128)(2,1)}, bf16[1024,1024]{1,0:T(8,128)(2,1)}) custom-call(bf16[512,1024]{1,0:T(8,128)(2,1)} %hid.5, bf16[512,1024]{1,0:T(8,128)(2,1)} %collective-permute-done.9.far, f32[1,1024]{1,0:T(1,128)} %get-tuple-element.274.gain), custom_call_target="tpu_custom_call" | custom-call | flops 1 | bytes 1 | tf_op jit(solution)/shard_map/norm_first/pallas_call | solution.py:411
  64.0 10.4 %collective-permute-done.16 = bf16[3,656,128]{2,1,0:T(8,128)(2,1)} collective-permute-done((bf16[3,656,128]{2,1,0:T(8,128)(2,1)}, bf16[3,656,128]{2,1,0:T(8,128)(2,1)}, u32[]{:S(2)}, u32[]{:S(2)}) %collective-permute-start.16) | collective-permute-done | bytes 503840 | tf_op jit(solution)/shard_map/ppermute | solution.py:458
  86.4 16.6 %attn_fwd.2 = (bf16[4,512,256]{2,1,0:T(8,128)(2,1)}, bf16[4,1024,256]{2,1,0:T(8,128)(2,1)}, bf16[4,1024,256]{2,1,0:T(8,128)(2,1)}, bf16[4,512,256]{2,1,0:T(8,128...) custom-call(s32[16]{0:T(128)} %pad_add_fusion.1.perm, bf16[1024,1024]{1,0:T(8,128)(2,1)} %get-tuple-element.303.a1, ...), custom_call_target="tpu_custom_call" | custom-call | flops 1 | bytes 1 | tf_op jit(solution)/shard_map/attn_fwd/pallas_call | solution.py:134
  112.7 20.1 %attn_fwd.3 = (bf16[4,512,256]{2,1,0:T(8,128)(2,1)}, bf16[4,1024,256]{2,1,0:T(8,128)(2,1)}, bf16[4,1024,256]{2,1,0:T(8,128)(2,1)}, bf16[4,512,256]{2,1,0:T(8,128...) custom-call(s32[16]{0:T(128)} %pad_add_fusion.1.perm, ...), custom_call_target="tpu_custom_call", output_to_operand_aliasing={{0}: (18, {}), {1}: (19, {}), {2}: (20, {}), {3}: (21, {}),... | custom-call | flops 1 | bytes 1 | tf_op jit(solution)/shard_map/attn_fwd/pallas_call | solution.py:134
  142.0 24.1 %mlp_both.2 = (f32[512,1024]{1,0:T(8,128)}, f32[512,1024]{1,0:T(8,128)}, bf16[4,2,3,656,128]{4,3,2,1,0:T(8,128)(2,1)}, bf16[4,2,3,656,128]{4,3,2,1,0:T(8,128)(2,1)}) custom-call(s32[16]{0:T(128)} %pad_add_fusion.1.perm, s32[4]{0:T(128)} %iota.18.slots, bf16[512,1024]{1,0:T(8,128)(2,1)} %get-tuple-element.357.a2, bf16[512,1024]{1,0:T(8,128)(2,1)} %g.3, ...), custom_call_target="tpu_custom_call" | custom-call | flops 1 | bytes 1 | tf_op jit(solution)/shard_map/mlp_both/pallas_call | solution.py:232
  172.6 26.3 %mlp_both.3 = (bf16[512,1024]{1,0:T(8,128)(2,1)}, f32[512,1024]{1,0:T(8,128)}, bf16[512,1024]{1,0:T(8,128)(2,1)}, bf16[1024,512]{1,0:T(8,128)(2,1)}, f32[1,1024]...) custom-call(s32[16]{0:T(128)} %pad_add_fusion.1.perm, ...), custom_call_target="tpu_custom_call" | custom-call | flops 1 | bytes 1 | tf_op jit(solution)/shard_map/mlp_both/pallas_call | solution.py:232
  203.2 19.0 %attn_bwd.2 = (bf16[4,512,256]{2,1,0:T(8,128)(2,1)}, bf16[4,1024,256]{2,1,0:T(8,128)(2,1)}, bf16[4,1024,256]{2,1,0:T(8,128)(2,1)}) custom-call(s32[16]{0:T(128)} %pad_add_fusion.1.perm, bf16[512,1024]{1,0:T(8,128)(2,1)} %get-tuple-element.431.dres, f32[1024,128]{1,0:T(8,128)} %get-tuple-element.305.cos, f32[1024,128]{1,0:T(8,128)} %get-tuple-element.306.sin, ...), custom_call_target="tpu_custom_call" | custom-call | flops 1 | bytes 1 | tf_op jit(solution)/shard_map/attn_bwd/pallas_call | solution.py:290
  226.4 3.0 fusion.29
  233.4 19.2 %attn_bwd.3 = (bf16[4,512,256]{2,1,0:T(8,128)(2,1)}, bf16[4,1024,256]{2,1,0:T(8,128)(2,1)}, bf16[4,1024,256]{2,1,0:T(8,128)(2,1)}) custom-call(s32[16]{0:T(128)} %pad_add_fusion.1.perm, bf16[512,1024]{1,0:T(8,128)(2,1)} %get-tuple-element.431.dres, ...), custom_call_target="tpu_custom_call", output_to_operand_aliasing={{0}: (26, {}), {1}: (27, {}), {2}: (28, {})} | custom-call | flops 1 | bytes 1 | tf_op jit(solution)/shard_map/attn_bwd/pallas_call | solution.py:290
  256.8 8.3 %collective-permute-done.55 = bf16[2,3,656,128]{3,2,1,0:T(8,128)(2,1)S(1)} collective-permute-done((bf16[2,3,656,128]{3,2,1,0:T(8,128)(2,1)}, bf16[2,3,656,128]{3,2,1,0:T(8,128)(2,1)S(1)}, u32[]{:S(2)}, u32[]{:S(2)}) %collective-permute-start.55) | collective-permute-done | bytes 1007648 | tf_op jit(solution)/shard_map/ppermute | solution.py:439
  271.3 22.6 %attn_grad.1 = (f32[512,1024]{1,0:T(8,128)}, bf16[512,1024]{1,0:T(8,128)(2,1)}, f32[1,1024]{1,0:T(1,128)}, bf16[4,4,4,128,256]{4,3,2,1,0:T(8,128)(2,1)}, bf16[4,4,4,128,256]{4,3,2,1,0:T(8,128)(2,1)}) custom-call(s32[16]{0:T(128)} %pad_add_fusion.1.perm, s32[4]{0:T(128)} %iota.18.slots, bf16[1024,1024]{1,0:T(8,128)(2,1)} %get-tuple-element.448.a1T, ...), custom_call_target="tpu_custom_call" | custom-call | flops 1 | bytes 1 | tf_op jit(solution)/shard_map/attn_grad/pallas_call | solution.py:346
  302.0 2.9 fusion.15
  308.5 3.7 collective-permute-done.67
  313.9 2.6 collective-permute-start.68
  316.6 2.7 collective-permute-done.62
  332.9 2.9 fusion.6.g_in
  335.8 14.6 %soap_mlp.1 = (f32[3,656,128]{2,1,0:T(8,128)}, f32[3,656,128]{2,1,0:T(8,128)}, f32[3,656,128]{2,1,0:T(8,128)}, f32[3,8,128]{2,1,0:T(8,128)}) custom-call(f32[3]{0:T(128)} %pad_maximum_fusion.11.sc, f32[3,656,128]{2,1,0:T(8,128)} %fusion.6.g_in, f32[3,656,128]{2,1,0:T(8,128)} %bitcast.173, f32[3,656,128]{2,1,0:T(8,128)} %bitcast.174, f32[3,128,128]{2,1,0:T(8,128)} %left.2, ...), custom_call_target="tpu_custom_call" | custom-call | flops 1 | bytes 1 | tf_op jit(solution)/shard_map/soap_mlp/pallas_call | solution.py:391
  354.1 5.2 %input_back.1 = bf16[512,1024]{1,0:T(8,128)(2,1)} custom-call(bf16[512,1024]{1,0:T(8,128)(2,1)} %hid.5, f32[512,1024]{1,0:T(8,128)} %get-tuple-element.489.da, f32[512,1024]{1,0:T(8,128)} %get-tuple-element.490.dres, f32[1,1024]{1,0:T(1,128)} %get-tuple-element.274.gain, bf16[512,1024]{1,0:T(8,128)(2,1)} %copy-done.16), custom_call_target="tpu_custom_call" | custom-call | flops 1 | bytes 1 | tf_op jit(solution)/shard_map/input_back/pallas_call | solution.py:429
  364.7 5.0 %collective-permute-done.74 = f32[3,1024]{1,0:T(4,128)S(1)} collective-permute-done((f32[3,1024]{1,0:T(4,128)S(1)}, f32[3,1024]{1,0:T(4,128)S(1)}, u32[]{:S(2)}, u32[]{:S(2)}) %collective-permute-start.74) | collective-permute-done | bytes 12320 | tf_op jit(solution)/shard_map/ppermute | solution.py:767
  372.4 5.0 %collective-permute-done.75 = bf16[4,128,256]{2,1,0:T(8,128)(2,1)S(1)} collective-permute-done((bf16[4,128,256]{2,1,0:T(8,128)(2,1)S(1)}, bf16[4,128,256]{2,1,0:T(8,128)(2,1)S(1)}, u32[]{:S(2)}, u32[]{:S(2)}) %collective-permute-start.75) | collective-permute-done | bytes 262176 | tf_op jit(solution)/shard_map/ppermute | solution.py:451
  381.1 6.0 %soap_attn.1 = (f32[4,128,256]{2,1,0:T(8,128)}, f32[4,128,256]{2,1,0:T(8,128)}, f32[4,128,256]{2,1,0:T(8,128)}, f32[4,8,128]{2,1,0:T(8,128)}) custom-call(f32[3]{0:T(128)} %pad_maximum_fusion.11.sc, f32[4,128,256]{2,1,0:T(8,128)} %fusion.16.g_in, f32[4,128,256]{2,1,0:T(8,128)} %first.1, f32[4,128,256]{2,1,0:T(8,128)} %second.1, f32[4,128,128]{2,1,0:T(8,128)} %left.3, ...), custom_call_target="tpu_custom_call" | custom-call | flops 1 | bytes 1 | tf_op jit(solution)/shard_map/soap_attn/pallas_call | solution.py:391
  (289 shorter events, 133.8 us)
Async XLA Ops:
  20.6 31.8 %collective-permute-start.9 = (bf16[512,1024]{1,0:T(8,128)(2,1)S(1)}, bf16[512,1024]{1,0:T(8,128)(2,1)}, u32[]{:S(2)}, u32[]{:S(2)}) collective-permute-start(bf16[512,1024]{1,0:T(8,128)(2,1)S(1)} %copy-done), channel_id=1, source_target_pairs={{1,0},{0,1},{3,2},{2,3},{5,4},{4,5},{7,6},{6,7},{9,8},{8,9},{11,10... | collective-permute-start | bytes 3145736 | tf_op jit(solution)/shard_map/ppermute | solution.py:579
  31.6 26.6 %collective-permute-start.7 = (bf16[2,4,128,256]{3,2,1,0:T(8,128)(2,1)S(1)}, bf16[2,4,128,256]{3,2,1,0:T(8,128)(2,1)S(1)}, u32[]{:S(2)}, u32[]{:S(2)}) collective-permute-start(bf16[2,4,128,256]{3,2,1,0:T(8,128)(2,1)S(1)} %collective-permute-done.3.rest_1_), channel_id=1, source_target_pairs={{0,16},{4,20},{8,24},{12,28},{16,0},{20,4},{24,8},{28,12},{1,17},{... | collective-permute-start | bytes 1572872 | tf_op jit(solution)/shard_map/ppermute | solution.py:439
  32.8 25.4 %collective-permute-start.8 = (bf16[3,656,128]{2,1,0:T(8,128)(2,1)}, bf16[3,656,128]{2,1,0:T(8,128)(2,1)}, u32[]{:S(2)}, u32[]{:S(2)}) collective-permute-start(bf16[3,656,128]{2,1,0:T(8,128)(2,1)} %copy-done.19), channel_id=1, source_target_pairs={{0,8},{4,12},{8,0},{12,4},{16,24},{20,28},{24,16},{28,20},{1,9},{5... | collective-permute-start | bytes 1511432 | tf_op jit(solution)/shard_map/ppermute | solution.py:439
  34.3 23.9 %collective-permute-start.10 = (bf16[4,128,256]{2,1,0:T(8,128)(2,1)}, bf16[4,128,256]{2,1,0:T(8,128)(2,1)}, u32[]{:S(2)}, u32[]{:S(2)}) collective-permute-start(bf16[4,128,256]{2,1,0:T(8,128)(2,1)} %collective-permute-done), channel_id=1, source_target_pairs={{0,2},{2,3},{3,1},{1,0},{4,6},{6,7},{7,5},{5,4},{8,10},{10,11},{11... | collective-permute-start | bytes 786440 | tf_op jit(solution)/shard_map/ppermute | solution.py:458
  79.2 25.8 %collective-permute-start.22 = (bf16[2,4,128,256]{3,2,1,0:T(8,128)(2,1)}, bf16[2,4,128,256]{3,2,1,0:T(8,128)(2,1)}, u32[]{:S(2)}, u32[]{:S(2)}) collective-permute-start(bf16[2,4,128,256]{3,2,1,0:T(8,128)(2,1)} %collective-permute-done.19.rest_2_.rest_10_), channel_id=1, source_target_pairs={{0,8},{4,12},{8,0},{12,4},{16,24},{20,28},{24,16},{28,20},{1,9},{5... | collective-permute-start | bytes 1572872 | tf_op jit(solution)/shard_map/ppermute | solution.py:439
  79.7 23.4 %collective-permute-start.25 = (bf16[3,656,128]{2,1,0:T(8,128)(2,1)}, bf16[3,656,128]{2,1,0:T(8,128)(2,1)}, u32[]{:S(2)}, u32[]{:S(2)}) collective-permute-start(bf16[3,656,128]{2,1,0:T(8,128)(2,1)} %bitcast.1), channel_id=1, source_target_pairs={{0,1},{2,0},{3,2},{1,3},{4,5},{6,4},{7,6},{5,7},{8,9},{10,8},{11,1... | collective-permute-start | bytes 1511432 | tf_op jit(solution)/shard_map/ppermute | solution.py:458
  81.7 23.3 %collective-permute-start.26 = (bf16[3,656,128]{2,1,0:T(8,128)(2,1)}, bf16[3,656,128]{2,1,0:T(8,128)(2,1)}, u32[]{:S(2)}, u32[]{:S(2)}) collective-permute-start(bf16[3,656,128]{2,1,0:T(8,128)(2,1)} %collective-permute-done.16), channel_id=1, source_target_pairs={{0,2},{2,3},{3,1},{1,0},{4,6},{6,7},{7,5},{5,4},{8,10},{10,11},{11... | collective-permute-start | bytes 1511432 | tf_op jit(solution)/shard_map/ppermute | solution.py:458
  108.7 24.1 %collective-permute-start.32 = (bf16[3,656,128]{2,1,0:T(8,128)(2,1)}, bf16[3,656,128]{2,1,0:T(8,128)(2,1)}, u32[]{:S(2)}, u32[]{:S(2)}) collective-permute-start(bf16[3,656,128]{2,1,0:T(8,128)(2,1)} %collective-permute-done.24), channel_id=1, source_target_pairs={{0,8},{4,12},{8,0},{12,4},{16,24},{20,28},{24,16},{28,20},{1,9},{5... | collective-permute-start | bytes 1511432 | tf_op jit(solution)/shard_map/ppermute | solution.py:439
  135.5 30.6 %collective-permute-start.41 = (bf16[3,656,128]{2,1,0:T(8,128)(2,1)}, bf16[3,656,128]{2,1,0:T(8,128)(2,1)S(1)}, u32[]{:S(2)}, u32[]{:S(2)}) collective-permute-start(bf16[3,656,128]{2,1,0:T(8,128)(2,1)} %collective-permute-done.25), channel_id=1, source_target_pairs={{0,4},{4,0},{8,12},{12,8},{16,20},{20,16},{24,28},{28,24},{1,5},{5... | collective-permute-start | bytes 1511432 | tf_op jit(solution)/shard_map/ppermute | solution.py:439
  138.7 27.4 %collective-permute-start.38 = (bf16[3,656,128]{2,1,0:T(8,128)(2,1)}, bf16[3,656,128]{2,1,0:T(8,128)(2,1)S(1)}, u32[]{:S(2)}, u32[]{:S(2)}) collective-permute-start(bf16[3,656,128]{2,1,0:T(8,128)(2,1)} %collective-permute-done.26), channel_id=1, source_target_pairs={{0,8},{4,12},{8,0},{12,4},{16,24},{20,28},{24,16},{28,20},{1,9},{5... | collective-permute-start | bytes 1511432 | tf_op jit(solution)/shard_map/ppermute | solution.py:439
  139.3 26.9 %collective-permute-start.39 = (bf16[3,656,128]{2,1,0:T(8,128)(2,1)S(1)}, bf16[3,656,128]{2,1,0:T(8,128)(2,1)S(1)}, u32[]{:S(2)}, u32[]{:S(2)}) collective-permute-start(bf16[3,656,128]{2,1,0:T(8,128)(2,1)S(1)} %collective-permute-done.33), channel_id=1, source_target_pairs={{0,8},{4,12},{8,0},{12,4},{16,24},{20,28},{24,16},{28,20},{1,9},{5... | collective-permute-start | bytes 1511432 | tf_op jit(solution)/shard_map/ppermute | solution.py:439
  140.8 25.4 %collective-permute-start.42 = (bf16[3,656,128]{2,1,0:T(8,128)(2,1)S(1)}, bf16[3,656,128]{2,1,0:T(8,128)(2,1)}, u32[]{:S(2)}, u32[]{:S(2)}) collective-permute-start(bf16[3,656,128]{2,1,0:T(8,128)(2,1)S(1)} %collective-permute-done.30), channel_id=1, source_target_pairs={{0,4},{4,0},{8,12},{12,8},{16,20},{20,16},{24,28},{28,24},{1,5},{5... | collective-permute-start | bytes 1511432 | tf_op jit(solution)/shard_map/ppermute | solution.py:439
  140.8 25.4 %collective-permute-start.40 = (bf16[3,656,128]{2,1,0:T(8,128)(2,1)S(1)}, bf16[3,656,128]{2,1,0:T(8,128)(2,1)}, u32[]{:S(2)}, u32[]{:S(2)}) collective-permute-start(bf16[3,656,128]{2,1,0:T(8,128)(2,1)S(1)} %collective-permute-done.30), channel_id=1, source_target_pairs={{0,16},{4,20},{8,24},{12,28},{16,0},{20,4},{24,8},{28,12},{1,17},{... | collective-permute-start | bytes 1511432 | tf_op jit(solution)/shard_map/ppermute | solution.py:439
  171.7 27.1 %collective-permute-start.49 = (bf16[4,2,3,656,128]{4,3,2,1,0:T(8,128)(2,1)}, bf16[4,2,3,656,128]{4,3,2,1,0:T(8,128)(2,1)}, u32[]{:S(2)}, u32[]{:S(2)}) collective-permute-start(bf16[4,2,3,656,128]{4,3,2,1,0:T(8,128)(2,1)} %get-tuple-element.392), channel_id=1, source_target_pairs={{0,4},{4,0},{8,12},{12,8},{16,20},{20,16},{24,28},{28,24},{1,5},{5... | collective-permute-start | bytes 12091400 | tf_op jit(solution)/shard_map/ppermute | solution.py:439
  198.9 23.3 %collective-permute-start.52 = (bf16[4,2,3,656,128]{4,3,2,1,0:T(8,128)(2,1)}, bf16[4,2,3,656,128]{4,3,2,1,0:T(8,128)(2,1)}, u32[]{:S(2)}, u32[]{:S(2)}) collective-permute-start(bf16[4,2,3,656,128]{4,3,2,1,0:T(8,128)(2,1)} %get-tuple-element.417), channel_id=1, source_target_pairs={{0,4},{4,0},{8,12},{12,8},{16,20},{20,16},{24,28},{28,24},{1,5},{5... | collective-permute-start | bytes 12091400 | tf_op jit(solution)/shard_map/ppermute | solution.py:439
  229.4 23.3 %collective-permute-start.53 = (bf16[1,3,656,128]{3,2,1,0:T(8,128)(2,1)}, bf16[1,3,656,128]{3,2,1,0:T(8,128)(2,1)S(1)}, u32[]{:S(2)}, u32[]{:S(2)}) collective-permute-start(bf16[1,3,656,128]{3,2,1,0:T(8,128)(2,1)} %get-tuple-element.429), channel_id=1, source_target_pairs={{0,16},{4,20},{8,24},{12,28},{16,0},{20,4},{24,8},{28,12},{1,17},{... | collective-permute-start | bytes 1511432 | tf_op jit(solution)/shard_map/ppermute | solution.py:439
  232.0 33.2 %collective-permute-start.55 = (bf16[2,3,656,128]{3,2,1,0:T(8,128)(2,1)}, bf16[2,3,656,128]{3,2,1,0:T(8,128)(2,1)S(1)}, u32[]{:S(2)}, u32[]{:S(2)}) collective-permute-start(bf16[2,3,656,128]{3,2,1,0:T(8,128)(2,1)} %pad_maximum_fusion.2), channel_id=1, source_target_pairs={{0,8},{4,12},{8,0},{12,4},{16,24},{20,28},{24,16},{28,20},{1,9},{5... | collective-permute-start | bytes 3022856 | tf_op jit(solution)/shard_map/ppermute | solution.py:439
  232.5 32.7 %collective-permute-start.56 = (bf16[2,3,656,128]{3,2,1,0:T(8,128)(2,1)}, bf16[2,3,656,128]{3,2,1,0:T(8,128)(2,1)S(1)}, u32[]{:S(2)}, u32[]{:S(2)}) collective-permute-start(bf16[2,3,656,128]{3,2,1,0:T(8,128)(2,1)} %pad_maximum_fusion.3), channel_id=1, source_target_pairs={{0,16},{4,20},{8,24},{12,28},{16,0},{20,4},{24,8},{28,12},{1,17},{... | collective-permute-start | bytes 3022856 | tf_op jit(solution)/shard_map/ppermute | solution.py:439
  265.2 28.9 %collective-permute-start.57 = (bf16[2,3,656,128]{3,2,1,0:T(8,128)(2,1)}, bf16[2,3,656,128]{3,2,1,0:T(8,128)(2,1)S(1)}, u32[]{:S(2)}, u32[]{:S(2)}) collective-permute-start(bf16[2,3,656,128]{3,2,1,0:T(8,128)(2,1)} %pad_maximum_fusion.4), channel_id=1, source_target_pairs={{0,8},{4,12},{8,0},{12,4},{16,24},{20,28},{24,16},{28,20},{1,9},{5... | collective-permute-start | bytes 3022856 | tf_op jit(solution)/shard_map/ppermute | solution.py:439
  266.8 27.3 %collective-permute-start.58 = (bf16[2,3,656,128]{3,2,1,0:T(8,128)(2,1)}, bf16[2,3,656,128]{3,2,1,0:T(8,128)(2,1)}, u32[]{:S(2)}, u32[]{:S(2)}) collective-permute-start(bf16[2,3,656,128]{3,2,1,0:T(8,128)(2,1)} %pad_maximum_fusion.5), channel_id=1, source_target_pairs={{0,16},{4,20},{8,24},{12,28},{16,0},{20,4},{24,8},{28,12},{1,17},{... | collective-permute-start | bytes 3022856 | tf_op jit(solution)/shard_map/ppermute | solution.py:439
  269.2 24.8 %collective-permute-start.59 = (bf16[3,656,128]{2,1,0:T(8,128)(2,1)S(1)}, bf16[3,656,128]{2,1,0:T(8,128)(2,1)}, u32[]{:S(2)}, u32[]{:S(2)}) collective-permute-start(bf16[3,656,128]{2,1,0:T(8,128)(2,1)S(1)} %fusion.7), channel_id=1, source_target_pairs={{0,2},{2,3},{3,1},{1,0},{4,6},{6,7},{7,5},{5,4},{8,10},{10,11},{11... | collective-permute-start | bytes 1511432 | tf_op jit(solution)/shard_map/ppermute | solution.py:451
  323.5 26.8 %collective-permute-start.65 = (bf16[4,4,128,256]{3,2,1,0:T(8,128)(2,1)}, bf16[4,4,128,256]{3,2,1,0:T(8,128)(2,1)S(1)}, u32[]{:S(2)}, u32[]{:S(2)}) collective-permute-start(bf16[4,4,128,256]{3,2,1,0:T(8,128)(2,1)} %pad_maximum_fusion), channel_id=1, source_target_pairs={{0,8},{4,12},{8,0},{12,4},{16,24},{20,28},{24,16},{28,20},{1,9},{5... | collective-permute-start | bytes 3145736 | tf_op jit(solution)/shard_map/ppermute | solution.py:439
  324.9 25.5 %collective-permute-start.66 = (bf16[4,4,128,256]{3,2,1,0:T(8,128)(2,1)}, bf16[4,4,128,256]{3,2,1,0:T(8,128)(2,1)S(1)}, u32[]{:S(2)}, u32[]{:S(2)}) collective-permute-start(bf16[4,4,128,256]{3,2,1,0:T(8,128)(2,1)} %pad_maximum_fusion.1), channel_id=1, source_target_pairs={{0,16},{4,20},{8,24},{12,28},{16,0},{20,4},{24,8},{28,12},{1,17},{... | collective-permute-start | bytes 3145736 | tf_op jit(solution)/shard_map/ppermute | solution.py:439
  326.7 24.9 %collective-permute-start.70 = (bf16[512,1024]{1,0:T(8,128)(2,1)}, bf16[512,1024]{1,0:T(8,128)(2,1)S(1)}, u32[]{:S(2)}, u32[]{:S(2)}) collective-permute-start(bf16[512,1024]{1,0:T(8,128)(2,1)} %get-tuple-element.487), channel_id=1, source_target_pairs={{0,1},{1,0},{2,3},{3,2},{4,5},{5,4},{6,7},{7,6},{8,9},{9,8},{10,11... | collective-permute-start | bytes 3145736 | tf_op jit(solution)/shard_map/ppermute | solution.py:763
  (98 other events, 1292.6 us)

commit v7 on v6

--- a/solution.py
+++ b/solution.py
@@ -531,12 +531,12 @@
 
 
 def side_sends(even, core, from_y, from_x, half):
-    to_x = jnp.concatenate(
-        [add_all(even[1, :half], core[1, :half], from_y), add_all(even[1, half:], core[1, half:])]
-    ).astype(BF)
-    to_y = jnp.concatenate(
-        [add_all(even[2, :half], core[2, :half]), add_all(even[2, half:], core[2, half:], from_x)]
-    ).astype(BF)
+    def widen(part, before):
+        after_it = even.shape[1] - before - part.shape[0]
+        return jnp.pad(part.astype(F32), [(before, after_it)] + [(0, 0)] * (part.ndim - 1))
+
+    to_x = (add_all(even[1], core[1]) + widen(from_y, 0)).astype(BF)
+    to_y = (add_all(even[2], core[2]) + widen(from_x, half)).astype(BF)
     return to_x, to_y
 
 

time: 396 us -> 399 us (level)
  waiting for transfers between devices: 79.5 us -> 90.8 us
  starting transfers between devices: 69.9 us -> 65.6 us
  other arithmetic: 48.9 us -> 44.7 us
    convert_element_type x0 -> x6, other arithmetic: none -> 16.8 us  [the longest x3 10.5 us: side_sends(): to_y = (add_all(even[2], core[2]) + widen(from_x, half)).astype(BF)]
    add x3 -> x0, other arithmetic: 8.48 us -> none  [add_all(): total = total + value.astype(F32)]
    concatenate x6 -> x0, other arithmetic: 6.35 us -> none  [the longest x3 3.21 us: side_sends(): jnp.concatenate([add_all(even[2, :half], core[2, :half]), add_all(even[2,...]
    ppermute x6, waiting for transfers between devices: 9.02 us -> 15.4 us  [to_ring_succ(): lax.ppermute(value, 'tensor', [(ring[p], ring[(p + 1) % shards]) for p in...]
    another operation x3 -> x0, other arithmetic: 6.17 us -> none
    ppermute x60, waiting for transfers between devices: 37.7 us -> 42 us  [swap_dp(): return lax.ppermute(value, 'dp', [(i, i ^ bit) for i in range(owners)])]
  transfers between devices with their start and end apart: 76 -> 76, of which waited for: 32 -> 34; matrix products, arithmetic and copies ran while one was open for 10% -> 9% of each run, Pallas kernels for 45% -> 44%
where the time goes in v7:
time: 399 us; the launch traced here: 392 us
  Pallas kernels  180 us (45%)
  waiting for transfers between devices  90.8 us (23%)
  starting transfers between devices  65.6 us (16%)
  other arithmetic  44.7 us (11%)
  local copies, waits for them, and re-layouts  6.39 us (2%)
  between operations  5.02 us (1%)
    pallas_call x2, Pallas kernels, mlp(): pl.pallas_call(functools.partial(mlp_kernel, T=T, D=D, HC=HC, R=R, metas=...  50.5 us
    ppermute x60, waiting for transfers between devices, swap_dp(): return lax.ppermute(value, 'dp', [(i, i ^ bit) for i in range(owners)])  42 us
    ppermute x60, starting transfers between devices, swap_dp(): return lax.ppermute(value, 'dp', [(i, i ^ bit) for i in range(owners)])  39.2 us
    pallas_call x2, Pallas kernels, bwd_attn(): pl.pallas_call(functools.partial(bwd_attn_kernel, T=T, KV=KV, C=C, metas=...  38.2 us
    pallas_call x2, Pallas kernels, fwd_attn(): pl.pallas_call(functools.partial(fwd_attn_kernel, T=T, KV=KV, C=C, metas=...  36.8 us
    pallas_call x1, Pallas kernels, grad_attn(): pl.pallas_call(functools.partial(grad_attn_kernel, T=T, KV=KV, C=C, R=R,...  22.6 us
    pallas_call x2, Pallas kernels, soap(): pl.pallas_call(functools.partial(soap_kernel, turned=turned, each=each),...  20.6 us
    ppermute x1, waiting for transfers between devices, from_peer(): return lax.ppermute(value, 'tensor', pairs)  15.4 us
  transfers between devices with their start and end apart: 76, of which 34 were waited for; matrix products, arithmetic and copies ran while one was open for 9% of the time, Pallas kernels for 44%

profile of v7, /device:TPU:0, one launch (start us, length us, event | category | flops | bytes accessed | tf_op | source)
XLA Modules:
  0.0 392.2 jit_solution(5994904280297175357)
XLA Ops:
  0.6 3.0 collective-permute-start.2
  24.7 5.8 %collective-permute-done.4.rest_2_ = bf16[2,4,128,256]{3,2,1,0:T(8,128)(2,1)S(1)} collective-permute-done((bf16[2,4,128,256]{3,2,1,0:T(8,128)(2,1)S(1)}, bf16[2,4,128,256]{3,2,1,0:T(8,128)(2,1)S(1)}, u32[]{:S(2)}, u32[]{:S(2)}) %collective-permute-start.4) | collective-permute-done | bytes 524320 | tf_op jit(solution)/shard_map/ppermute | solution.py:439
  36.9 15.4 %collective-permute-done.9.far = bf16[512,1024]{1,0:T(8,128)(2,1)} collective-permute-done((bf16[512,1024]{1,0:T(8,128)(2,1)S(1)}, bf16[512,1024]{1,0:T(8,128)(2,1)}, u32[]{:S(2)}, u32[]{:S(2)}) %collective-permute-start.9) | collective-permute-done | bytes 1048608 | tf_op jit(solution)/shard_map/ppermute | solution.py:579
  52.3 5.8 %norm_first.1 = (bf16[1024,1024]{1,0:T(8,128)(2,1)}, bf16[1024,1024]{1,0:T(8,128)(2,1)}, bf16[1024,1024]{1,0:T(8,128)(2,1)}) custom-call(bf16[512,1024]{1,0:T(8,128)(2,1)} %hid.5, bf16[512,1024]{1,0:T(8,128)(2,1)} %collective-permute-done.9.far, f32[1,1024]{1,0:T(1,128)} %get-tuple-element.274.gain), custom_call_target="tpu_custom_call" | custom-call | flops 1 | bytes 1 | tf_op jit(solution)/shard_map/norm_first/pallas_call | solution.py:411
  63.9 10.4 %collective-permute-done.16 = bf16[3,656,128]{2,1,0:T(8,128)(2,1)} collective-permute-done((bf16[3,656,128]{2,1,0:T(8,128)(2,1)}, bf16[3,656,128]{2,1,0:T(8,128)(2,1)}, u32[]{:S(2)}, u32[]{:S(2)}) %collective-permute-start.16) | collective-permute-done | bytes 503840 | tf_op jit(solution)/shard_map/ppermute | solution.py:458
  86.4 16.8 %attn_fwd.2 = (bf16[4,512,256]{2,1,0:T(8,128)(2,1)}, bf16[4,1024,256]{2,1,0:T(8,128)(2,1)}, bf16[4,1024,256]{2,1,0:T(8,128)(2,1)}, bf16[4,512,256]{2,1,0:T(8,128...) custom-call(s32[16]{0:T(128)} %pad_add_fusion.1.perm, bf16[1024,1024]{1,0:T(8,128)(2,1)} %get-tuple-element.303.a1, ...), custom_call_target="tpu_custom_call" | custom-call | flops 1 | bytes 1 | tf_op jit(solution)/shard_map/attn_fwd/pallas_call | solution.py:134
  112.7 20.1 %attn_fwd.3 = (bf16[4,512,256]{2,1,0:T(8,128)(2,1)}, bf16[4,1024,256]{2,1,0:T(8,128)(2,1)}, bf16[4,1024,256]{2,1,0:T(8,128)(2,1)}, bf16[4,512,256]{2,1,0:T(8,128...) custom-call(s32[16]{0:T(128)} %pad_add_fusion.1.perm, ...), custom_call_target="tpu_custom_call", output_to_operand_aliasing={{0}: (18, {}), {1}: (19, {}), {2}: (20, {}), {3}: (21, {}),... | custom-call | flops 1 | bytes 1 | tf_op jit(solution)/shard_map/attn_fwd/pallas_call | solution.py:134
  141.9 24.2 %mlp_both.2 = (f32[512,1024]{1,0:T(8,128)}, f32[512,1024]{1,0:T(8,128)}, bf16[4,2,3,656,128]{4,3,2,1,0:T(8,128)(2,1)}, bf16[4,2,3,656,128]{4,3,2,1,0:T(8,128)(2,1)}) custom-call(s32[16]{0:T(128)} %pad_add_fusion.1.perm, s32[4]{0:T(128)} %iota.18.slots, bf16[512,1024]{1,0:T(8,128)(2,1)} %get-tuple-element.357.a2, bf16[512,1024]{1,0:T(8,128)(2,1)} %g.3, ...), custom_call_target="tpu_custom_call" | custom-call | flops 1 | bytes 1 | tf_op jit(solution)/shard_map/mlp_both/pallas_call | solution.py:232
  172.6 26.3 %mlp_both.3 = (bf16[512,1024]{1,0:T(8,128)(2,1)}, f32[512,1024]{1,0:T(8,128)}, bf16[512,1024]{1,0:T(8,128)(2,1)}, bf16[1024,512]{1,0:T(8,128)(2,1)}, f32[1,1024]...) custom-call(s32[16]{0:T(128)} %pad_add_fusion.1.perm, ...), custom_call_target="tpu_custom_call" | custom-call | flops 1 | bytes 1 | tf_op jit(solution)/shard_map/mlp_both/pallas_call | solution.py:232
  202.4 19.0 %attn_bwd.2 = (bf16[4,512,256]{2,1,0:T(8,128)(2,1)}, bf16[4,1024,256]{2,1,0:T(8,128)(2,1)}, bf16[4,1024,256]{2,1,0:T(8,128)(2,1)}) custom-call(s32[16]{0:T(128)} %pad_add_fusion.1.perm, bf16[512,1024]{1,0:T(8,128)(2,1)} %get-tuple-element.431.dres, f32[1024,128]{1,0:T(8,128)} %get-tuple-element.305.cos, f32[1024,128]{1,0:T(8,128)} %get-tuple-element.306.sin, ...), custom_call_target="tpu_custom_call" | custom-call | flops 1 | bytes 1 | tf_op jit(solution)/shard_map/attn_bwd/pallas_call | solution.py:290
  221.4 3.7 fusion.3
  231.7 19.3 %attn_bwd.3 = (bf16[4,512,256]{2,1,0:T(8,128)(2,1)}, bf16[4,1024,256]{2,1,0:T(8,128)(2,1)}, bf16[4,1024,256]{2,1,0:T(8,128)(2,1)}) custom-call(s32[16]{0:T(128)} %pad_add_fusion.1.perm, bf16[512,1024]{1,0:T(8,128)(2,1)} %get-tuple-element.431.dres, ...), custom_call_target="tpu_custom_call", output_to_operand_aliasing={{0}: (26, {}), {1}: (27, {}), {2}: (28, {})} | custom-call | flops 1 | bytes 1 | tf_op jit(solution)/shard_map/attn_bwd/pallas_call | solution.py:290
  251.0 12.8 %collective-permute-done.53 = bf16[1,3,656,128]{3,2,1,0:T(8,128)(2,1)} collective-permute-done((bf16[1,3,656,128]{3,2,1,0:T(8,128)(2,1)}, bf16[1,3,656,128]{3,2,1,0:T(8,128)(2,1)}, u32[]{:S(2)}, u32[]{:S(2)}) %collective-permute-start.53) | collective-permute-done | bytes 503840 | tf_op jit(solution)/shard_map/ppermute | solution.py:439
  263.8 4.3 %fusion.2 = (bf16[2,3,656,128]{3,2,1,0:T(8,128)(2,1)}, bf16[2,3,656,128]{3,2,1,0:T(8,128)(2,1)}) fusion(bf16[1,3,656,128]{3,2,1,0:T(8,128)(2,1)} %collective-permute-done.54, bf16[4,2,3,656,128]{4,3,2,1,0:T(8,128)(2,1)} %collective-permute-done.52, bf16[4,2,3,656,128]{4,3,2,1,0:T(8,128)(2,1)} %get-tuple-element.411, ...), kind=kLoop, calls=%fused_computation.5 | loop fusion | flops 6045696 | bytes 7053312 | tf_op jit(solution)/shard_map/convert_element_type | solution.py:539
  273.9 22.6 %attn_grad.1 = (f32[512,1024]{1,0:T(8,128)}, bf16[512,1024]{1,0:T(8,128)(2,1)}, f32[1,1024]{1,0:T(1,128)}, bf16[4,4,4,128,256]{4,3,2,1,0:T(8,128)(2,1)}, bf16[4,4,4,128,256]{4,3,2,1,0:T(8,128)(2,1)}) custom-call(s32[16]{0:T(128)} %pad_add_fusion.1.perm, s32[4]{0:T(128)} %iota.18.slots, bf16[1024,1024]{1,0:T(8,128)(2,1)} %get-tuple-element.448.a1T, ...), custom_call_target="tpu_custom_call" | custom-call | flops 1 | bytes 1 | tf_op jit(solution)/shard_map/attn_grad/pallas_call | solution.py:346
  308.7 6.1 %collective-permute-done.67 = bf16[3,656,128]{2,1,0:T(8,128)(2,1)S(1)} collective-permute-done((bf16[3,656,128]{2,1,0:T(8,128)(2,1)S(1)}, bf16[3,656,128]{2,1,0:T(8,128)(2,1)S(1)}, u32[]{:S(2)}, u32[]{:S(2)}) %collective-permute-start.67) | collective-permute-done | bytes 503840 | tf_op jit(solution)/shard_map/ppermute | solution.py:451
  325.1 4.1 %collective-permute-done.68 = bf16[3,656,128]{2,1,0:T(8,128)(2,1)} collective-permute-done((bf16[3,656,128]{2,1,0:T(8,128)(2,1)S(1)}, bf16[3,656,128]{2,1,0:T(8,128)(2,1)}, u32[]{:S(2)}, u32[]{:S(2)}) %collective-permute-start.68) | collective-permute-done | bytes 503840 | tf_op jit(solution)/shard_map/ppermute | solution.py:451
  334.8 2.9 fusion.10.g_in
  337.6 14.6 %soap_mlp.1 = (f32[3,656,128]{2,1,0:T(8,128)}, f32[3,656,128]{2,1,0:T(8,128)}, f32[3,656,128]{2,1,0:T(8,128)}, f32[3,8,128]{2,1,0:T(8,128)}) custom-call(f32[3]{0:T(128)} %pad_maximum_fusion.5.sc, f32[3,656,128]{2,1,0:T(8,128)} %fusion.10.g_in, f32[3,656,128]{2,1,0:T(8,128)} %bitcast.161, f32[3,656,128]{2,1,0:T(8,128)} %bitcast.162, f32[3,128,128]{2,1,0:T(8,128)} %left.2, ...), custom_call_target="tpu_custom_call" | custom-call | flops 1 | bytes 1 | tf_op jit(solution)/shard_map/soap_mlp/pallas_call | solution.py:391
  353.6 2.7 collective-permute-start.71
  356.4 5.2 %input_back.1 = bf16[512,1024]{1,0:T(8,128)(2,1)} custom-call(bf16[512,1024]{1,0:T(8,128)(2,1)} %hid.5, f32[512,1024]{1,0:T(8,128)} %get-tuple-element.489.da, f32[512,1024]{1,0:T(8,128)} %get-tuple-element.490.dres, f32[1,1024]{1,0:T(1,128)} %get-tuple-element.274.gain, bf16[512,1024]{1,0:T(8,128)(2,1)} %copy-done.17), custom_call_target="tpu_custom_call" | custom-call | flops 1 | bytes 1 | tf_op jit(solution)/shard_map/input_back/pallas_call | solution.py:429
  366.4 5.8 %collective-permute-done.74 = f32[3,1024]{1,0:T(4,128)S(1)} collective-permute-done((f32[3,1024]{1,0:T(4,128)S(1)}, f32[3,1024]{1,0:T(4,128)S(1)}, u32[]{:S(2)}, u32[]{:S(2)}) %collective-permute-start.74) | collective-permute-done | bytes 12320 | tf_op jit(solution)/shard_map/ppermute | solution.py:767
  374.8 5.2 %collective-permute-done.75 = bf16[4,128,256]{2,1,0:T(8,128)(2,1)S(1)} collective-permute-done((bf16[4,128,256]{2,1,0:T(8,128)(2,1)S(1)}, bf16[4,128,256]{2,1,0:T(8,128)(2,1)S(1)}, u32[]{:S(2)}, u32[]{:S(2)}) %collective-permute-start.75) | collective-permute-done | bytes 262176 | tf_op jit(solution)/shard_map/ppermute | solution.py:451
  383.9 6.0 %soap_attn.1 = (f32[4,128,256]{2,1,0:T(8,128)}, f32[4,128,256]{2,1,0:T(8,128)}, f32[4,128,256]{2,1,0:T(8,128)}, f32[4,8,128]{2,1,0:T(8,128)}) custom-call(f32[3]{0:T(128)} %pad_maximum_fusion.5.sc, f32[4,128,256]{2,1,0:T(8,128)} %fusion.14.g_in, f32[4,128,256]{2,1,0:T(8,128)} %first.1, f32[4,128,256]{2,1,0:T(8,128)} %second.1, f32[4,128,128]{2,1,0:T(8,128)} %left.3, ...), custom_call_target="tpu_custom_call" | custom-call | flops 1 | bytes 1 | tf_op jit(solution)/shard_map/soap_attn/pallas_call | solution.py:391
  (287 shorter events, 125.0 us)
Async XLA Ops:
  20.5 31.8 %collective-permute-start.9 = (bf16[512,1024]{1,0:T(8,128)(2,1)S(1)}, bf16[512,1024]{1,0:T(8,128)(2,1)}, u32[]{:S(2)}, u32[]{:S(2)}) collective-permute-start(bf16[512,1024]{1,0:T(8,128)(2,1)S(1)} %copy-done), channel_id=1, source_target_pairs={{1,0},{0,1},{3,2},{2,3},{5,4},{4,5},{7,6},{6,7},{9,8},{8,9},{11,10... | collective-permute-start | bytes 3145736 | tf_op jit(solution)/shard_map/ppermute | solution.py:579
  31.5 26.6 %collective-permute-start.7 = (bf16[2,4,128,256]{3,2,1,0:T(8,128)(2,1)S(1)}, bf16[2,4,128,256]{3,2,1,0:T(8,128)(2,1)S(1)}, u32[]{:S(2)}, u32[]{:S(2)}) collective-permute-start(bf16[2,4,128,256]{3,2,1,0:T(8,128)(2,1)S(1)} %collective-permute-done.3.rest_1_), channel_id=1, source_target_pairs={{0,16},{4,20},{8,24},{12,28},{16,0},{20,4},{24,8},{28,12},{1,17},{... | collective-permute-start | bytes 1572872 | tf_op jit(solution)/shard_map/ppermute | solution.py:439
  32.8 25.4 %collective-permute-start.8 = (bf16[3,656,128]{2,1,0:T(8,128)(2,1)}, bf16[3,656,128]{2,1,0:T(8,128)(2,1)}, u32[]{:S(2)}, u32[]{:S(2)}) collective-permute-start(bf16[3,656,128]{2,1,0:T(8,128)(2,1)} %copy-done.20), channel_id=1, source_target_pairs={{0,8},{4,12},{8,0},{12,4},{16,24},{20,28},{24,16},{28,20},{1,9},{5... | collective-permute-start | bytes 1511432 | tf_op jit(solution)/shard_map/ppermute | solution.py:439
  34.3 23.9 %collective-permute-start.10 = (bf16[4,128,256]{2,1,0:T(8,128)(2,1)}, bf16[4,128,256]{2,1,0:T(8,128)(2,1)}, u32[]{:S(2)}, u32[]{:S(2)}) collective-permute-start(bf16[4,128,256]{2,1,0:T(8,128)(2,1)} %collective-permute-done), channel_id=1, source_target_pairs={{0,2},{2,3},{3,1},{1,0},{4,6},{6,7},{7,5},{5,4},{8,10},{10,11},{11... | collective-permute-start | bytes 786440 | tf_op jit(solution)/shard_map/ppermute | solution.py:458
  79.1 25.8 %collective-permute-start.22 = (bf16[2,4,128,256]{3,2,1,0:T(8,128)(2,1)}, bf16[2,4,128,256]{3,2,1,0:T(8,128)(2,1)}, u32[]{:S(2)}, u32[]{:S(2)}) collective-permute-start(bf16[2,4,128,256]{3,2,1,0:T(8,128)(2,1)} %collective-permute-done.19.rest_2_.rest_10_), channel_id=1, source_target_pairs={{0,8},{4,12},{8,0},{12,4},{16,24},{20,28},{24,16},{28,20},{1,9},{5... | collective-permute-start | bytes 1572872 | tf_op jit(solution)/shard_map/ppermute | solution.py:439
  79.7 23.5 %collective-permute-start.25 = (bf16[3,656,128]{2,1,0:T(8,128)(2,1)}, bf16[3,656,128]{2,1,0:T(8,128)(2,1)}, u32[]{:S(2)}, u32[]{:S(2)}) collective-permute-start(bf16[3,656,128]{2,1,0:T(8,128)(2,1)} %bitcast.1), channel_id=1, source_target_pairs={{0,1},{2,0},{3,2},{1,3},{4,5},{6,4},{7,6},{5,7},{8,9},{10,8},{11,1... | collective-permute-start | bytes 1511432 | tf_op jit(solution)/shard_map/ppermute | solution.py:458
  81.6 23.3 %collective-permute-start.26 = (bf16[3,656,128]{2,1,0:T(8,128)(2,1)}, bf16[3,656,128]{2,1,0:T(8,128)(2,1)}, u32[]{:S(2)}, u32[]{:S(2)}) collective-permute-start(bf16[3,656,128]{2,1,0:T(8,128)(2,1)} %collective-permute-done.16), channel_id=1, source_target_pairs={{0,2},{2,3},{3,1},{1,0},{4,6},{6,7},{7,5},{5,4},{8,10},{10,11},{11... | collective-permute-start | bytes 1511432 | tf_op jit(solution)/shard_map/ppermute | solution.py:458
  108.6 24.1 %collective-permute-start.32 = (bf16[3,656,128]{2,1,0:T(8,128)(2,1)}, bf16[3,656,128]{2,1,0:T(8,128)(2,1)}, u32[]{:S(2)}, u32[]{:S(2)}) collective-permute-start(bf16[3,656,128]{2,1,0:T(8,128)(2,1)} %collective-permute-done.24), channel_id=1, source_target_pairs={{0,8},{4,12},{8,0},{12,4},{16,24},{20,28},{24,16},{28,20},{1,9},{5... | collective-permute-start | bytes 1511432 | tf_op jit(solution)/shard_map/ppermute | solution.py:439
  135.5 30.6 %collective-permute-start.41 = (bf16[3,656,128]{2,1,0:T(8,128)(2,1)}, bf16[3,656,128]{2,1,0:T(8,128)(2,1)S(1)}, u32[]{:S(2)}, u32[]{:S(2)}) collective-permute-start(bf16[3,656,128]{2,1,0:T(8,128)(2,1)} %collective-permute-done.25), channel_id=1, source_target_pairs={{0,4},{4,0},{8,12},{12,8},{16,20},{20,16},{24,28},{28,24},{1,5},{5... | collective-permute-start | bytes 1511432 | tf_op jit(solution)/shard_map/ppermute | solution.py:439
  138.7 27.4 %collective-permute-start.38 = (bf16[3,656,128]{2,1,0:T(8,128)(2,1)}, bf16[3,656,128]{2,1,0:T(8,128)(2,1)S(1)}, u32[]{:S(2)}, u32[]{:S(2)}) collective-permute-start(bf16[3,656,128]{2,1,0:T(8,128)(2,1)} %collective-permute-done.26), channel_id=1, source_target_pairs={{0,8},{4,12},{8,0},{12,4},{16,24},{20,28},{24,16},{28,20},{1,9},{5... | collective-permute-start | bytes 1511432 | tf_op jit(solution)/shard_map/ppermute | solution.py:439
  139.2 26.9 %collective-permute-start.39 = (bf16[3,656,128]{2,1,0:T(8,128)(2,1)S(1)}, bf16[3,656,128]{2,1,0:T(8,128)(2,1)S(1)}, u32[]{:S(2)}, u32[]{:S(2)}) collective-permute-start(bf16[3,656,128]{2,1,0:T(8,128)(2,1)S(1)} %collective-permute-done.33), channel_id=1, source_target_pairs={{0,8},{4,12},{8,0},{12,4},{16,24},{20,28},{24,16},{28,20},{1,9},{5... | collective-permute-start | bytes 1511432 | tf_op jit(solution)/shard_map/ppermute | solution.py:439
  140.8 25.4 %collective-permute-start.42 = (bf16[3,656,128]{2,1,0:T(8,128)(2,1)S(1)}, bf16[3,656,128]{2,1,0:T(8,128)(2,1)}, u32[]{:S(2)}, u32[]{:S(2)}) collective-permute-start(bf16[3,656,128]{2,1,0:T(8,128)(2,1)S(1)} %collective-permute-done.30), channel_id=1, source_target_pairs={{0,4},{4,0},{8,12},{12,8},{16,20},{20,16},{24,28},{28,24},{1,5},{5... | collective-permute-start | bytes 1511432 | tf_op jit(solution)/shard_map/ppermute | solution.py:439
  140.8 25.4 %collective-permute-start.40 = (bf16[3,656,128]{2,1,0:T(8,128)(2,1)S(1)}, bf16[3,656,128]{2,1,0:T(8,128)(2,1)}, u32[]{:S(2)}, u32[]{:S(2)}) collective-permute-start(bf16[3,656,128]{2,1,0:T(8,128)(2,1)S(1)} %collective-permute-done.30), channel_id=1, source_target_pairs={{0,16},{4,20},{8,24},{12,28},{16,0},{20,4},{24,8},{28,12},{1,17},{... | collective-permute-start | bytes 1511432 | tf_op jit(solution)/shard_map/ppermute | solution.py:439
  171.7 27.2 %collective-permute-start.49 = (bf16[4,2,3,656,128]{4,3,2,1,0:T(8,128)(2,1)}, bf16[4,2,3,656,128]{4,3,2,1,0:T(8,128)(2,1)}, u32[]{:S(2)}, u32[]{:S(2)}) collective-permute-start(bf16[4,2,3,656,128]{4,3,2,1,0:T(8,128)(2,1)} %get-tuple-element.392), channel_id=1, source_target_pairs={{0,4},{4,0},{8,12},{12,8},{16,20},{20,16},{24,28},{28,24},{1,5},{5... | collective-permute-start | bytes 12091400 | tf_op jit(solution)/shard_map/ppermute | solution.py:439
  227.7 40.5 %collective-permute-start.55 = (bf16[2,3,656,128]{3,2,1,0:T(8,128)(2,1)}, bf16[2,3,656,128]{3,2,1,0:T(8,128)(2,1)S(1)}, u32[]{:S(2)}, u32[]{:S(2)}) collective-permute-start(bf16[2,3,656,128]{3,2,1,0:T(8,128)(2,1)} %get-tuple-element.440), channel_id=1, source_target_pairs={{0,8},{4,12},{8,0},{12,4},{16,24},{20,28},{24,16},{28,20},{1,9},{5... | collective-permute-start | bytes 3022856 | tf_op jit(solution)/shard_map/ppermute | solution.py:439
  229.2 38.9 %collective-permute-start.56 = (bf16[2,3,656,128]{3,2,1,0:T(8,128)(2,1)S(1)}, bf16[2,3,656,128]{3,2,1,0:T(8,128)(2,1)S(1)}, u32[]{:S(2)}, u32[]{:S(2)}) collective-permute-start(bf16[2,3,656,128]{3,2,1,0:T(8,128)(2,1)S(1)} %get-tuple-element.441), channel_id=1, source_target_pairs={{0,16},{4,20},{8,24},{12,28},{16,0},{20,4},{24,8},{28,12},{1,17},{... | collective-permute-start | bytes 3022856 | tf_op jit(solution)/shard_map/ppermute | solution.py:439
  230.3 33.5 %collective-permute-start.53 = (bf16[1,3,656,128]{3,2,1,0:T(8,128)(2,1)}, bf16[1,3,656,128]{3,2,1,0:T(8,128)(2,1)}, u32[]{:S(2)}, u32[]{:S(2)}) collective-permute-start(bf16[1,3,656,128]{3,2,1,0:T(8,128)(2,1)} %get-tuple-element.429), channel_id=1, source_target_pairs={{0,16},{4,20},{8,24},{12,28},{16,0},{20,4},{24,8},{28,12},{1,17},{... | collective-permute-start | bytes 1511432 | tf_op jit(solution)/shard_map/ppermute | solution.py:439
  231.2 32.6 %collective-permute-start.54 = (bf16[1,3,656,128]{3,2,1,0:T(8,128)(2,1)S(1)}, bf16[1,3,656,128]{3,2,1,0:T(8,128)(2,1)}, u32[]{:S(2)}, u32[]{:S(2)}) collective-permute-start(bf16[1,3,656,128]{3,2,1,0:T(8,128)(2,1)S(1)} %get-tuple-element.430), channel_id=1, source_target_pairs={{0,8},{4,12},{8,0},{12,4},{16,24},{20,28},{24,16},{28,20},{1,9},{5... | collective-permute-start | bytes 1511432 | tf_op jit(solution)/shard_map/ppermute | solution.py:439
  268.1 28.4 %collective-permute-start.57 = (bf16[2,3,656,128]{3,2,1,0:T(8,128)(2,1)}, bf16[2,3,656,128]{3,2,1,0:T(8,128)(2,1)S(1)}, u32[]{:S(2)}, u32[]{:S(2)}) collective-permute-start(bf16[2,3,656,128]{3,2,1,0:T(8,128)(2,1)} %get-tuple-element.442), channel_id=1, source_target_pairs={{0,8},{4,12},{8,0},{12,4},{16,24},{20,28},{24,16},{28,20},{1,9},{5... | collective-permute-start | bytes 3022856 | tf_op jit(solution)/shard_map/ppermute | solution.py:439
  268.7 27.8 %collective-permute-start.58 = (bf16[2,3,656,128]{3,2,1,0:T(8,128)(2,1)}, bf16[2,3,656,128]{3,2,1,0:T(8,128)(2,1)}, u32[]{:S(2)}, u32[]{:S(2)}) collective-permute-start(bf16[2,3,656,128]{3,2,1,0:T(8,128)(2,1)} %get-tuple-element.443), channel_id=1, source_target_pairs={{0,16},{4,20},{8,24},{12,28},{16,0},{20,4},{24,8},{28,12},{1,17},{... | collective-permute-start | bytes 3022856 | tf_op jit(solution)/shard_map/ppermute | solution.py:439
  271.3 25.2 %collective-permute-start.59 = (bf16[3,656,128]{2,1,0:T(8,128)(2,1)S(1)}, bf16[3,656,128]{2,1,0:T(8,128)(2,1)}, u32[]{:S(2)}, u32[]{:S(2)}) collective-permute-start(bf16[3,656,128]{2,1,0:T(8,128)(2,1)S(1)} %fusion.11), channel_id=1, source_target_pairs={{0,2},{2,3},{3,1},{1,0},{4,6},{6,7},{7,5},{5,4},{8,10},{10,11},{11... | collective-permute-start | bytes 1511432 | tf_op jit(solution)/shard_map/ppermute | solution.py:451
  323.8 28.4 %collective-permute-start.65 = (bf16[4,4,128,256]{3,2,1,0:T(8,128)(2,1)S(1)}, bf16[4,4,128,256]{3,2,1,0:T(8,128)(2,1)}, u32[]{:S(2)}, u32[]{:S(2)}) collective-permute-start(bf16[4,4,128,256]{3,2,1,0:T(8,128)(2,1)S(1)} %get-tuple-element.474), channel_id=1, source_target_pairs={{0,8},{4,12},{8,0},{12,4},{16,24},{20,28},{24,16},{28,20},{1,9},{5... | collective-permute-start | bytes 3145736 | tf_op jit(solution)/shard_map/ppermute | solution.py:439
  324.6 27.7 %collective-permute-start.66 = (bf16[4,4,128,256]{3,2,1,0:T(8,128)(2,1)S(1)}, bf16[4,4,128,256]{3,2,1,0:T(8,128)(2,1)}, u32[]{:S(2)}, u32[]{:S(2)}) collective-permute-start(bf16[4,4,128,256]{3,2,1,0:T(8,128)(2,1)S(1)} %get-tuple-element.475), channel_id=1, source_target_pairs={{0,16},{4,20},{8,24},{12,28},{16,0},{20,4},{24,8},{28,12},{1,17},{... | collective-permute-start | bytes 3145736 | tf_op jit(solution)/shard_map/ppermute | solution.py:439
  329.2 24.4 %collective-permute-start.70 = (bf16[512,1024]{1,0:T(8,128)(2,1)}, bf16[512,1024]{1,0:T(8,128)(2,1)S(1)}, u32[]{:S(2)}, u32[]{:S(2)}) collective-permute-start(bf16[512,1024]{1,0:T(8,128)(2,1)} %get-tuple-element.487), channel_id=1, source_target_pairs={{0,1},{1,0},{2,3},{3,2},{4,5},{5,4},{6,7},{7,6},{8,9},{9,8},{10,11... | collective-permute-start | bytes 3145736 | tf_op jit(solution)/shard_map/ppermute | solution.py:763
  (100 other events, 1197.7 us)
